TPU v7x, 32 devices: a whole 2x2x4 slice. The times are simulated.
32 devices in a mesh: batch: 8 (over z, x), shard: 4 (over y, core).
Axes of the slice: x: 2, y: 2, z: 4, core: 2. Of those that a mesh axis runs over, the one named last changes fastest.
Arguments:
- windows: bfloat16 [32, 1500, 512], P(('batch', 'shard')), may hold values from -6 to 6
- cotangent: bfloat16 [32, 1500, 512], P(('batch', 'shard')), may hold values from -6 to 6
- valid: int32 [32], P(('batch', 'shard')), may hold values 0 or 1
- query_weight: bfloat16 [512, 512], P(('batch', 'shard')), may hold values from -0.375 to 0.375
- key_weight: bfloat16 [512, 512], P(('batch', 'shard')), may hold values from -0.375 to 0.375
- value_weight: bfloat16 [512, 512], P(('batch', 'shard')), may hold values from -0.25 to 0.25
- out_weight: bfloat16 [512, 512], P(('batch', 'shard')), may hold values from -1.5 to 1.5
- up_weight: bfloat16 [512, 2048], P(('batch', 'shard')), may hold values from -0.25 to 0.25
- down_weight: bfloat16 [2048, 512], P(('batch', 'shard')), may hold values from -0.1875 to 0.1875
- query_bias: bfloat16 [512], P(('batch', 'shard')), may hold values from -3 to 3
- value_bias: bfloat16 [512], P(('batch', 'shard')), may hold values from -3 to 3
- out_bias: bfloat16 [512], P(('batch', 'shard')), may hold values from -3 to 3
- up_bias: bfloat16 [2048], P(('batch', 'shard')), may hold values from -3 to 3
- down_bias: bfloat16 [512], P(('batch', 'shard')), may hold values from -3 to 3
- norm_gain: bfloat16 [512], P(('batch', 'shard')), may hold values from 0.5 to 1.5
- norm_shift: bfloat16 [512], P(('batch', 'shard')), may hold values from -2 to 2
- mlp_gain: bfloat16 [512], P(('batch', 'shard')), may hold values from 0.5 to 1.5
- mlp_shift: bfloat16 [512], P(('batch', 'shard')), may hold values from -2 to 2
Outputs:
- output: float32 [32, 1500, 512], P(('batch', 'shard'))
- input_grad: float32 [32, 1500, 512], P(('batch', 'shard'))
- grad_query_weight: float32 [512, 512], P(('batch', 'shard'))
- grad_key_weight: float32 [512, 512], P(('batch', 'shard'))
- grad_value_weight: float32 [512, 512], P(('batch', 'shard'))
- grad_out_weight: float32 [512, 512], P(('batch', 'shard'))
- grad_up_weight: float32 [512, 2048], P(('batch', 'shard'))
- grad_down_weight: float32 [2048, 512], P(('batch', 'shard'))
- grad_query_bias: float32 [512], P(('batch', 'shard'))
- grad_value_bias: float32 [512], P(('batch', 'shard'))
- grad_out_bias: float32 [512], P(('batch', 'shard'))
- grad_up_bias: float32 [2048], P(('batch', 'shard'))
- grad_down_bias: float32 [512], P(('batch', 'shard'))
- grad_norm_gain: float32 [512], P(('batch', 'shard'))
- grad_norm_shift: float32 [512], P(('batch', 'shard'))
- grad_mlp_gain: float32 [512], P(('batch', 'shard'))
- grad_mlp_shift: float32 [512], P(('batch', 'shard'))
Inputs may be any that keep to these rules, and one draw needn't show every extreme that they name: `valid`: 1 marks a slot that holds a window, 0 an empty slot.
All inputs are finite; a program needn't handle non-finite values. No bound on the sum of `valid` on one device may be relied on, other than what follows from the above.
Results may differ from a plain program's by a relative error of at most 0.012.
The roundings to bfloat16 on the way count: a program that leaves them out, or rounds other values in their place, can miss the bound.
Values may be sent and summed in bfloat16 or wider, within the bound.
A program may use at most 192 MiB of HBM per device.

v0:
```python
import math

import jax
import jax.numpy as jnp
from jax import lax
from jax.sharding import PartitionSpec as P

D = 512
HEADS = 8


NORM_EPS = 1e-05


def product(left, right):
    return jnp.dot(left, right, preferred_element_type=jnp.float32)


def inner_rows(left, right):
    return lax.dot_general(
        left, right, (((0,), (0,)), ((), ())), preferred_element_type=jnp.float32
    )


def outer_cols(left, right):
    return lax.dot_general(
        left, right, (((1,), (1,)), ((), ())), preferred_element_type=jnp.float32
    )


def normalize(values, gain, shift):
    row_mean = jnp.mean(values, axis=-1, keepdims=True)
    centred = values - row_mean
    variance = jnp.mean(centred * centred, axis=-1, keepdims=True)
    inv_std = lax.rsqrt(variance + NORM_EPS)
    unit_rows = centred * inv_std
    return (unit_rows * gain + shift, unit_rows, inv_std)


def normalize_back(grad_rows, unit_rows, inv_std, gain):
    scaled = grad_rows * gain
    first_mean = jnp.mean(scaled, axis=-1, keepdims=True)
    second_mean = jnp.mean(scaled * unit_rows, axis=-1, keepdims=True)
    grad_values = inv_std * (scaled - first_mean - unit_rows * second_mean)
    return (grad_values, jnp.sum(grad_rows * unit_rows, axis=0), jnp.sum(grad_rows, axis=0))


def split_heads(table):
    return table.reshape(table.shape[0], HEADS, D // HEADS).transpose(1, 0, 2)


def merge_heads(table):
    return table.transpose(1, 0, 2).reshape(table.shape[1], D)


def attend_head(inputs):
    query_rows, key_rows, value_rows = inputs
    score_scale = 1.0 / math.sqrt(D // HEADS)
    scores = outer_cols(query_rows, key_rows) * score_scale
    row_peak = jnp.max(scores, axis=-1, keepdims=True)
    exp_scores = jnp.exp(scores - row_peak)
    row_total = jnp.sum(exp_scores, axis=-1, keepdims=True)
    probabilities = (exp_scores / row_total).astype(jnp.bfloat16)
    return (product(probabilities, value_rows), (row_peak + jnp.log(row_total))[:, 0])


def attend_back(inputs):
    query_rows, key_rows, value_rows, log_total, grad_rows = inputs
    score_scale = 1.0 / math.sqrt(D // HEADS)
    scores = outer_cols(query_rows, key_rows) * score_scale
    probabilities = jnp.exp(scores - log_total[:, None])
    grad_probs = outer_cols(grad_rows, value_rows)
    grad_scores = probabilities * (
        grad_probs - jnp.sum(probabilities * grad_probs, axis=-1, keepdims=True)
    )
    grad_scores = grad_scores.astype(jnp.bfloat16)
    grad_value = inner_rows(probabilities.astype(jnp.bfloat16), grad_rows)
    grad_query = product(grad_scores, key_rows) * score_scale
    grad_key = inner_rows(grad_scores, query_rows) * score_scale
    return (grad_query, grad_key, grad_value)


def per_device(
    windows,
    cotangent,
    valid,
    query_weight,
    key_weight,
    value_weight,
    out_weight,
    up_weight,
    down_weight,
    query_bias,
    value_bias,
    out_bias,
    up_bias,
    down_bias,
    norm_gain,
    norm_shift,
    mlp_gain,
    mlp_shift,
):
    owned_params = (
        query_weight,
        key_weight,
        value_weight,
        out_weight,
        up_weight,
        down_weight,
        query_bias,
        value_bias,
        out_bias,
        up_bias,
        down_bias,
        norm_gain,
        norm_shift,
        mlp_gain,
        mlp_shift,
    )
    gathered = (
        lax.all_gather(owned_params[0], ("batch", "shard"), axis=0, tiled=True),
        lax.all_gather(owned_params[1], ("batch", "shard"), axis=0, tiled=True),
        lax.all_gather(owned_params[2], ("batch", "shard"), axis=0, tiled=True),
        lax.all_gather(owned_params[3], ("batch", "shard"), axis=0, tiled=True),
        lax.all_gather(owned_params[4], ("batch", "shard"), axis=0, tiled=True),
        lax.all_gather(owned_params[5], ("batch", "shard"), axis=0, tiled=True),
        lax.all_gather(owned_params[6], ("batch", "shard"), axis=0, tiled=True),
        lax.all_gather(owned_params[7], ("batch", "shard"), axis=0, tiled=True),
        lax.all_gather(owned_params[8], ("batch", "shard"), axis=0, tiled=True),
        lax.all_gather(owned_params[9], ("batch", "shard"), axis=0, tiled=True),
        lax.all_gather(owned_params[10], ("batch", "shard"), axis=0, tiled=True),
        lax.all_gather(owned_params[11], ("batch", "shard"), axis=0, tiled=True),
        lax.all_gather(owned_params[12], ("batch", "shard"), axis=0, tiled=True),
        lax.all_gather(owned_params[13], ("batch", "shard"), axis=0, tiled=True),
        lax.all_gather(owned_params[14], ("batch", "shard"), axis=0, tiled=True),
    )
    (
        wq_full,
        wk_full,
        wv_full,
        wo_full,
        wup_full,
        wdown_full,
        bq_full,
        bv_full,
        bo_full,
        bup_full,
        bdown_full,
        gain_one,
        shift_one,
        gain_two,
        shift_two,
    ) = gathered

    def forward(slot_item):
        window_rows, slot_flag = slot_item
        inputs = window_rows.astype(jnp.float32)
        normed, unit_one, inv_one = normalize(
            inputs, gain_one.astype(jnp.float32), shift_one.astype(jnp.float32)
        )
        normed_low = normed.astype(jnp.bfloat16)
        query_rows = (product(normed_low, wq_full) + bq_full.astype(jnp.float32)).astype(
            jnp.bfloat16
        )
        key_rows = product(normed_low, wk_full).astype(jnp.bfloat16)
        value_rows = (product(normed_low, wv_full) + bv_full.astype(jnp.float32)).astype(
            jnp.bfloat16
        )
        mixed_heads, log_total = lax.map(
            attend_head, (split_heads(query_rows), split_heads(key_rows), split_heads(value_rows))
        )
        attended = merge_heads(mixed_heads).astype(jnp.bfloat16)
        residual = inputs + (product(attended, wo_full) + bo_full.astype(jnp.float32))
        normed_two, unit_two, inv_two = normalize(
            residual, gain_two.astype(jnp.float32), shift_two.astype(jnp.float32)
        )
        normed_two_low = normed_two.astype(jnp.bfloat16)
        hidden = product(normed_two_low, wup_full) + bup_full.astype(jnp.float32)
        active = jax.nn.gelu(hidden, approximate=False).astype(jnp.bfloat16)
        layer_out = residual + product(active, wdown_full) + bdown_full.astype(jnp.float32)
        saved_state = (
            normed_low,
            query_rows,
            key_rows,
            value_rows,
            log_total,
            attended,
            unit_one,
            inv_one,
            unit_two,
            inv_two,
            normed_two_low,
            hidden,
            active,
        )
        return (layer_out * slot_flag.astype(jnp.float32), saved_state)

    outputs, saved_all = lax.map(forward, (windows, valid))
    gathered_back = (
        lax.all_gather(owned_params[0], ("batch", "shard"), axis=0, tiled=True),
        lax.all_gather(owned_params[1], ("batch", "shard"), axis=0, tiled=True),
        lax.all_gather(owned_params[2], ("batch", "shard"), axis=0, tiled=True),
        lax.all_gather(owned_params[3], ("batch", "shard"), axis=0, tiled=True),
        lax.all_gather(owned_params[4], ("batch", "shard"), axis=0, tiled=True),
        lax.all_gather(owned_params[5], ("batch", "shard"), axis=0, tiled=True),
        lax.all_gather(owned_params[6], ("batch", "shard"), axis=0, tiled=True),
        lax.all_gather(owned_params[7], ("batch", "shard"), axis=0, tiled=True),
        lax.all_gather(owned_params[8], ("batch", "shard"), axis=0, tiled=True),
        lax.all_gather(owned_params[9], ("batch", "shard"), axis=0, tiled=True),
        lax.all_gather(owned_params[10], ("batch", "shard"), axis=0, tiled=True),
        lax.all_gather(owned_params[11], ("batch", "shard"), axis=0, tiled=True),
        lax.all_gather(owned_params[12], ("batch", "shard"), axis=0, tiled=True),
        lax.all_gather(owned_params[13], ("batch", "shard"), axis=0, tiled=True),
        lax.all_gather(owned_params[14], ("batch", "shard"), axis=0, tiled=True),
    )
    (
        wq_back,
        wk_back,
        wv_back,
        wo_back,
        wup_back,
        wdown_back,
        bq_back,
        bv_back,
        bo_back,
        bup_back,
        bdown_back,
        gain_one_back,
        shift_one_back,
        gain_two_back,
        shift_two_back,
    ) = gathered_back
    zero_grads = tuple((jnp.zeros(weight_arg.shape, jnp.float32) for weight_arg in gathered_back))

    def backward(totals, slot_item):
        grad_in, slot_flag, saved_state = slot_item
        (
            normed_low,
            query_rows,
            key_rows,
            value_rows,
            log_total,
            attended,
            unit_one,
            inv_one,
            unit_two,
            inv_two,
            normed_two_low,
            hidden,
            active,
        ) = saved_state
        grad_out = grad_in.astype(jnp.float32) * slot_flag.astype(jnp.float32)
        grad_low = grad_out.astype(jnp.bfloat16)
        grad_down = inner_rows(active, grad_low)
        grad_down_bias = jnp.sum(grad_out, axis=0)
        grad_active = outer_cols(grad_low, wdown_back)
        normal_cdf = 0.5 * (1.0 + lax.erf(hidden * (1.0 / math.sqrt(2.0))))
        normal_pdf = jnp.exp(-0.5 * hidden * hidden) * (1.0 / math.sqrt(2.0 * math.pi))
        grad_hidden = (grad_active * (normal_cdf + hidden * normal_pdf)).astype(jnp.bfloat16)
        grad_up = inner_rows(normed_two_low, grad_hidden)
        grad_up_bias = jnp.sum(grad_hidden.astype(jnp.float32), axis=0)
        grad_normed_two = outer_cols(grad_hidden, wup_back)
        grad_resid_part, grad_gain_two, grad_shift_two = normalize_back(
            grad_normed_two, unit_two, inv_two, gain_two_back.astype(jnp.float32)
        )
        grad_resid = grad_out + grad_resid_part
        grad_branch = grad_resid.astype(jnp.bfloat16)
        grad_out_w = inner_rows(attended, grad_branch)
        grad_out_bias = jnp.sum(grad_branch.astype(jnp.float32), axis=0)
        grad_attended = outer_cols(grad_branch, wo_back).astype(jnp.bfloat16)
        query_heads, key_heads, value_heads = lax.map(
            attend_back,
            (
                split_heads(query_rows),
                split_heads(key_rows),
                split_heads(value_rows),
                log_total,
                split_heads(grad_attended),
            ),
        )
        grad_query = merge_heads(query_heads).astype(jnp.bfloat16)
        grad_key = merge_heads(key_heads).astype(jnp.bfloat16)
        grad_value = merge_heads(value_heads).astype(jnp.bfloat16)
        grad_query_w = inner_rows(normed_low, grad_query)
        grad_key_w = inner_rows(normed_low, grad_key)
        grad_value_w = inner_rows(normed_low, grad_value)
        grad_query_bias = jnp.sum(grad_query.astype(jnp.float32), axis=0)
        grad_value_bias = jnp.sum(grad_value.astype(jnp.float32), axis=0)
        grad_normed = (
            outer_cols(grad_query, wq_back)
            + outer_cols(grad_key, wk_back)
            + outer_cols(grad_value, wv_back)
        )
        grad_input_part, grad_gain_one, grad_shift_one = normalize_back(
            grad_normed, unit_one, inv_one, gain_one_back.astype(jnp.float32)
        )
        grad_input = grad_resid + grad_input_part
        new_terms = (
            grad_query_w,
            grad_key_w,
            grad_value_w,
            grad_out_w,
            grad_up,
            grad_down,
            grad_query_bias,
            grad_value_bias,
            grad_out_bias,
            grad_up_bias,
            grad_down_bias,
            grad_gain_one,
            grad_shift_one,
            grad_gain_two,
            grad_shift_two,
        )
        totals = tuple((carry_term + new_term for carry_term, new_term in zip(totals, new_terms)))
        return (totals, grad_input)

    totals, input_grads = lax.scan(backward, zero_grads, (cotangent, valid, saved_all))
    owned_grads = (
        lax.psum_scatter(totals[0], ("batch", "shard"), scatter_dimension=0, tiled=True),
        lax.psum_scatter(totals[1], ("batch", "shard"), scatter_dimension=0, tiled=True),
        lax.psum_scatter(totals[2], ("batch", "shard"), scatter_dimension=0, tiled=True),
        lax.psum_scatter(totals[3], ("batch", "shard"), scatter_dimension=0, tiled=True),
        lax.psum_scatter(totals[4], ("batch", "shard"), scatter_dimension=0, tiled=True),
        lax.psum_scatter(totals[5], ("batch", "shard"), scatter_dimension=0, tiled=True),
        lax.psum_scatter(totals[6], ("batch", "shard"), scatter_dimension=0, tiled=True),
        lax.psum_scatter(totals[7], ("batch", "shard"), scatter_dimension=0, tiled=True),
        lax.psum_scatter(totals[8], ("batch", "shard"), scatter_dimension=0, tiled=True),
        lax.psum_scatter(totals[9], ("batch", "shard"), scatter_dimension=0, tiled=True),
        lax.psum_scatter(totals[10], ("batch", "shard"), scatter_dimension=0, tiled=True),
        lax.psum_scatter(totals[11], ("batch", "shard"), scatter_dimension=0, tiled=True),
        lax.psum_scatter(totals[12], ("batch", "shard"), scatter_dimension=0, tiled=True),
        lax.psum_scatter(totals[13], ("batch", "shard"), scatter_dimension=0, tiled=True),
        lax.psum_scatter(totals[14], ("batch", "shard"), scatter_dimension=0, tiled=True),
    )
    return (outputs, input_grads) + tuple(owned_grads)


def solution(mesh):
    in_specs = (
        P(("batch", "shard"), None, None),
        P(("batch", "shard"), None, None),
        P(("batch", "shard")),
        P(("batch", "shard"), None),
        P(("batch", "shard"), None),
        P(("batch", "shard"), None),
        P(("batch", "shard"), None),
        P(("batch", "shard"), None),
        P(("batch", "shard"), None),
        P(("batch", "shard")),
        P(("batch", "shard")),
        P(("batch", "shard")),
        P(("batch", "shard")),
        P(("batch", "shard")),
        P(("batch", "shard")),
        P(("batch", "shard")),
        P(("batch", "shard")),
        P(("batch", "shard")),
    )
    out_specs = (
        P(("batch", "shard"), None, None),
        P(("batch", "shard"), None, None),
        P(("batch", "shard"), None),
        P(("batch", "shard"), None),
        P(("batch", "shard"), None),
        P(("batch", "shard"), None),
        P(("batch", "shard"), None),
        P(("batch", "shard"), None),
        P(("batch", "shard")),
        P(("batch", "shard")),
        P(("batch", "shard")),
        P(("batch", "shard")),
        P(("batch", "shard")),
        P(("batch", "shard")),
        P(("batch", "shard")),
        P(("batch", "shard")),
        P(("batch", "shard")),
    )
    return jax.shard_map(
        per_device, mesh=mesh, in_specs=in_specs, out_specs=out_specs, check_vma=False
    )
```

profile of v0, /device:TPU:0, one launch (start us, length us, event | category | flops | bytes accessed | tf_op | source)
XLA Modules:
  0.0 1325.1 jit_solution(882152880115425450)
XLA Ops:
  17.1 42.2 %all-reduce.19 = (bf16[512]{0:T(512)(128)(2,1)S(1)}, bf16[512]{0:T(512)(128)(2,1)S(1)}, bf16[512]{0:T(512)(128)(2,1)S(1)}, bf16[512]{0:T(512)(128)(2,1)S(1)}, bf...) all-reduce(bf16[512]{0:T(512)(128)(2,1)S(1)} %dynamic-update-slice., ...), channel_id=1, replica_groups=mesh['batch'=8,'shard'=4] {'batch','shard'}, use_global_device_ids=true, to_apply=%add.2 | all-reduce | flops 6144 | bytes 24576
  63.3 45.0 %all_gather.55 = bf16[512,512]{1,0:T(8,128)(2,1)} all-gather(bf16[16,512]{1,0:T(8,128)(2,1)S(1)} %copy-done.28), channel_id=1, replica_groups=mesh['batch'=8,'shard'=4] {'batch','shard'}, dimensions={0}, use_global_device_ids=true | all-gather | bytes 540672 | tf_op jit(solution)/shard_map/all_gather | solution.py:121
  108.3 41.0 %all_gather.57 = bf16[512,512]{1,0:T(8,128)(2,1)} all-gather(bf16[16,512]{1,0:T(8,128)(2,1)S(1)} %copy-done.29), channel_id=1, replica_groups=mesh['batch'=8,'shard'=4] {'batch','shard'}, dimensions={0}, use_global_device_ids=true | all-gather | bytes 540672 | tf_op jit(solution)/shard_map/all_gather | solution.py:122
  149.3 39.4 %all_gather.58 = bf16[512,512]{1,0:T(8,128)(2,1)S(1)} all-gather(bf16[16,512]{1,0:T(8,128)(2,1)S(1)} %copy-done.30), channel_id=1, replica_groups=mesh['batch'=8,'shard'=4] {'batch','shard'}, dimensions={0}, use_global_device_ids=true | all-gather | bytes 540672 | tf_op jit(solution)/shard_map/all_gather | solution.py:123
  188.7 40.9 %all_gather.60 = bf16[512,512]{1,0:T(8,128)(2,1)} all-gather(bf16[16,512]{1,0:T(8,128)(2,1)S(1)} %copy-done.31), channel_id=1, replica_groups=mesh['batch'=8,'shard'=4] {'batch','shard'}, dimensions={0}, use_global_device_ids=true | all-gather | bytes 540672 | tf_op jit(solution)/shard_map/all_gather | solution.py:124
  254.5 58.4 %while.29 = (s32[]{:T(128)}, bf16[8,1500,64]{1,2,0:T(8,128)(2,1)}, f32[8,1500]{1,0:T(8,128)S(1)}, bf16[8,1500,64]{2,1,0:T(8,128)(2,1)}, bf16[8,1500,64]{2,1,0:T(...) while((s32[]{:T(128)}, bf16[8,1500,64]{1,2,0:T(8,128)(2,1)}, ...), condition=%wide.region_5.6_spmd, body=%wide.region_2.5_spmd.sunk | while | flops 591748480 | bytes 28622432 | solution.py:169
  312.9 4.3 fusion.105
  319.4 33.1 %fusion.48 = (bf16[1500,2048]{1,0:T(8,128)(2,1)}, f32[1500,2048]{1,0:T(8,128)}) fusion(f32[2048]{0:T(1024)S(1)} %convert_element_type.209, bf16[512,2048]{1,0:T(8,128)(2,1)} %all-gather.3.cloned.1.call-done, f32[1500,512]{1,0:T(8,128)} %copy-done.7, f32[512]{0:T(512)S(1)} %convert_element_type.207, f32[512]{0:T(512)S(1)} %convert_element_type.206, ...), kind=kOutput, calls=%fused_computation.56 | convolution fusion | flops 3352320000 | bytes 23625440 | tf_op jit(solution)/shard_map/while/body/eval_jaxpr/dot_general | solution.py:16
  352.6 10.9 convert_reduce_fusion
  363.5 5.1 multiply_reduce_fusion.1
  380.6 252.8 %while.30 = (s32[]{:T(128)}, bf16[8,1500,64]{1,2,0:T(8,128)(2,1)S(1)}, bf16[8,1500,64]{1,2,0:T(8,128)(2,1)}, bf16[8,1500,64]{1,2,0:T(8,128)(2,1)}, bf16[8,1500,6...) while((s32[]{:T(128)}, ...), condition=%wide.region_12.13_spmd, body=%wide.region_10.12_spmd.sunk | while | flops 1458190464 | bytes 125394128 | solution.py:271
  383.0 7.4 multiply_reduce_fusion.7
  390.5 10.8 multiply_convert_fusion.2
  401.2 6.0 fusion.170
  414.7 7.4 multiply_reduce_fusion.7
  422.1 10.8 multiply_convert_fusion.2
  432.9 6.0 fusion.170
  446.3 7.4 multiply_reduce_fusion.7
  453.8 10.7 multiply_convert_fusion.2
  464.5 6.0 fusion.170
  478.0 7.4 multiply_reduce_fusion.7
  485.4 10.7 multiply_convert_fusion.2
  496.1 6.0 fusion.170
  509.5 7.4 multiply_reduce_fusion.7
  517.0 10.7 multiply_convert_fusion.2
  527.7 6.0 fusion.170
  541.1 7.4 multiply_reduce_fusion.7
  548.6 10.7 multiply_convert_fusion.2
  559.3 6.0 fusion.170
  572.7 7.4 multiply_reduce_fusion.7
  580.1 10.7 multiply_convert_fusion.2
  590.9 6.0 fusion.170
  604.3 7.4 multiply_reduce_fusion.7
  611.7 10.7 multiply_convert_fusion.2
  622.4 6.0 fusion.170
  633.5 3.9 fusion.109
  644.6 8.6 fusion.91
  653.9 9.3 fusion.99
  665.7 7.7 fusion.72
  673.4 8.8 copy.65
  687.1 4.1 fusion.80
  691.3 37.7 %all-reduce.18 = (f32[512]{0:T(512)S(1)}, f32[512]{0:T(512)S(1)}, f32[512]{0:T(512)S(1)}, f32[2048]{0:T(1024)S(1)}, f32[512]{0:T(512)S(1)}, /*index=5*/f32[512]{...) all-reduce(f32[512]{0:T(512)S(1)} %reduce_sum.201, ...), channel_id=8, replica_groups=mesh['batch'=8,'shard'=4] {'batch','shard'}, use_global_device_ids=true, to_apply=%region_22.23.clone | all-reduce | flops 6144 | bytes 49152
  736.6 8.8 copy.66
  746.0 24.1 %reduce-scatter.11.cloned.1.call-done = f32[16,512]{1,0:T(8,128)} async-done(((f32[512,512]{1,0:T(8,128)}), f32[16,512]{1,0:T(8,128)}) %reduce-scatter.11.cloned.1.call-update) | async-done | bytes 32784 | tf_op jit(solution)/shard_map/reduce_scatter | solution.py:322
  770.1 133.4 %reduce-scatter.7.cloned.1.call-done = f32[16,512]{1,0:T(8,128)} async-done(((f32[512,512]{1,0:T(8,128)}), f32[16,512]{1,0:T(8,128)}) %reduce-scatter.7.cloned.1.call-update) | async-done | bytes 32784 | tf_op jit(solution)/shard_map/reduce_scatter | solution.py:320
  903.5 133.5 %reduce-scatter.9.cloned.1.call-done = f32[16,512]{1,0:T(8,128)} async-done(((f32[512,512]{1,0:T(8,128)}), f32[16,512]{1,0:T(8,128)}) %reduce-scatter.9.cloned.1.call-update) | async-done | bytes 32784 | tf_op jit(solution)/shard_map/reduce_scatter | solution.py:321
  1037.0 140.7 %reduce-scatter.17.cloned.1.call-done = f32[64,512]{1,0:T(8,128)} async-done(((f32[2048,512]{1,0:T(8,128)}), f32[64,512]{1,0:T(8,128)}) %reduce-scatter.17.cloned.1.call-update) | async-done | bytes 131088 | tf_op jit(solution)/shard_map/reduce_scatter | solution.py:325
  1177.7 140.3 %reduce-scatter.15.cloned.1.call-done = f32[16,2048]{1,0:T(8,128)} async-done(((f32[512,2048]{1,0:T(8,128)}), f32[16,2048]{1,0:T(8,128)}) %reduce-scatter.15.cloned.1.call-update) | async-done | bytes 131088 | tf_op jit(solution)/shard_map/reduce_scatter | solution.py:324
  (288 shorter events, 193.0 us)
Async XLA Ops:
  7.2 222.4 %copy-start.5 = (bf16[1,1500,512]{2,1,0:T(8,128)(2,1)S(1)}, bf16[1,1500,512]{2,1,0:T(8,128)(2,1)}, u32[]{:S(2)}) copy-start(bf16[1,1500,512]{2,1,0:T(8,128)(2,1)} %param.22) | copy-start | bytes 4608004
  7.2 56.0 %copy-start.28 = (bf16[16,512]{1,0:T(8,128)(2,1)S(1)}, bf16[16,512]{1,0:T(8,128)(2,1)}, u32[]{:S(2)}) copy-start(bf16[16,512]{1,0:T(8,128)(2,1)} %param.25) | copy-start | bytes 49156
  7.2 101.1 %copy-start.29 = (bf16[16,512]{1,0:T(8,128)(2,1)S(1)}, bf16[16,512]{1,0:T(8,128)(2,1)}, u32[]{:S(2)}) copy-start(bf16[16,512]{1,0:T(8,128)(2,1)} %param.26) | copy-start | bytes 49156
  7.2 142.1 %copy-start.30 = (bf16[16,512]{1,0:T(8,128)(2,1)S(1)}, bf16[16,512]{1,0:T(8,128)(2,1)}, u32[]{:S(2)}) copy-start(bf16[16,512]{1,0:T(8,128)(2,1)} %param.27) | copy-start | bytes 49156
  7.2 181.5 %copy-start.31 = (bf16[16,512]{1,0:T(8,128)(2,1)S(1)}, bf16[16,512]{1,0:T(8,128)(2,1)}, u32[]{:S(2)}) copy-start(bf16[16,512]{1,0:T(8,128)(2,1)} %param.28) | copy-start | bytes 49156
  7.2 312.2 %all-gather.3.cloned.1.call-start = ((), (), s32[]{:S(2)}) async-start(), calls=%async_computation.6 | async-start | bytes 2162688 | tf_op jit(solution)/shard_map/all_gather | solution.py:125
  8.0 344.6 %all-gather.5.cloned.1.call-start = ((), (), s32[]{:S(2)}) async-start(), calls=%async_computation.7 | async-start | bytes 2162688 | tf_op jit(solution)/shard_map/all_gather | solution.py:126
  8.7 737.3 %reduce-scatter.13.cloned.1.call-start = ((), (), s32[]{:S(2)}) async-start(), calls=%async_computation.11 | async-start | bytes 1081344 | tf_op jit(solution)/shard_map/reduce_scatter | solution.py:323
  59.3 186.9 %copy-start.26 = (f32[512]{0:T(512)}, f32[512]{0:T(512)S(1)}, u32[]{:S(2)}) copy-start(f32[512]{0:T(512)S(1)} %convert_element_type.194) | copy-start | bytes 6148
  59.4 309.3 %copy-start.33 = (f32[512]{0:T(512)}, f32[512]{0:T(512)S(1)}, u32[]{:S(2)}) copy-start(f32[512]{0:T(512)S(1)} %convert_element_type.206) | copy-start | bytes 6148
  59.4 260.1 %copy-start.38 = (f32[512]{0:T(512)}, f32[512]{0:T(512)S(1)}, u32[]{:S(2)}) copy-start(f32[512]{0:T(512)S(1)} %convert_element_type.207) | copy-start | bytes 6148
  61.1 185.1 %copy-start.18 = (f32[1500]{0:T(1024)}, f32[1500]{0:T(1024)S(1)}, u32[]{:S(2)}) copy-start(f32[1500]{0:T(1024)S(1)} %broadcast_multiply_fusion.5) | copy-start | bytes 18004
  63.2 183.0 %copy-start.22 = (f32[1500]{0:T(1024)}, f32[1500]{0:T(1024)S(1)}, u32[]{:S(2)}) copy-start(f32[1500]{0:T(1024)S(1)} %add_rsqrt_fusion.1) | copy-start | bytes 18004
  188.7 42.6 %copy-start.16 = (bf16[512,512]{1,0:T(8,128)(2,1)}, bf16[512,512]{1,0:T(8,128)(2,1)S(1)}, u32[]{:S(2)}) copy-start(bf16[512,512]{1,0:T(8,128)(2,1)S(1)} %all_gather.58) | copy-start | bytes 1572868
  312.9 4.3 copy-start.4
  317.2 51.4 %copy-start.20 = (f32[1500]{0:T(1024)}, f32[1500]{0:T(1024)S(1)}, u32[]{:S(2)}) copy-start(f32[1500]{0:T(1024)S(1)} %broadcast_multiply_fusion.4) | copy-start | bytes 18004
  319.4 49.3 %copy-start.24 = (f32[1500]{0:T(1024)}, f32[1500]{0:T(1024)S(1)}, u32[]{:S(2)}) copy-start(f32[1500]{0:T(1024)S(1)} %add_rsqrt_fusion) | copy-start | bytes 18004
  319.4 33.2 %copy-start.12 = (bf16[1,1500,512]{2,1,0:T(8,128)(2,1)S(1)}, bf16[1,1500,512]{2,1,0:T(8,128)(2,1)}, u32[]{:S(2)}) copy-start(bf16[1,1500,512]{2,1,0:T(8,128)(2,1)} %param.23) | copy-start | bytes 4608004
  352.6 10.9 copy-start.8
  352.6 10.9 copy-start.41
  363.5 5.1 copy-start.42
  363.5 5.1 copy-start.13
  376.0 394.1 %reduce-scatter.11.cloned.1.call-start = ((), (), s32[]{:S(2)}) async-start(), calls=%async_computation.10 | async-start | bytes 1081344 | tf_op jit(solution)/shard_map/reduce_scatter | solution.py:322
  383.0 7.4 copy-start
  401.2 6.0 copy-start.1
  414.7 7.4 copy-start
  432.9 6.0 copy-start.1
  446.3 7.4 copy-start
  464.5 6.0 copy-start.1
  477.9 7.4 copy-start
  496.1 6.0 copy-start.1
  509.5 7.4 copy-start
  527.7 6.0 copy-start.1
  541.1 7.4 copy-start
  559.3 6.0 copy-start.1
  572.7 7.4 copy-start
  590.9 6.0 copy-start.1
  604.3 7.4 copy-start
  622.4 6.0 copy-start.1
  637.4 266.1 %reduce-scatter.7.cloned.1.call-start = ((), (), s32[]{:S(2)}) async-start(), calls=%async_computation.8 | async-start | bytes 1081344 | tf_op jit(solution)/shard_map/reduce_scatter | solution.py:320
  641.0 395.9 %reduce-scatter.9.cloned.1.call-start = ((), (), s32[]{:S(2)}) async-start(), calls=%async_computation.9 | async-start | bytes 1081344 | tf_op jit(solution)/shard_map/reduce_scatter | solution.py:321
  644.6 533.1 %reduce-scatter.17.cloned.1.call-start = ((), (), s32[]{:S(2)}) async-start(), calls=%async_computation.13 | async-start | bytes 4325376 | tf_op jit(solution)/shard_map/reduce_scatter | solution.py:325
  653.2 664.7 %reduce-scatter.15.cloned.1.call-start = ((), (), s32[]{:S(2)}) async-start(), calls=%async_computation.12 | async-start | bytes 4325376 | tf_op jit(solution)/shard_map/reduce_scatter | solution.py:324
  673.4 8.8 copy-start.9
  687.1 4.2 copy-start.32
  687.1 4.2 copy-start.35
  687.1 4.2 copy-start.36
  687.1 46.6 %copy-start.3 = (f32[1500,512]{1,0:T(8,128)S(1)}, f32[1500,512]{1,0:T(8,128)}, u32[]{:S(2)}) copy-start(f32[1500,512]{1,0:T(8,128)} %copy-done.2) | copy-start | bytes 9216004
  (17 other events, 30.2 us)
Sparse Core Ops, SparseCore 0:
  10.9 59.2 all-gather.2
  73.0 55.9 all-gather.4
  376.1 132.2 reduce-scatter.12
  637.5 132.5 reduce-scatter.10
  772.8 130.6 reduce-scatter.6
  906.3 130.6 reduce-scatter.8
  1039.8 137.7 reduce-scatter.16
  1180.5 137.4 reduce-scatter.14
where the time goes:
time: 1330 us
  waiting for transfers between devices  573 us (43%)
  matrix products  323 us (24%)
  blocking collectives  246 us (18%)
  other arithmetic  110 us (8%)
  local copies, waits for them, and re-layouts  55.4 us (4%)
  between operations  15.7 us (1%)
    reduce_scatter x1, waiting for transfers between devices, per_device(): lax.psum_scatter(totals[5], ('batch', 'shard'), scatter_dimension=0, tile...  141 us
    reduce_scatter x1, waiting for transfers between devices, per_device(): lax.psum_scatter(totals[4], ('batch', 'shard'), scatter_dimension=0, tile...  140 us
    reduce_scatter x1, waiting for transfers between devices, per_device(): lax.psum_scatter(totals[1], ('batch', 'shard'), scatter_dimension=0, tile...  133 us
    reduce_scatter x1, waiting for transfers between devices, per_device(): lax.psum_scatter(totals[0], ('batch', 'shard'), scatter_dimension=0, tile...  133 us
    dot_general x30, matrix products, outer_cols(): lax.dot_general(left, right, (((1,), (1,)), ((), ())), preferred_element_...  124 us
    dot_general x22, matrix products, inner_rows(): lax.dot_general(left, right, (((0,), (0,)), ((), ())), preferred_element_...  103 us
    dot_general x22, matrix products, product(): return jnp.dot(left, right, preferred_element_type=jnp.float32)  96.2 us
    convert_element_type x8, other arithmetic, attend_back(): grad_scores = grad_scores.astype(jnp.bfloat16)  85.9 us
  transfers between devices with their start and end apart: 8, of which 5 were waited for; matrix products, arithmetic and copies ran while one was open for 35% of the time, Pallas kernels for 0%

commit v1 on v0

v1 whole, which is shorter than its diff:
```python
import functools
import math

import jax
import jax.numpy as jnp
from jax import lax
from jax.experimental import pallas as pl
from jax.experimental.pallas import tpu as pltpu
from jax.sharding import PartitionSpec as P

HEADS = 8
NORM_EPS = 1e-05
LOG2E = math.log2(math.e)
LN2 = math.log(2.0)
F32 = jnp.float32
BF16 = jnp.bfloat16
ROWS = 256
QUERIES = 768
FF_CHUNK = 512
MASKED = -1e30

NN = (((1,), (0,)), ((), ()))
NT = (((1,), (1,)), ((), ()))
TN = (((0,), (0,)), ((), ()))

TAIL_RATE = 0.2625
TAIL = (
    0.10474836168174968,
    0.10416468281706748,
    0.10263486984927783,
    0.056568077030165455,
    0.14744499390073365,
    -0.13092736820325213,
    0.23259357413631826,
    -0.14775373854130247,
    0.03052653723595064,
)


def dot(left, right, dims):
    return lax.dot_general(left, right, dims, preferred_element_type=F32)


def normalize(values):
    centred = values - jnp.mean(values, axis=-1, keepdims=True)
    variance = jnp.mean(centred * centred, axis=-1, keepdims=True)
    inv_std = lax.rsqrt(variance + NORM_EPS)
    return centred * inv_std, inv_std


def normalize_back(grad_rows, unit_rows, inv_std, gain):
    scaled = grad_rows * gain
    first_mean = jnp.mean(scaled, axis=-1, keepdims=True)
    second_mean = jnp.mean(scaled * unit_rows, axis=-1, keepdims=True)
    return inv_std * (scaled - first_mean - unit_rows * second_mean)


def column_sums(rows):
    return jnp.sum(rows, axis=0, keepdims=True)


def in_three(values):
    high = values.astype(BF16).astype(F32)
    rest = values - high
    middle = rest.astype(BF16).astype(F32)
    return high, middle, rest - middle


def gelu_and_slope(z):
    size = jnp.abs(z)
    t = 1.0 / (1.0 + TAIL_RATE * size)
    poly = jnp.full_like(t, TAIL[-1])
    for coefficient in TAIL[-2::-1]:
        poly = poly * t + coefficient
    bell = jnp.exp2(z * z * (-0.5 * LOG2E))
    tail = poly * t * bell
    cdf = jnp.where(z > 0, 1.0 - tail, tail)
    return z * cdf, cdf + z * bell * (1.0 / math.sqrt(2.0 * math.pi))


def key_extra(head, keys, frames, masked):
    row = lax.broadcasted_iota(jnp.int32, (keys, 128), 0)
    lane = lax.broadcasted_iota(jnp.int32, (keys, 128), 1) - head * 16
    mask = jnp.where(row < frames, 0.0, MASKED)
    ones = jnp.where((lane > 0) & (lane < 4), 1.0, 0.0)
    return jnp.where(lane == 0, mask, ones).astype(BF16)


def attend_kernel(
    frames,
    x_ref,
    wq_ref,
    wk_ref,
    wv_ref,
    bq_ref,
    bv_ref,
    gain_ref,
    shift_ref,
    qa_ref,
    ka_ref,
    vt_ref,
    ht_ref,
    ot_ref,
    qe_ref,
    xs,
    scores,
    peaks,
    key_ext,
    log_rows,
):
    padded, width = xs.shape
    depth = width // HEADS
    xs[pl.ds(0, frames), :] = x_ref[...]
    xs[pl.ds(frames, padded - frames), :] = jnp.zeros((padded - frames, width), BF16)
    gain = gain_ref[...].astype(F32)
    shift = shift_ref[...].astype(F32)
    bq = bq_ref[...].astype(F32)
    bv = bv_ref[...].astype(F32)

    def project(i, carry):
        rows = pl.ds(pl.multiple_of(i * ROWS, ROWS), ROWS)
        unit, _ = normalize(xs[rows, :].astype(F32))
        h1 = (unit * gain + shift).astype(BF16)
        ht_ref[:, rows] = h1.T
        q = (dot(h1, wq_ref[...], NN) + bq).astype(BF16)
        k = dot(h1, wk_ref[...], NN).astype(BF16).astype(F32) * (LOG2E / math.sqrt(depth))
        v = (dot(h1, wv_ref[...], NN) + bv).astype(BF16)
        k_high = k.astype(BF16)
        k_low = (k - k_high.astype(F32)).astype(BF16)
        vt = v.T
        for h in range(HEADS):
            cols = slice(h * depth, (h + 1) * depth)
            qa_ref[h, rows, :] = jnp.concatenate([q[:, cols], q[:, cols]], axis=1)
            ka_ref[h, rows, :] = jnp.concatenate([k_high[:, cols], k_low[:, cols]], axis=1)
            vt_ref[h, 0:depth, rows] = vt[cols, :]
            vt_ref[h, depth : depth + 16, rows] = jnp.ones((16, ROWS), BF16)
        return carry

    lax.fori_loop(0, padded // ROWS, project, 0)

    blocks = padded // QUERIES
    steps = HEADS * blocks
    lane = lax.broadcasted_iota(jnp.int32, (QUERIES, 128), 1)
    query_ext = jnp.where(lane % 16 == 0, 1.0, 0.0).astype(BF16)

    def score(step, slot):
        head = step // blocks
        rows = pl.ds(pl.multiple_of((step % blocks) * QUERIES, QUERIES), QUERIES)
        key_ext[slot] = key_extra(head, padded, frames, True)
        left = jnp.concatenate([ka_ref[head], key_ext[slot]], axis=1)
        right = jnp.concatenate([qa_ref[head, rows, :], query_ext], axis=1)
        s = dot(left, right, NT)
        scores[slot] = s
        peaks[slot] = jnp.max(s, axis=0, keepdims=True)

    def finish(step, slot):
        head = step // blocks
        cols = pl.ds(pl.multiple_of((step % blocks) * QUERIES, QUERIES), QUERIES)
        peak = peaks[slot]
        weights = jnp.exp2(scores[slot] - peak).astype(BF16)
        mixed = dot(vt_ref[head], weights, NN)
        total = mixed[depth : depth + 1, :]
        rows = pl.ds(pl.multiple_of(head * depth, depth), depth)
        ot_ref[rows, cols] = (mixed[:depth, :] * (1.0 / total)).astype(BF16)
        log_rows[head, :, cols] = peak + jnp.log2(total)

    score(0, 0)

    def pair(i, carry):
        score(i * 2 + 1, 1)
        finish(i * 2, 0)
        score(jnp.minimum(i * 2 + 2, steps - 1), 0)
        finish(i * 2 + 1, 1)
        return carry

    lax.fori_loop(0, steps // 2, pair, 0)

    def extend(i, carry):
        rows = pl.ds(pl.multiple_of(i * ROWS, ROWS), ROWS)
        pieces = []
        for h in range(HEADS):
            high, middle, low = in_three(-log_rows[h, :, rows])
            pieces += [jnp.ones((1, ROWS), F32), high, middle, low, jnp.zeros((12, ROWS), F32)]
        qe_ref[rows, :] = jnp.concatenate(pieces, axis=0).T.astype(BF16)
        return carry

    lax.fori_loop(0, padded // ROWS, extend, 0)


def attend(x, wq, wk, wv, bq, bv, gain, shift):
    frames, width = x.shape
    padded = -(-frames // QUERIES) * QUERIES
    vmem = pl.BlockSpec(memory_space=pltpu.VMEM)
    return pl.pallas_call(
        functools.partial(attend_kernel, frames),
        out_shape=[
            jax.ShapeDtypeStruct((HEADS, padded, 128), BF16),
            jax.ShapeDtypeStruct((HEADS, padded, 128), BF16),
            jax.ShapeDtypeStruct((HEADS, 80, padded), BF16),
            jax.ShapeDtypeStruct((width, padded), BF16),
            jax.ShapeDtypeStruct((width, padded), BF16),
            jax.ShapeDtypeStruct((padded, 128), BF16),
        ],
        in_specs=[vmem] * 8,
        out_specs=[vmem] * 6,
        scratch_shapes=[
            pltpu.VMEM((padded, width), BF16),
            pltpu.VMEM((2, padded, QUERIES), F32),
            pltpu.VMEM((2, 1, QUERIES), F32),
            pltpu.VMEM((2, padded, 128), BF16),
            pltpu.VMEM((HEADS, 1, padded), F32),
        ],
        compiler_params=pltpu.CompilerParams(vmem_limit_bytes=60 << 20),
        name="attend",
    )(x, wq, wk, wv, bq, bv, gain, shift)


def mlp_kernel(
    frames,
    flag_ref,
    x_ref,
    cot_ref,
    ot_ref,
    wo_ref,
    wu_ref,
    wd_ref,
    bo_ref,
    bu_ref,
    bd_ref,
    gain_ref,
    shift_ref,
    out_ref,
    dx_ref,
    da_ref,
    gwo_ref,
    gwu_ref,
    gwd_ref,
    gbu_ref,
    small_ref,
):
    step = pl.program_id(0)
    rows, width = x_ref.shape
    hidden = wu_ref.shape[1]
    depth = width // HEADS

    @pl.when(step == 0)
    def _():
        gwo_ref[...] = jnp.zeros_like(gwo_ref)
        gwu_ref[...] = jnp.zeros_like(gwu_ref)
        gwd_ref[...] = jnp.zeros_like(gwd_ref)
        gbu_ref[...] = jnp.zeros_like(gbu_ref)
        small_ref[...] = jnp.zeros_like(small_ref)

    flag = flag_ref[0].astype(F32)
    inside = step * rows + lax.broadcasted_iota(jnp.int32, (rows, width), 0) < frames
    x = jnp.where(inside, x_ref[...].astype(F32), 0.0)
    dy = jnp.where(inside, cot_ref[...].astype(F32), 0.0) * flag
    dy_low = dy.astype(BF16)
    ot = ot_ref[...]
    o = ot.T
    x1 = x + (dot(o, wo_ref[...], NN) + bo_ref[...].astype(F32))
    unit, inv_std = normalize(x1)
    gain = gain_ref[...].astype(F32)
    h2 = (unit * gain + shift_ref[...].astype(F32)).astype(BF16)
    h2t = h2.T
    chunks = hidden // FF_CHUNK
    col = [slice(j * FF_CHUNK, (j + 1) * FF_CHUNK) for j in range(chunks)]
    z_next = dot(h2, wu_ref[:, col[0]], NN)
    out = x1 + bd_ref[...].astype(F32)
    dh2 = jnp.zeros((rows, width), F32)
    for j in range(chunks):
        z = z_next + bu_ref[:, col[j]].astype(F32)
        if j + 1 < chunks:
            z_next = dot(h2, wu_ref[:, col[j + 1]], NN)
        dg = dot(dy_low, wd_ref[col[j], :], NT)
        g, slope = gelu_and_slope(z)
        g = g.astype(BF16)
        dz = (dg * slope).astype(BF16)
        out = out + dot(g, wd_ref[col[j], :], NN)
        gwd_ref[col[j], :] += dot(g, dy_low, TN)
        gwu_ref[:, col[j]] += dot(h2t, dz, NN)
        gbu_ref[:, col[j]] += column_sums(dz.astype(F32))
        dh2 = dh2 + dot(dz, wu_ref[:, col[j]], NT)
    out_ref[...] = out * flag
    dx1 = dy + normalize_back(dh2, unit, inv_std, gain)
    dx_ref[...] = dx1
    da = dx1.astype(BF16)
    gwo_ref[...] += dot(ot, da, NN)
    do = dot(da, wo_ref[...], NT).astype(BF16)
    small_ref[0:1, :] += column_sums(da.astype(F32))
    small_ref[1:2, :] += column_sums(dy)
    small_ref[2:3, :] += column_sums(dh2 * unit)
    small_ref[3:4, :] += column_sums(dh2)
    prod = do.astype(F32) * o.astype(F32)
    lane = lax.broadcasted_iota(jnp.int32, (rows, 64), 1)
    for h in range(HEADS):
        cols = slice(h * depth, (h + 1) * depth)
        high, middle, low = in_three(-jnp.sum(prod[:, cols], axis=1, keepdims=True))
        extra = jnp.where(
            lane == 0, high, jnp.where(lane == 1, middle, jnp.where(lane == 2, low, 0.0))
        ).astype(BF16)
        da_ref[h, :, :] = jnp.concatenate([do[:, cols], extra], axis=1)


def mlp(flag, x, cot, ot, wo, wu, wd, bo, bu, bd, gain, shift):
    frames, width = x.shape
    hidden = wu.shape[1]
    padded = ot.shape[1]
    by_rows = pl.BlockSpec((ROWS, width), lambda i: (i, 0))
    whole = lambda shape: pl.BlockSpec(shape, lambda i: (0,) * len(shape))
    fixed = lambda shape: pl.BlockSpec(
        shape, lambda i: (0,) * len(shape), pipeline_mode=pl.Buffered(1)
    )
    return pl.pallas_call(
        functools.partial(mlp_kernel, frames),
        grid=(padded // ROWS,),
        out_shape=[
            jax.ShapeDtypeStruct((frames, width), F32),
            jax.ShapeDtypeStruct((frames, width), F32),
            jax.ShapeDtypeStruct((HEADS, padded, 128), BF16),
            jax.ShapeDtypeStruct((width, width), F32),
            jax.ShapeDtypeStruct((width, hidden), F32),
            jax.ShapeDtypeStruct((hidden, width), F32),
            jax.ShapeDtypeStruct((1, hidden), F32),
            jax.ShapeDtypeStruct((8, width), F32),
        ],
        in_specs=[
            pl.BlockSpec(memory_space=pltpu.SMEM),
            by_rows,
            by_rows,
            pl.BlockSpec((width, ROWS), lambda i: (0, i)),
            fixed((width, width)),
            fixed((width, hidden)),
            fixed((hidden, width)),
            fixed((1, width)),
            fixed((1, hidden)),
            fixed((1, width)),
            fixed((1, width)),
            fixed((1, width)),
        ],
        out_specs=[
            by_rows,
            by_rows,
            pl.BlockSpec((HEADS, ROWS, 128), lambda i: (0, i, 0)),
            fixed((width, width)),
            fixed((width, hidden)),
            fixed((hidden, width)),
            fixed((1, hidden)),
            fixed((8, width)),
        ],
        compiler_params=pltpu.CompilerParams(
            vmem_limit_bytes=60 << 20, dimension_semantics=("arbitrary",)
        ),
        name="mlp",
    )(flag, x, cot, ot, wo, wu, wd, bo, bu, bd, gain, shift)


def attend_back_kernel(
    frames,
    x_ref,
    dx_ref,
    qa_ref,
    ka_ref,
    vt_ref,
    ht_ref,
    qe_ref,
    da_ref,
    wq_ref,
    wk_ref,
    wv_ref,
    gain_ref,
    shift_ref,
    dinput_ref,
    gwq_ref,
    gwk_ref,
    gwv_ref,
    small_ref,
    dq,
    dkt,
    dvt,
    sum_k,
    sum_v,
    key_ext,
):
    padded = qa_ref.shape[1]
    width = ht_ref.shape[0]
    depth = width // HEADS

    def one_head(head, carry):
        key_ext[...] = key_extra(head, padded, frames, True)
        for i in range(padded // ROWS):
            rows = slice(i * ROWS, (i + 1) * ROWS)
            q = qa_ref[head, rows, :]
            d = da_ref[head, rows, :]
            s = dot(
                jnp.concatenate([q, qe_ref[rows, :]], axis=1),
                jnp.concatenate([ka_ref[head], key_ext[...]], axis=1),
                NT,
            )
            p = jnp.exp2(s)
            dp = dot(d[:, :80], vt_ref[head], NN)
            ds = (p * dp).astype(BF16)
            p = p.astype(BF16)
            new_v = dot(d[:, :depth], p, TN)
            new_k = dot(q[:, :depth], ds, TN)
            if i == 0:
                sum_v[...] = new_v
                sum_k[...] = new_k
            else:
                sum_v[...] += new_v
                sum_k[...] += new_k
            both = dot(ds, ka_ref[head], NN)
            both = both + pltpu.roll(both, depth, 1)
            dq[head, rows, :] = (both * LN2).astype(BF16)
        out_rows = pl.ds(pl.multiple_of(head * depth, depth), depth)
        dkt[out_rows, :] = (sum_k[...] * (1.0 / math.sqrt(depth))).astype(BF16)
        dvt[out_rows, :] = sum_v[...].astype(BF16)
        return carry

    lax.fori_loop(0, HEADS, one_head, 0)

    half = lax.broadcasted_iota(jnp.int32, (padded, 128), 1) < depth
    gwk_ref[...] = dot(ht_ref[...], dkt[...], NT)
    gwv_ref[...] = dot(ht_ref[...], dvt[...], NT)
    for h in range(0, HEADS, 2):
        both = jnp.where(half, dq[h], dq[h + 1])
        gwq_ref[:, h * depth : (h + 2) * depth] = dot(ht_ref[...], both, NN)

    gain = gain_ref[...].astype(F32)
    small_ref[...] = jnp.zeros_like(small_ref)
    for start in range(0, frames, ROWS):
        count = min(ROWS, frames - start)
        rows = slice(start, start + count)
        wide = slice(start, start + ROWS)
        some = half[:ROWS]
        dq_rows = jnp.concatenate(
            [jnp.where(some, dq[h, wide, :], dq[h + 1, wide, :]) for h in range(0, HEADS, 2)],
            axis=1,
        )
        dk_rows = dkt[:, wide].T
        dv_rows = dvt[:, wide].T
        dh1 = (
            dot(dq_rows, wq_ref[...], NT)
            + dot(dk_rows, wk_ref[...], NT)
            + dot(dv_rows, wv_ref[...], NT)
        )
        small_ref[0:1, :] += column_sums(dq_rows.astype(F32))
        small_ref[1:2, :] += column_sums(dv_rows.astype(F32))
        dh1 = dh1[:count]
        unit, inv_std = normalize(x_ref[rows, :].astype(F32))
        small_ref[2:3, :] += column_sums(dh1 * unit)
        small_ref[3:4, :] += column_sums(dh1)
        dinput_ref[rows, :] = dx_ref[rows, :] + normalize_back(dh1, unit, inv_std, gain)


def attend_back(x, dx, qa, ka, vt, ht, qe, da, wq, wk, wv, gain, shift):
    frames, width = x.shape
    padded = ht.shape[1]
    vmem = pl.BlockSpec(memory_space=pltpu.VMEM)
    return pl.pallas_call(
        functools.partial(attend_back_kernel, frames),
        out_shape=[
            jax.ShapeDtypeStruct((frames, width), F32),
            jax.ShapeDtypeStruct((width, width), F32),
            jax.ShapeDtypeStruct((width, width), F32),
            jax.ShapeDtypeStruct((width, width), F32),
            jax.ShapeDtypeStruct((8, width), F32),
        ],
        in_specs=[vmem] * 13,
        out_specs=[vmem] * 5,
        scratch_shapes=[
            pltpu.VMEM((HEADS, padded, 128), BF16),
            pltpu.VMEM((width, padded), BF16),
            pltpu.VMEM((width, padded), BF16),
            pltpu.VMEM((width // HEADS, padded), F32),
            pltpu.VMEM((width // HEADS, padded), F32),
            pltpu.VMEM((padded, 128), BF16),
        ],
        compiler_params=pltpu.CompilerParams(vmem_limit_bytes=60 << 20),
        name="attend_back",
    )(x, dx, qa, ka, vt, ht, qe, da, wq, wk, wv, gain, shift)


def per_device(windows, cotangent, valid, *owned):
    axes = ("batch", "shard")
    full = [lax.all_gather(part, axes, axis=0, tiled=True) for part in owned]
    wq, wk, wv, wo, wu, wd = full[:6]
    bq, bv, bo, bu, bd, gain_one, shift_one, gain_two, shift_two = [
        vector[None, :] for vector in full[6:]
    ]
    x, cot = windows[0], cotangent[0]
    qa, ka, vt, ht, ot, qe = attend(x, wq, wk, wv, bq, bv, gain_one, shift_one)
    out, dx, da, gwo, gwu, gwd, gbu, small_two = mlp(
        valid, x, cot, ot, wo, wu, wd, bo, bu, bd, gain_two, shift_two
    )
    dinput, gwq, gwk, gwv, small_one = attend_back(
        x, dx, qa, ka, vt, ht, qe, da, wq, wk, wv, gain_one, shift_one
    )
    totals = (
        gwq,
        gwk,
        gwv,
        gwo,
        gwu,
        gwd,
        small_one[0],
        small_one[1],
        small_two[0],
        gbu[0],
        small_two[1],
        small_one[2],
        small_one[3],
        small_two[2],
        small_two[3],
    )
    grads = [lax.psum_scatter(total, axes, scatter_dimension=0, tiled=True) for total in totals]
    return (out[None], dinput[None], *grads)


def solution(mesh):
    both = ("batch", "shard")
    windows_spec, matrix, vector = P(both, None, None), P(both, None), P(both)
    params = (matrix,) * 6 + (vector,) * 9
    return jax.shard_map(
        per_device,
        mesh=mesh,
        in_specs=(windows_spec, windows_spec, vector) + params,
        out_specs=(windows_spec, windows_spec) + params,
        check_vma=False,
    )
```

time: 1330 us -> 1200 us (0.902)
  matrix products: 323 us -> 0 us
  waiting for transfers between devices: 573 us -> 753 us
  Pallas kernels: 0 us -> 151 us
  other arithmetic: 110 us -> 0 us
  local copies, waits for them, and re-layouts: 55.4 us -> 35.6 us
    dot_general x74 -> x0, matrix products: 323 us -> none  [the longest x30 124 us: outer_cols(): lax.dot_general(left, right, (((1,), (1,)), ((), ())), preferred_element_...]
    reduce_scatter x6, waiting for transfers between devices: 572 us -> 749 us  [per_device(): lax.psum_scatter(total, axes, scatter_dimension=0, tiled=True)]
    pallas_call x0 -> x3, Pallas kernels: none -> 151 us  [the longest x1 59.5 us: attend_back(): pl.pallas_call(functools.partial(attend_back_kernel, frames), out_shape=[...]
    convert_element_type x18 -> x0, other arithmetic: 87.7 us -> none  [the longest x8 85.9 us: attend_back(): grad_scores = grad_scores.astype(jnp.bfloat16)]
    reduce_sum x15 -> x0, other arithmetic: 19.4 us -> none  [the longest x8 10.6 us: attend_head(): row_total = jnp.sum(exp_scores, axis=-1, keepdims=True)]
    unnamed x111 -> x41, local copies, waits for them, and re-layouts: 34 us -> 30.3 us
  transfers between devices with their start and end apart: 8 -> 8, of which waited for: 5 -> 6; matrix products, arithmetic and copies ran while one was open for 35% -> 3% of each run, Pallas kernels for 0% -> 3%
where the time goes in v1:
time: 1200 us
  waiting for transfers between devices  753 us (63%)
  blocking collectives  249 us (21%)
  Pallas kernels  151 us (13%)
  local copies, waits for them, and re-layouts  35.6 us (3%)
  between operations  14.9 us (1%)
    reduce_scatter x6, waiting for transfers between devices, per_device(): lax.psum_scatter(total, axes, scatter_dimension=0, tiled=True)  749 us
    all_gather x4, blocking collectives, per_device(): full = [lax.all_gather(part, axes, axis=0, tiled=True) for part in owned]  169 us
    unnamed x2, blocking collectives  79.9 us
    pallas_call x1, Pallas kernels, attend_back(): pl.pallas_call(functools.partial(attend_back_kernel, frames), out_shape=[...  59.5 us
    pallas_call x1, Pallas kernels, mlp(): pl.pallas_call(functools.partial(mlp_kernel, frames), grid=(padded // ROW...  58.9 us
    pallas_call x1, Pallas kernels, attend(): pl.pallas_call(functools.partial(attend_kernel, frames), out_shape=[jax.S...  32.3 us
    unnamed x41, local copies, waits for them, and re-layouts  30.3 us
  transfers between devices with their start and end apart: 8, of which 6 were waited for; matrix products, arithmetic and copies ran while one was open for 3% of the time, Pallas kernels for 3%

profile of v1, /device:TPU:0, one launch (start us, length us, event | category | flops | bytes accessed | tf_op | source)
XLA Modules:
  0.0 1204.2 jit_solution(7713971273077348467)
XLA Ops:
  7.2 0.7 all-gather.3.cloned.1.call-update
  8.0 0.7 all-gather.5.cloned.1.call-update
  8.7 0.9 dynamic-update-slice
  9.6 0.8 dynamic-update-slice.1
  10.5 0.8 dynamic-update-slice.2
  11.3 0.8 dynamic-update-slice.3
  12.2 0.8 dynamic-update-slice.4
  13.0 0.8 dynamic-update-slice.6
  13.9 0.8 dynamic-update-slice.7
  14.7 0.8 dynamic-update-slice.8
  15.5 0.8 dynamic-update-slice.5
  16.4 42.2 %all-reduce.19 = (bf16[512]{0:T(512)(128)(2,1)S(1)}, bf16[512]{0:T(512)(128)(2,1)S(1)}, bf16[512]{0:T(512)(128)(2,1)S(1)}, bf16[512]{0:T(512)(128)(2,1)S(1)}, bf...) all-reduce(bf16[512]{0:T(512)(128)(2,1)S(1)} %dynamic-update-slice,, ...), channel_id=1, replica_groups=mesh['batch'=8,'shard'=4] {'batch','shard'}, use_global_device_ids=true, to_apply=%add | all-reduce | flops 6144 | bytes 24576
  58.6 0.6 broadcast_in_dim.35.gain_ref
  59.2 0.6 broadcast_in_dim.36.shift_ref
  59.8 0.6 broadcast_in_dim.33.bq_ref
  60.4 0.6 broadcast_in_dim.34.bv_ref
  61.0 0.6 broadcast_in_dim.38.bu_ref
  61.6 0.6 broadcast_in_dim.37.bo_ref
  62.1 0.6 broadcast_in_dim.39.bd_ref
  62.7 0.6 broadcast_in_dim.40.gain_ref
  63.3 0.6 broadcast_in_dim.41.shift_ref
  64.6 44.6 %all_gather.45.wq_ref = bf16[512,512]{1,0:T(8,128)(2,1)} all-gather(bf16[16,512]{1,0:T(8,128)(2,1)} %param.21), channel_id=1, replica_groups=mesh['batch'=8,'shard'=4] {'batch','shard'}, dimensions={0}, use_global_device_ids=true | all-gather | bytes 540672 | tf_op jit(solution)/shard_map/all_gather | solution.py:486
  109.2 41.4 %all_gather.46.wk_ref = bf16[512,512]{1,0:T(8,128)(2,1)} all-gather(bf16[16,512]{1,0:T(8,128)(2,1)} %param.22), channel_id=1, replica_groups=mesh['batch'=8,'shard'=4] {'batch','shard'}, dimensions={0}, use_global_device_ids=true | all-gather | bytes 540672 | tf_op jit(solution)/shard_map/all_gather | solution.py:486
  150.6 42.1 %all_gather.47.wv_ref = bf16[512,512]{1,0:T(8,128)(2,1)} all-gather(bf16[16,512]{1,0:T(8,128)(2,1)} %param.23), channel_id=1, replica_groups=mesh['batch'=8,'shard'=4] {'batch','shard'}, dimensions={0}, use_global_device_ids=true | all-gather | bytes 540672 | tf_op jit(solution)/shard_map/all_gather | solution.py:486
  192.7 32.3 %attend.1 = (bf16[8,1536,128]{2,1,0:T(8,128)(2,1)}, bf16[8,1536,128]{2,1,0:T(8,128)(2,1)}, bf16[8,80,1536]{2,1,0:T(8,128)(2,1)}, bf16[512,1536]{1,0:T(8,128)(2,1...) custom-call(bf16[1500,512]{1,0:T(8,128)(2,1)} %bitcast.13, bf16[512,512]{1,0:T(8,128)(2,1)} %all_gather.45.wq_ref, ...), custom_call_target="tpu_custom_call" | custom-call | tf_op jit(solution)/shard_map/attend/pallas_call | solution.py:194
  225.0 41.2 %all_gather.52.wo_ref = bf16[512,512]{1,0:T(8,128)(2,1)} all-gather(bf16[16,512]{1,0:T(8,128)(2,1)S(1)} %copy-done.2), channel_id=1, replica_groups=mesh['batch'=8,'shard'=4] {'batch','shard'}, dimensions={0}, use_global_device_ids=true | all-gather | bytes 540672 | tf_op jit(solution)/shard_map/all_gather | solution.py:486
  266.2 58.9 %mlp.1 = (f32[1500,512]{1,0:T(8,128)}, f32[1500,512]{1,0:T(8,128)}, bf16[8,1536,128]{2,1,0:T(8,128)(2,1)}, f32[512,512]{1,0:T(8,128)}, f32[512,2048]{1,0:T(8,128...) custom-call(s32[1]{0:T(128)S(6)} %copy.48.flag_ref, bf16[1500,512]{1,0:T(8,128)(2,1)} %bitcast.14, ...), custom_call_target="tpu_custom_call" | custom-call | tf_op jit(solution)/shard_map/mlp/pallas_call | solution.py:314
  325.1 59.5 %attend_back.1 = (f32[1500,512]{1,0:T(8,128)}, f32[512,512]{1,0:T(8,128)}, f32[512,512]{1,0:T(8,128)}, f32[512,512]{1,0:T(8,128)}, f32[8,512]{1,0:T(8,128)}) custom-call(bf16[1500,512]{1,0:T(8,128)(2,1)} %bitcast.15, f32[1500,512]{1,0:T(8,128)} %get-tuple-element.38.dx_ref, bf16[8,1536,128]{2,1,0:T(8,128)(2,1)} %get-tuple-element.39.qa_ref, ...), custom_call_target="tpu_custom_call" | custom-call | tf_op jit(solution)/shard_map/attend_back/pallas_call | solution.py:460
  386.4 0.7 reduce-scatter.15.cloned.1.call-update
  387.2 0.7 reduce-scatter.17.cloned.1.call-update
  388.0 37.7 %all-reduce.18 = (f32[512]{0:T(512)S(1)}, f32[512]{0:T(512)S(1)}, f32[512]{0:T(512)S(1)}, f32[2048]{0:T(1024)S(1)}, f32[512]{0:T(512)S(1)}, /*index=5*/f32[512]{...) all-reduce(f32[512]{0:T(512)S(1)} %bitcast.23, ...), channel_id=8, replica_groups=mesh['batch'=8,'shard'=4] {'batch','shard'}, use_global_device_ids=true, to_apply=%region_6.0.clone | all-reduce | flops 6144 | bytes 49152
  425.6 0.6 dynamic-slice
  426.2 0.6 dynamic-slice.1
  426.8 0.6 dynamic-slice.2
  427.4 0.6 dynamic-slice.4
  428.0 0.6 dynamic-slice.5
  428.6 0.6 dynamic-slice.6
  429.1 0.6 dynamic-slice.7
  429.7 0.6 dynamic-slice.8
  430.3 8.7 copy.38
  439.0 8.7 copy.37
  447.8 0.6 dynamic-slice.3
  448.3 68.5 %reduce-scatter.11.cloned.1.call-done = f32[16,512]{1,0:T(8,128)} async-done(((f32[512,512]{1,0:T(8,128)}), f32[16,512]{1,0:T(8,128)}) %reduce-scatter.11.cloned.1.call-update) | async-done | bytes 32784 | tf_op jit(solution)/shard_map/reduce_scatter | solution.py:516
  516.9 133.6 %reduce-scatter.7.cloned.1.call-done = f32[16,512]{1,0:T(8,128)} async-done(((f32[512,512]{1,0:T(8,128)}), f32[16,512]{1,0:T(8,128)}) %reduce-scatter.7.cloned.1.call-update) | async-done | bytes 32784 | tf_op jit(solution)/shard_map/reduce_scatter | solution.py:516
  650.4 133.4 %reduce-scatter.9.cloned.1.call-done = f32[16,512]{1,0:T(8,128)} async-done(((f32[512,512]{1,0:T(8,128)}), f32[16,512]{1,0:T(8,128)}) %reduce-scatter.9.cloned.1.call-update) | async-done | bytes 32784 | tf_op jit(solution)/shard_map/reduce_scatter | solution.py:516
  783.8 133.5 %reduce-scatter.13.cloned.1.call-done = f32[16,512]{1,0:T(8,128)} async-done(((f32[512,512]{1,0:T(8,128)}), f32[16,512]{1,0:T(8,128)}) %reduce-scatter.13.cloned.1.call-update) | async-done | bytes 32784 | tf_op jit(solution)/shard_map/reduce_scatter | solution.py:516
  917.3 140.2 %reduce-scatter.15.cloned.1.call-done = f32[16,2048]{1,0:T(8,128)} async-done(((f32[512,2048]{1,0:T(8,128)}), f32[16,2048]{1,0:T(8,128)}) %reduce-scatter.15.cloned.1.call-update) | async-done | bytes 131088 | tf_op jit(solution)/shard_map/reduce_scatter | solution.py:516
  1057.4 140.0 %reduce-scatter.17.cloned.1.call-done = f32[64,512]{1,0:T(8,128)} async-done(((f32[2048,512]{1,0:T(8,128)}), f32[64,512]{1,0:T(8,128)}) %reduce-scatter.17.cloned.1.call-update) | async-done | bytes 131088 | tf_op jit(solution)/shard_map/reduce_scatter | solution.py:516
  (37 shorter events, 2.0 us)
Async XLA Ops:
  7.2 217.8 %copy-start.2 = (bf16[16,512]{1,0:T(8,128)(2,1)S(1)}, bf16[16,512]{1,0:T(8,128)(2,1)}, u32[]{:S(2)}) copy-start(bf16[16,512]{1,0:T(8,128)(2,1)} %param.24) | copy-start | bytes 49156
  7.2 259.0 %all-gather.3.cloned.1.call-start = ((), (), s32[]{:S(2)}) async-start(), calls=%async_computation.6 | async-start | bytes 2162688 | tf_op jit(solution)/shard_map/all_gather | solution.py:486
  7.9 258.3 %all-gather.5.cloned.1.call-start = ((), (), s32[]{:S(2)}) async-start(), calls=%async_computation.7 | async-start | bytes 2162688 | tf_op jit(solution)/shard_map/all_gather | solution.py:486
  8.7 508.2 %reduce-scatter.11.cloned.1.call-start = ((), (), s32[]{:S(2)}) async-start(), calls=%async_computation.10 | async-start | bytes 1081344 | tf_op jit(solution)/shard_map/reduce_scatter | solution.py:516
  384.6 265.8 %reduce-scatter.7.cloned.1.call-start = ((), (), s32[]{:S(2)}) async-start(), calls=%async_computation.8 | async-start | bytes 1081344 | tf_op jit(solution)/shard_map/reduce_scatter | solution.py:516
  385.2 398.6 %reduce-scatter.9.cloned.1.call-start = ((), (), s32[]{:S(2)}) async-start(), calls=%async_computation.9 | async-start | bytes 1081344 | tf_op jit(solution)/shard_map/reduce_scatter | solution.py:516
  385.8 531.5 %reduce-scatter.13.cloned.1.call-start = ((), (), s32[]{:S(2)}) async-start(), calls=%async_computation.11 | async-start | bytes 1081344 | tf_op jit(solution)/shard_map/reduce_scatter | solution.py:516
  386.4 671.1 %reduce-scatter.15.cloned.1.call-start = ((), (), s32[]{:S(2)}) async-start(), calls=%async_computation.12 | async-start | bytes 4325376 | tf_op jit(solution)/shard_map/reduce_scatter | solution.py:516
  387.1 0.8 copy-start.5
  387.1 0.8 copy-start.4
  387.1 0.8 copy-start.3
  387.1 43.2 %copy-start.1 = (f32[1500,512]{1,0:T(8,128)S(1)}, f32[1500,512]{1,0:T(8,128)}, u32[]{:S(2)}) copy-start(f32[1500,512]{1,0:T(8,128)} %get-tuple-element.45) | copy-start | bytes 9216004
  387.2 810.2 %reduce-scatter.17.cloned.1.call-start = ((), (), s32[]{:S(2)}) async-start(), calls=%async_computation.13 | async-start | bytes 4325376 | tf_op jit(solution)/shard_map/reduce_scatter | solution.py:516
  430.3 8.7 copy-start
Sparse Core Ops, SparseCore 0:
  10.9 59.1 all-gather.2
  73.0 56.1 all-gather.4
  384.7 132.0 reduce-scatter.10
  519.6 130.7 reduce-scatter.6
  653.1 130.6 reduce-scatter.8
  786.6 130.6 reduce-scatter.12
  920.1 137.2 reduce-scatter.14
  1060.3 137.0 reduce-scatter.16

commit v2 on v1

v2 whole, which is shorter than its diff:
```python
import functools
import math

import jax
import jax.numpy as jnp
from jax import lax
from jax.experimental import pallas as pl
from jax.experimental.pallas import tpu as pltpu
from jax.sharding import PartitionSpec as P

HEADS = 8
NORM_EPS = 1e-05
LOG2E = math.log2(math.e)
LN2 = math.log(2.0)
F32 = jnp.float32
BF16 = jnp.bfloat16
MESH = pl.DeviceIdType.MESH
ROWS = 256
QUERIES = 768
FF_CHUNK = 512
MASKED = -1e30

NN = (((1,), (0,)), ((), ()))
NT = (((1,), (1,)), ((), ()))
TN = (((0,), (0,)), ((), ()))

TAIL_RATE = 0.2625
TAIL = (
    0.10474836168174968,
    0.10416468281706748,
    0.10263486984927783,
    0.056568077030165455,
    0.14744499390073365,
    -0.13092736820325213,
    0.23259357413631826,
    -0.14775373854130247,
    0.03052653723595064,
)


def dot(left, right, dims):
    return lax.dot_general(left, right, dims, preferred_element_type=F32)


def normalize(values):
    centred = values - jnp.mean(values, axis=-1, keepdims=True)
    variance = jnp.mean(centred * centred, axis=-1, keepdims=True)
    inv_std = lax.rsqrt(variance + NORM_EPS)
    return centred * inv_std, inv_std


def normalize_back(grad_rows, unit_rows, inv_std, gain):
    scaled = grad_rows * gain
    first_mean = jnp.mean(scaled, axis=-1, keepdims=True)
    second_mean = jnp.mean(scaled * unit_rows, axis=-1, keepdims=True)
    return inv_std * (scaled - first_mean - unit_rows * second_mean)


def column_sums(rows):
    return jnp.sum(rows, axis=0, keepdims=True)


def in_three(values):
    high = values.astype(BF16).astype(F32)
    rest = values - high
    middle = rest.astype(BF16).astype(F32)
    return high, middle, rest - middle


def gelu_and_slope(z):
    size = jnp.abs(z)
    t = 1.0 / (1.0 + TAIL_RATE * size)
    poly = jnp.full_like(t, TAIL[-1])
    for coefficient in TAIL[-2::-1]:
        poly = poly * t + coefficient
    bell = jnp.exp2(z * z * (-0.5 * LOG2E))
    tail = poly * t * bell
    cdf = jnp.where(z > 0, 1.0 - tail, tail)
    return z * cdf, cdf + z * bell * (1.0 / math.sqrt(2.0 * math.pi))


def key_extra(head, keys, frames):
    row = lax.broadcasted_iota(jnp.int32, (keys, 128), 0)
    lane = lax.broadcasted_iota(jnp.int32, (keys, 128), 1) - head * 16
    mask = jnp.where(row < frames, 0.0, MASKED)
    ones = jnp.where((lane > 0) & (lane < 4), 1.0, 0.0)
    return jnp.where(lane == 0, mask, ones).astype(BF16)


class Place:
    def __init__(self, mesh_shape):
        self.batch, self.shard = mesh_shape
        self.deep = self.batch // 2
        b, s = lax.axis_index("batch"), lax.axis_index("shard")
        self.z, self.x, self.y, self.core = b // 2, b % 2, s // 2, s % 2
        self.me = b * self.shard + s
        self.square = self.x * 2 + self.y

    def moved(self, dz=0, dxy=0, flip=0):
        dx, dy = dxy // 2, dxy % 2
        x = 1 - self.x if dx else self.x
        y = 1 - self.y if dy else self.y
        core = 1 - self.core if flip else self.core
        return (self.z + self.deep + dz) % self.deep * 2 + x, y * 2 + core

    def block(self, dz=0, dxy=0, flip=0):
        b, s = self.moved(-dz, dxy, flip)
        return b * self.shard + s

    def partners(self):
        far = [self.moved(dz=dz) for dz in range(1, self.deep)]
        near = [self.moved(dxy=dxy) for dxy in range(1, 4)]
        return far + near + [self.moved(flip=1)]

    def meet(self):
        barrier = pltpu.get_barrier_semaphore()
        for partner in self.partners():
            pl.semaphore_signal(barrier, inc=1, device_id=partner, device_id_type=MESH)
        pl.semaphore_wait(barrier, self.deep + 3)


class Spread:
    def __init__(self, place, own, table, send_sem, recv_sem):
        self.place, self.own, self.table = place, own, table
        self.send_sem, self.recv_sem = send_sem, recv_sem
        self.started = []

    def copy(self, slot, dz, dxy, device):
        block = self.place.block(dz, dxy)
        here = dz == 0 and dxy == 0
        return pltpu.make_async_remote_copy(
            src_ref=self.own if here else self.table.at[block],
            dst_ref=self.table.at[block],
            send_sem=self.send_sem.at[slot],
            recv_sem=self.recv_sem.at[slot],
            device_id=device,
            device_id_type=MESH,
        )

    def far(self, dz):
        return self.copy(dz - 1, 0, 0, self.place.moved(dz=dz))

    def near(self, dz, dxy):
        slot = self.place.deep - 1 + dz * 3 + dxy - 1
        return self.copy(slot, dz, 0, self.place.moved(dxy=dxy))

    def across(self, dz, dxy):
        slot = self.place.deep * 4 - 1 + dz * 4 + dxy
        return self.copy(slot, dz, dxy, self.place.moved(flip=1))

    def launch(self, copy):
        copy.start()
        self.started.append(copy)

    def begin(self):
        for dz in range(1, self.place.deep):
            self.launch(self.far(dz))
        for dxy in range(1, 4):
            self.launch(self.near(0, dxy))
        self.launch(self.across(0, 0))

    def relay_far(self):
        for dz in range(1, self.place.deep):
            self.far(dz).wait_recv()
            for dxy in range(1, 4):
                self.launch(self.near(dz, dxy))
            self.launch(self.across(dz, 0))

    def relay_near(self):
        for dz in range(self.place.deep):
            for dxy in range(1, 4):
                self.near(dz, dxy).wait_recv()
                self.launch(self.across(dz, dxy))

    def arrive(self):
        for dz in range(self.place.deep):
            for dxy in range(4):
                self.across(dz, dxy).wait_recv()

    def drain(self):
        deep = self.place.deep
        for dz in range(1, deep):
            self.far(dz).wait_send()
        for dz in range(deep):
            for dxy in range(1, 4):
                self.near(dz, dxy).wait_send()
        for dz in range(deep):
            for dxy in range(4):
                self.across(dz, dxy).wait_send()


def spread_small(vector, place):
    row = vector.astype(F32)
    width = 2 * row.shape[1]
    row = jnp.broadcast_to(jnp.concatenate([row, row], axis=1), (8, width))
    lane = lax.broadcasted_iota(jnp.int32, (8, width), 1)
    line = lax.broadcasted_iota(jnp.int32, (8, width), 0)
    short = row
    for p in range(1, 8):
        short = jnp.where(line == p, pltpu.roll(row, width - 16 * p, 1), short)
    start = place.me * 16
    short = pltpu.roll(short, start, 1)
    short = jnp.where((lane >= start) & (lane < start + 16), short, 0.0)
    start = place.me % 8 * 64
    long = pltpu.roll(pltpu.roll(row, width - 128, 1), start, 1)
    long = jnp.where((lane >= start) & (lane < start + 64) & (line == place.me // 8), long, 0.0)
    return jnp.concatenate([long, short], axis=0).astype(BF16)


def matrix(table, first, count=16):
    part = table[:, first : first + count, :]
    return part.reshape(part.shape[0] * count, part.shape[2])


def attend_kernel(frames, mesh_shape, *refs):
    if mesh_shape is None:
        x_ref, table, small_ref = refs[:3]
        qa_ref, ka_ref, vt_ref, ht_ref, ot_ref, qe_ref = refs[3:9]
        xs, scores, peaks, key_ext, log_rows = refs[9:]
    else:
        x_ref, vec_ref, wq_own, wk_own, wv_own, wo_own, wu_own, wd_own = refs[:8]
        qa_ref, ka_ref, vt_ref, ht_ref, ot_ref, qe_ref, small_ref, first_ref, second_ref = refs[
            8:17
        ]
        xs, scores, peaks, key_ext, log_rows, table, own, send_1, recv_1, send_2, recv_2, keep = (
            refs[17:]
        )
        place = Place(mesh_shape)
        first = Spread(place, table.at[place.me], table, send_1, recv_1)
        second = Spread(place, own, second_ref, send_2, recv_2)
        table[place.me, 0:16, :] = wq_own[...]
        table[place.me, 16:32, :] = wk_own[...]
        table[place.me, 32:48, :] = wv_own[...]
        table[place.me, 48:64, :] = spread_small(vec_ref[...], place)
        own[0:16, :] = wo_own[...]
        chunks = wu_own.shape[1] // FF_CHUNK
        for j in range(chunks):
            own[16 + 16 * j : 32 + 16 * j, :] = wu_own[:, j * FF_CHUNK : (j + 1) * FF_CHUNK]
        own[16 + 16 * chunks :, :] = wd_own[...]
        place.meet()
        first.begin()
        first.relay_far()
        first.relay_near()
        second.begin()
        keep_own = pltpu.make_async_copy(own, second_ref.at[place.me], keep.at[0])
        keep_own.start()

    padded, width = xs.shape
    depth = width // HEADS
    xs[pl.ds(0, frames), :] = x_ref[...]
    xs[pl.ds(frames, padded - frames), :] = jnp.zeros((padded - frames, width), BF16)
    if mesh_shape is not None:
        first.arrive()
        keep_first = pltpu.make_async_copy(table, first_ref, keep.at[1])
        keep_first.start()
        small_ref[...] = jnp.sum(table[:, 48:64, :].astype(F32), axis=0)
    bq, bv, gain, shift = (small_ref[r : r + 1, :] for r in (8, 9, 12, 13))

    def project(i, carry):
        rows = pl.ds(pl.multiple_of(i * ROWS, ROWS), ROWS)
        unit, _ = normalize(xs[rows, :].astype(F32))
        h1 = (unit * gain + shift).astype(BF16)
        ht_ref[:, rows] = h1.T
        q = (dot(h1, matrix(table, 0), NN) + bq).astype(BF16)
        k = dot(h1, matrix(table, 16), NN).astype(BF16).astype(F32)
        k = k * (LOG2E / math.sqrt(depth))
        v = (dot(h1, matrix(table, 32), NN) + bv).astype(BF16)
        k_high = k.astype(BF16)
        k_low = (k - k_high.astype(F32)).astype(BF16)
        vt = v.T
        for h in range(HEADS):
            cols = slice(h * depth, (h + 1) * depth)
            qa_ref[h, rows, :] = jnp.concatenate([q[:, cols], q[:, cols]], axis=1)
            ka_ref[h, rows, :] = jnp.concatenate([k_high[:, cols], k_low[:, cols]], axis=1)
            vt_ref[h, 0:depth, rows] = vt[cols, :]
            vt_ref[h, depth : depth + 16, rows] = jnp.ones((16, ROWS), BF16)
        return carry

    lax.fori_loop(0, padded // ROWS, project, 0)

    blocks = padded // QUERIES
    steps = HEADS * blocks
    lane = lax.broadcasted_iota(jnp.int32, (QUERIES, 128), 1)
    query_ext = jnp.where(lane % 16 == 0, 1.0, 0.0).astype(BF16)

    def score(step, slot):
        head = step // blocks
        rows = pl.ds(pl.multiple_of((step % blocks) * QUERIES, QUERIES), QUERIES)
        key_ext[slot] = key_extra(head, padded, frames)
        left = jnp.concatenate([ka_ref[head], key_ext[slot]], axis=1)
        right = jnp.concatenate([qa_ref[head, rows, :], query_ext], axis=1)
        s = dot(left, right, NT)
        scores[slot] = s
        peaks[slot] = jnp.max(s, axis=0, keepdims=True)

    def finish(step, slot):
        head = step // blocks
        cols = pl.ds(pl.multiple_of((step % blocks) * QUERIES, QUERIES), QUERIES)
        peak = peaks[slot]
        weights = jnp.exp2(scores[slot] - peak).astype(BF16)
        mixed = dot(vt_ref[head], weights, NN)
        total = mixed[depth : depth + 1, :]
        rows = pl.ds(pl.multiple_of(head * depth, depth), depth)
        ot_ref[rows, cols] = (mixed[:depth, :] * (1.0 / total)).astype(BF16)
        log_rows[head, :, cols] = peak + jnp.log2(total)

    score(0, 0)

    def pair(i, carry):
        if mesh_shape is not None:
            pl.when(i == 1)(second.relay_far)
            pl.when(i == 5)(second.relay_near)
        score(i * 2 + 1, 1)
        finish(i * 2, 0)
        score(jnp.minimum(i * 2 + 2, steps - 1), 0)
        finish(i * 2 + 1, 1)
        return carry

    lax.fori_loop(0, steps // 2, pair, 0)

    def extend(i, carry):
        rows = pl.ds(pl.multiple_of(i * ROWS, ROWS), ROWS)
        pieces = []
        for h in range(HEADS):
            high, middle, low = in_three(-log_rows[h, :, rows])
            pieces += [jnp.ones((1, ROWS), F32), high, middle, low, jnp.zeros((12, ROWS), F32)]
        qe_ref[rows, :] = jnp.concatenate(pieces, axis=0).T.astype(BF16)
        return carry

    lax.fori_loop(0, padded // ROWS, extend, 0)
    if mesh_shape is not None:
        second.arrive()
        keep_own.wait()
        keep_first.wait()
        first.drain()
        second.drain()


def attend(mesh_shape, x, *rest):
    frames, width = x.shape
    padded = -(-frames // QUERIES) * QUERIES
    blocks = width // 16
    vmem = pl.BlockSpec(memory_space=pltpu.VMEM)
    anywhere = pl.BlockSpec(memory_space=pl.ANY)
    out_shape = [
        jax.ShapeDtypeStruct((HEADS, padded, 128), BF16),
        jax.ShapeDtypeStruct((HEADS, padded, 128), BF16),
        jax.ShapeDtypeStruct((HEADS, 80, padded), BF16),
        jax.ShapeDtypeStruct((width, padded), BF16),
        jax.ShapeDtypeStruct((width, padded), BF16),
        jax.ShapeDtypeStruct((padded, 128), BF16),
    ]
    scratch = [
        pltpu.VMEM((padded, width), BF16),
        pltpu.VMEM((2, padded, QUERIES), F32),
        pltpu.VMEM((2, 1, QUERIES), F32),
        pltpu.VMEM((2, padded, 128), BF16),
        pltpu.VMEM((HEADS, 1, padded), F32),
    ]
    out_specs = [vmem] * 6
    options = {}
    if mesh_shape is not None:
        hidden = rest[5].shape[1]
        own_rows = 16 + hidden // FF_CHUNK * 16 + rest[6].shape[0]
        out_shape += [
            jax.ShapeDtypeStruct((16, width), F32),
            jax.ShapeDtypeStruct((blocks, 64, width), BF16),
            jax.ShapeDtypeStruct((blocks, own_rows, width), BF16),
        ]
        out_specs += [vmem, anywhere, anywhere]
        scratch += [
            pltpu.VMEM((blocks, 64, width), BF16),
            pltpu.VMEM((own_rows, width), BF16),
        ]
        scratch += [pltpu.SemaphoreType.DMA((blocks - 1,)) for _ in range(4)]
        scratch += [pltpu.SemaphoreType.DMA((2,))]
        options = dict(collective_id=0, has_side_effects=True)
    return pl.pallas_call(
        functools.partial(attend_kernel, frames, mesh_shape),
        out_shape=out_shape,
        in_specs=[vmem] * (1 + len(rest)),
        out_specs=out_specs,
        scratch_shapes=scratch,
        compiler_params=pltpu.CompilerParams(vmem_limit_bytes=60 << 20, **options),
        name="attend",
    )(x, *rest)


def mlp_kernel(
    frames,
    flag_ref,
    x_ref,
    cot_ref,
    ot_ref,
    table,
    vec_ref,
    out_ref,
    dx_ref,
    da_ref,
    grads_ref,
    small_ref,
    gwo,
    gwu,
    gwd,
):
    step = pl.program_id(0)
    rows, width = x_ref.shape
    chunks = gwu.shape[0]
    depth = width // HEADS
    down = table.shape[1] - 16 - 16 * chunks
    per_chunk = FF_CHUNK // down

    def up_part(j):
        return matrix(table, 16 + 16 * j)

    def down_part(j):
        part = table[j * per_chunk : (j + 1) * per_chunk, 16 + 16 * chunks :, :]
        return part.reshape(FF_CHUNK, width)

    @pl.when(step == 0)
    def _():
        gwo[...] = jnp.zeros_like(gwo)
        gwu[...] = jnp.zeros_like(gwu)
        gwd[...] = jnp.zeros_like(gwd)
        small_ref[...] = jnp.zeros_like(small_ref)

    flag = flag_ref[0].astype(F32)
    inside = step * rows + lax.broadcasted_iota(jnp.int32, (rows, width), 0) < frames
    x = jnp.where(inside, x_ref[...].astype(F32), 0.0)
    dy = jnp.where(inside, cot_ref[...].astype(F32), 0.0) * flag
    dy_low = dy.astype(BF16)
    bo, bd, gain, shift = (vec_ref[r : r + 1, :] for r in (10, 11, 14, 15))
    wo = matrix(table, 0)
    ot = ot_ref[...]
    o = ot.T
    x1 = x + (dot(o, wo, NN) + bo)
    unit, inv_std = normalize(x1)
    h2 = (unit * gain + shift).astype(BF16)
    h2t = h2.T
    z_next = dot(h2, up_part(0), NN)
    out = x1 + bd
    dh2 = jnp.zeros((rows, width), F32)
    for j in range(chunks):
        z = z_next + vec_ref[j : j + 1, :]
        if j + 1 < chunks:
            z_next = dot(h2, up_part(j + 1), NN)
        dg = dot(dy_low, down_part(j), NT)
        g, slope = gelu_and_slope(z)
        g = g.astype(BF16)
        dz = (dg * slope).astype(BF16)
        out = out + dot(g, down_part(j), NN)
        gwd[j] += dot(g, dy_low, TN)
        gwu[j] += dot(h2t, dz, NN)
        small_ref[j : j + 1, :] += column_sums(dz.astype(F32))
        dh2 = dh2 + dot(dz, up_part(j), NT)
    out_ref[...] = out * flag
    dx1 = dy + normalize_back(dh2, unit, inv_std, gain)
    dx_ref[...] = dx1
    da = dx1.astype(BF16)
    gwo[...] += dot(ot, da, NN)
    do = dot(da, wo, NT).astype(BF16)
    small_ref[10:11, :] += column_sums(da.astype(F32))
    small_ref[11:12, :] += column_sums(dy)
    small_ref[14:15, :] += column_sums(dh2 * unit)
    small_ref[15:16, :] += column_sums(dh2)
    prod = do.astype(F32) * o.astype(F32)
    lane = lax.broadcasted_iota(jnp.int32, (rows, 64), 1)
    for h in range(HEADS):
        cols = slice(h * depth, (h + 1) * depth)
        high, middle, low = in_three(-jnp.sum(prod[:, cols], axis=1, keepdims=True))
        extra = jnp.where(
            lane == 0, high, jnp.where(lane == 1, middle, jnp.where(lane == 2, low, 0.0))
        ).astype(BF16)
        da_ref[h, :, :] = jnp.concatenate([do[:, cols], extra], axis=1)

    @pl.when(step == pl.num_programs(0) - 1)
    def _():
        split = lambda part, count: part.astype(BF16).reshape(-1, count, width)
        grads_ref[:, 0:16, :] = split(gwo[...], 16)
        for j in range(chunks):
            grads_ref[:, 16 + 16 * j : 32 + 16 * j, :] = split(gwu[j], 16)
            grads_ref[j * per_chunk : (j + 1) * per_chunk, 16 + 16 * chunks :, :] = split(
                gwd[j], down
            )


def mlp(flag, x, cot, ot, table, vectors):
    frames, width = x.shape
    padded = ot.shape[1]
    blocks, rows = table.shape[:2]
    chunks = (rows - 16) * blocks // (2 * FF_CHUNK)
    by_rows = pl.BlockSpec((ROWS, width), lambda i: (i, 0))
    fixed = lambda shape: pl.BlockSpec(
        shape, lambda i: (0,) * len(shape), pipeline_mode=pl.Buffered(1)
    )
    return pl.pallas_call(
        functools.partial(mlp_kernel, frames),
        grid=(padded // ROWS,),
        out_shape=[
            jax.ShapeDtypeStruct((frames, width), F32),
            jax.ShapeDtypeStruct((frames, width), F32),
            jax.ShapeDtypeStruct((HEADS, padded, 128), BF16),
            jax.ShapeDtypeStruct(table.shape, BF16),
            jax.ShapeDtypeStruct((16, width), F32),
        ],
        in_specs=[
            pl.BlockSpec(memory_space=pltpu.SMEM),
            by_rows,
            by_rows,
            pl.BlockSpec((width, ROWS), lambda i: (0, i)),
            fixed(table.shape),
            fixed((16, width)),
        ],
        out_specs=[
            by_rows,
            by_rows,
            pl.BlockSpec((HEADS, ROWS, 128), lambda i: (0, i, 0)),
            fixed(table.shape),
            fixed((16, width)),
        ],
        scratch_shapes=[
            pltpu.VMEM((width, width), F32),
            pltpu.VMEM((chunks, width, FF_CHUNK), F32),
            pltpu.VMEM((chunks, FF_CHUNK, width), F32),
        ],
        compiler_params=pltpu.CompilerParams(
            vmem_limit_bytes=60 << 20, dimension_semantics=("arbitrary",)
        ),
        name="mlp",
    )(flag, x, cot, ot, table, vectors)


class Gather:
    def __init__(self, place, source, from_core, halves, from_near, quarter, from_far, sems):
        self.place, self.source = place, source
        self.from_core, self.halves = from_core, halves
        self.from_near, self.quarter = from_near, quarter
        self.from_far = from_far
        self.send_sem, self.recv_sem = sems

    def copy(self, slot, src, dst, device):
        return pltpu.make_async_remote_copy(
            src_ref=src,
            dst_ref=dst,
            send_sem=self.send_sem.at[slot],
            recv_sem=self.recv_sem.at[slot],
            device_id=device,
            device_id_type=MESH,
        )

    def across(self):
        place = self.place
        return [
            self.copy(
                z, self.source.at[z, :, 1 - place.core], self.from_core.at[z], place.moved(flip=1)
            )
            for z in range(place.deep)
        ]

    def near(self):
        place = self.place
        copies = []
        for dxy in range(1, 4):
            b, s = place.moved(dxy=dxy)
            square = b % 2 * 2 + s // 2
            copies.append(
                self.copy(
                    place.deep + dxy - 1,
                    self.halves.at[:, square],
                    self.from_near.at[dxy - 1],
                    (b, s),
                )
            )
        return copies

    def far(self):
        place = self.place
        copies = []
        for dz in range(1, place.deep):
            z = (place.z + dz) % place.deep
            copies.append(
                self.copy(
                    place.deep + 2 + dz,
                    self.quarter.at[z],
                    self.from_far.at[dz - 1],
                    place.moved(dz=dz),
                )
            )
        return copies

    def fold_across(self, own):
        for copy in self.across():
            copy.wait_recv()

        def one(i, carry):
            z, q = i // 4, i % 4
            total = own(z, q).astype(F32) + self.from_core[z, q].astype(F32)
            self.halves[z, q] = total.astype(BF16)
            return carry

        lax.fori_loop(0, self.place.deep * 4, one, 0)
        for copy in self.near():
            copy.start()

    def fold_near(self):
        for copy in self.near():
            copy.wait_recv()

        def one(z, carry):
            total = self.halves[z, self.place.square].astype(F32)
            for dxy in range(3):
                total = total + self.from_near[dxy, z].astype(F32)
            self.quarter[z] = total.astype(BF16)
            return carry

        lax.fori_loop(0, self.place.deep, one, 0)
        for copy in self.far():
            copy.start()

    def result(self):
        for copy in self.far():
            copy.wait_recv()
        total = self.quarter[self.place.z].astype(F32)
        for dz in range(self.place.deep - 1):
            total = total + self.from_far[dz].astype(F32)
        return total

    def drain(self):
        for copy in self.across() + self.near() + self.far():
            copy.wait_send()


class SmallSum:
    def __init__(self, place, buffers, received, sems):
        self.place, self.buffers, self.received = place, buffers, received
        self.send_sem, self.recv_sem = sems

    def copies(self, stage):
        place = self.place
        if stage == 0:
            devices, first = [place.moved(flip=1)], 0
        elif stage == 1:
            devices, first = [place.moved(dxy=dxy) for dxy in range(1, 4)], 1
        else:
            devices, first = [place.moved(dz=dz) for dz in range(1, place.deep)], 4
        return [
            pltpu.make_async_remote_copy(
                src_ref=self.buffers.at[stage],
                dst_ref=self.received.at[first + i],
                send_sem=self.send_sem.at[first + i],
                recv_sem=self.recv_sem.at[first + i],
                device_id=device,
                device_id_type=MESH,
            )
            for i, device in enumerate(devices)
        ]

    def send(self, stage, value):
        self.buffers[stage] = value
        for copy in self.copies(stage):
            copy.start()

    def receive(self, stage):
        total = self.buffers[stage]
        first = (0, 1, 4)[stage]
        for i, copy in enumerate(self.copies(stage)):
            copy.wait_recv()
            total = total + self.received[first + i]
        return total

    def drain(self):
        for stage in range(3):
            for copy in self.copies(stage):
                copy.wait_send()


def own_small(total, place):
    width = total.shape[1]
    line = lax.broadcasted_iota(jnp.int32, total.shape, 0)
    short = pltpu.roll(total, width - place.me * 16, 1)
    long = jnp.sum(jnp.where(line == place.me // 8, total, 0.0), axis=0, keepdims=True)
    long = pltpu.roll(jnp.broadcast_to(long, total.shape), width - place.me % 8 * 64, 1)
    return jnp.where(line == 0, long, short)[:, :128]


def attend_back_kernel(frames, mesh_shape, *refs):
    x_ref, dx_ref, qa_ref, ka_ref, vt_ref, ht_ref, qe_ref, da_ref, table, vec_ref, small_in = refs[
        :11
    ]
    if mesh_shape is None:
        dinput_ref, first_source, small_ref = refs[11:14]
        dq, dkt, dvt, sum_k, sum_v, key_ext, small = refs[14:]
    else:
        grads_ref = refs[11]
        dinput_ref, first_own, second_own, small_ref = refs[12:16]
        dq, dkt, dvt, sum_k, sum_v, key_ext, small, first_source = refs[16:24]
        place = Place(mesh_shape)
        first = Gather(place, first_source, *refs[24:29], refs[29:31])
        second = Gather(place, grads_ref, *refs[31:36], refs[36:38])
        shorts = SmallSum(place, refs[38], refs[39], refs[40:42])
        second_half, keep = refs[42:]
        place.meet()
        for copy in second.across():
            copy.start()
        keep_half = pltpu.make_async_copy(grads_ref.at[:, :, place.core], second_half, keep)
        keep_half.start()

    padded = qa_ref.shape[1]
    width = ht_ref.shape[0]
    depth = width // HEADS

    def second_across():
        keep_half.wait()
        second.fold_across(lambda z, q: second_half[z, q])

    def one_head(head, carry):
        if mesh_shape is not None:
            pl.when(head == 1)(second_across)
            pl.when(head == 5)(second.fold_near)
        key_ext[...] = key_extra(head, padded, frames)
        for i in range(padded // ROWS):
            rows = slice(i * ROWS, (i + 1) * ROWS)
            q = qa_ref[head, rows, :]
            d = da_ref[head, rows, :]
            s = dot(
                jnp.concatenate([q, qe_ref[rows, :]], axis=1),
                jnp.concatenate([ka_ref[head], key_ext[...]], axis=1),
                NT,
            )
            p = jnp.exp2(s)
            dp = dot(d[:, :80], vt_ref[head], NN)
            ds = (p * dp).astype(BF16)
            p = p.astype(BF16)
            new_v = dot(d[:, :depth], p, TN)
            new_k = dot(q[:, :depth], ds, TN)
            if i == 0:
                sum_v[...] = new_v
                sum_k[...] = new_k
            else:
                sum_v[...] += new_v
                sum_k[...] += new_k
            both = dot(ds, ka_ref[head], NN)
            both = both + pltpu.roll(both, depth, 1)
            dq[head, rows, :] = (both * LN2).astype(BF16)
        out_rows = pl.ds(pl.multiple_of(head * depth, depth), depth)
        dkt[out_rows, :] = (sum_k[...] * (1.0 / math.sqrt(depth))).astype(BF16)
        dvt[out_rows, :] = sum_v[...].astype(BF16)
        return carry

    lax.fori_loop(0, HEADS, one_head, 0)

    half = lax.broadcasted_iota(jnp.int32, (padded, 128), 1) < depth

    def keep_grad(first_row, cols, value):
        shape = first_source.shape[:-2] + (16, value.shape[1])
        index = (slice(None),) * (len(shape) - 2)
        first_source[index + (slice(first_row, first_row + 16), cols)] = value.astype(BF16).reshape(
            shape
        )

    for h in range(0, HEADS, 2):
        both = jnp.where(half, dq[h], dq[h + 1])
        keep_grad(0, slice(h * depth, (h + 2) * depth), dot(ht_ref[...], both, NN))
    keep_grad(16, slice(0, width), dot(ht_ref[...], dkt[...], NT))
    keep_grad(32, slice(0, width), dot(ht_ref[...], dvt[...], NT))
    if mesh_shape is not None:
        for copy in first.across():
            copy.start()
        second_own[...] = second.result()

    gain = vec_ref[12:13, :]
    small[...] = small_in[...]
    for index, start in enumerate(range(0, frames, ROWS)):
        if mesh_shape is not None and index == 2:
            first.fold_across(lambda z, q: first_source[z, q, place.core])
        count = min(ROWS, frames - start)
        rows = slice(start, start + count)
        wide = slice(start, start + ROWS)
        some = half[:ROWS]
        dq_rows = jnp.concatenate(
            [jnp.where(some, dq[h, wide, :], dq[h + 1, wide, :]) for h in range(0, HEADS, 2)],
            axis=1,
        )
        dk_rows = dkt[:, wide].T
        dv_rows = dvt[:, wide].T
        dh1 = (
            dot(dq_rows, matrix(table, 0), NT)
            + dot(dk_rows, matrix(table, 16), NT)
            + dot(dv_rows, matrix(table, 32), NT)
        )
        small[8:9, :] += column_sums(dq_rows.astype(F32))
        small[9:10, :] += column_sums(dv_rows.astype(F32))
        dh1 = dh1[:count]
        unit, inv_std = normalize(x_ref[rows, :].astype(F32))
        small[12:13, :] += column_sums(dh1 * unit)
        small[13:14, :] += column_sums(dh1)
        dinput_ref[rows, :] = dx_ref[rows, :] + normalize_back(dh1, unit, inv_std, gain)
    if mesh_shape is None:
        small_ref[...] = small[...]
    else:
        shorts.send(0, small[...])
        first.fold_near()
        shorts.send(1, shorts.receive(0))
        shorts.send(2, shorts.receive(1))
        first_own[...] = first.result()
        small_ref[...] = own_small(shorts.receive(2), place)
        second.drain()
        first.drain()
        shorts.drain()


def attend_back(mesh_shape, x, dx, qa, ka, vt, ht, qe, da, table, vectors, small, grads):
    frames, width = x.shape
    padded = ht.shape[1]
    blocks = width // 16
    vmem = pl.BlockSpec(memory_space=pltpu.VMEM)
    args = [x, dx, qa, ka, vt, ht, qe, da, table, vectors, small]
    in_specs = [vmem] * len(args)
    out_shape = [jax.ShapeDtypeStruct((frames, width), F32)]
    scratch = [
        pltpu.VMEM((HEADS, padded, 128), BF16),
        pltpu.VMEM((width, padded), BF16),
        pltpu.VMEM((width, padded), BF16),
        pltpu.VMEM((width // HEADS, padded), F32),
        pltpu.VMEM((width // HEADS, padded), F32),
        pltpu.VMEM((padded, 128), BF16),
        pltpu.VMEM((16, width), F32),
    ]
    options = {}
    if mesh_shape is None:
        out_shape += [
            jax.ShapeDtypeStruct((blocks, 48, width), BF16),
            jax.ShapeDtypeStruct((16, width), F32),
        ]
    else:
        deep = mesh_shape[0] // 2
        rows = grads.shape[1]
        args.append(grads.reshape(deep, 4, 2, rows, width))
        in_specs.append(pl.BlockSpec(memory_space=pl.ANY))
        out_shape += [
            jax.ShapeDtypeStruct((48, width), F32),
            jax.ShapeDtypeStruct((rows, width), F32),
            jax.ShapeDtypeStruct((16, 128), F32),
        ]
        scratch.append(pltpu.VMEM((deep, 4, 2, 48, width), BF16))
        for count in (48, rows):
            scratch += [
                pltpu.VMEM((deep, 4, count, width), BF16),
                pltpu.VMEM((deep, 4, count, width), BF16),
                pltpu.VMEM((3, deep, count, width), BF16),
                pltpu.VMEM((deep, count, width), BF16),
                pltpu.VMEM((deep - 1, count, width), BF16),
                pltpu.SemaphoreType.DMA((2 * deep + 2,)),
                pltpu.SemaphoreType.DMA((2 * deep + 2,)),
            ]
        scratch += [
            pltpu.VMEM((3, 16, width), F32),
            pltpu.VMEM((deep + 3, 16, width), F32),
            pltpu.SemaphoreType.DMA((deep + 3,)),
            pltpu.SemaphoreType.DMA((deep + 3,)),
            pltpu.VMEM((deep, 4, rows, width), BF16),
            pltpu.SemaphoreType.DMA,
        ]
        options = dict(collective_id=1, has_side_effects=True)
    return pl.pallas_call(
        functools.partial(attend_back_kernel, frames, mesh_shape),
        out_shape=out_shape,
        in_specs=in_specs,
        out_specs=[vmem] * len(out_shape),
        scratch_shapes=scratch,
        compiler_params=pltpu.CompilerParams(vmem_limit_bytes=60 << 20, **options),
        name="attend_back",
    )(*args)


def staged(mesh_shape, windows, cotangent, valid, *owned):
    x, cot = windows[0], cotangent[0]
    bq, bv, bo, bu, bd, gain_one, shift_one, gain_two, shift_two = owned[6:]
    short = [bq, bv, bo, bd, gain_one, shift_one, gain_two, shift_two, bu]
    width = x.shape[1]
    vector = jnp.concatenate(short + [jnp.zeros((width // 2 - 192,), BF16)])[None]
    qa, ka, vt, ht, ot, qe, vectors, first, second = attend(mesh_shape, x, vector, *owned[:6])
    out, dx, da, grads, small = mlp(valid, x, cot, ot, second, vectors)
    dinput, first_own, second_own, small_own = attend_back(
        mesh_shape, x, dx, qa, ka, vt, ht, qe, da, first, vectors, small, grads
    )
    hidden = owned[4].shape[1]
    ups = second_own[16 : 16 + hidden // FF_CHUNK * 16]
    up = ups.reshape(-1, 16, FF_CHUNK).transpose(1, 0, 2).reshape(16, hidden)
    down = second_own[16 + hidden // FF_CHUNK * 16 :]
    line = lambda r: small_own[r, :16]
    return (
        out[None],
        dinput[None],
        first_own[0:16],
        first_own[16:32],
        first_own[32:48],
        second_own[0:16],
        up,
        down,
        line(8),
        line(9),
        line(10),
        small_own[0, :64],
        line(11),
        line(12),
        line(13),
        line(14),
        line(15),
    )


def collective(windows, cotangent, valid, *owned):
    axes = ("batch", "shard")
    wq, wk, wv, wo, wu, wd, bq, bv, bo, bu, bd, gain_one, shift_one, gain_two, shift_two = [
        lax.all_gather(part, axes, axis=0, tiled=True) for part in owned
    ]
    x, cot = windows[0], cotangent[0]
    width, hidden = wu.shape
    blocks, chunks = width // 16, hidden // FF_CHUNK
    split = lambda part: part.reshape(blocks, -1, width)
    vectors = jnp.concatenate(
        [jnp.pad(bu.reshape(chunks, FF_CHUNK), ((0, 8 - chunks), (0, 0)))]
        + [v[None] for v in (bq, bv, bo, bd, gain_one, shift_one, gain_two, shift_two)]
    ).astype(F32)
    first = jnp.concatenate([split(wq), split(wk), split(wv)], axis=1)
    ups = wu.reshape(blocks, 16, chunks, FF_CHUNK).transpose(0, 2, 1, 3)
    ups = ups.reshape(blocks, 16 * chunks, FF_CHUNK)
    second = jnp.concatenate([split(wo), ups, split(wd)], axis=1)
    qa, ka, vt, ht, ot, qe = attend(None, x, first, vectors)
    out, dx, da, grads, small = mlp(valid, x, cot, ot, second, vectors)
    dinput, first_grads, small = attend_back(
        None, x, dx, qa, ka, vt, ht, qe, da, first, vectors, small, None
    )
    first_grads, grads = first_grads.astype(F32), grads.astype(F32)
    joined = lambda part: part.reshape(-1, width)
    gwu = grads[:, 16 : 16 + 16 * chunks].reshape(blocks, chunks, 16, FF_CHUNK)
    gwu = gwu.transpose(0, 2, 1, 3).reshape(width, hidden)
    totals = (
        joined(first_grads[:, 0:16]),
        joined(first_grads[:, 16:32]),
        joined(first_grads[:, 32:48]),
        joined(grads[:, 0:16]),
        gwu,
        joined(grads[:, 16 + 16 * chunks :]),
        small[8],
        small[9],
        small[10],
        small[:chunks].reshape(hidden),
        small[11],
        small[12],
        small[13],
        small[14],
        small[15],
    )
    grads = [lax.psum_scatter(total, axes, scatter_dimension=0, tiled=True) for total in totals]
    return (out[None], dinput[None], *grads)


def solution(mesh):
    both = ("batch", "shard")
    windows_spec, matrix_spec, vector_spec = P(both, None, None), P(both, None), P(both)
    params = (matrix_spec,) * 6 + (vector_spec,) * 9
    mesh_shape = (mesh.shape["batch"], mesh.shape["shard"])

    def per_device(windows, cotangent, valid, *owned):
        if mesh_shape[1] == 4 and mesh_shape[0] % 2 == 0 and owned[0].shape[0] == 16:
            return staged(mesh_shape, windows, cotangent, valid, *owned)
        return collective(windows, cotangent, valid, *owned)

    return jax.shard_map(
        per_device,
        mesh=mesh,
        in_specs=(windows_spec, windows_spec, vector_spec) + params,
        out_specs=(windows_spec, windows_spec) + params,
        check_vma=False,
    )
```

time: 1200 us -> 242 us (0.20)
  waiting for transfers between devices: 753 us -> 0 us
  blocking collectives: 249 us -> 0 us
  Pallas kernels: 151 us -> 212 us
  between operations: 14.9 us -> 1.36 us
    reduce_scatter x6 -> x0, waiting for transfers between devices: 749 us -> none  [per_device(): lax.psum_scatter(total, axes, scatter_dimension=0, tiled=True)]
    all_gather x4 -> x0, blocking collectives: 169 us -> none  [per_device(): full = [lax.all_gather(part, axes, axis=0, tiled=True) for part in owned]]
    unnamed x2 -> x0, blocking collectives: 79.9 us -> none
    pallas_call x2, Pallas kernels: 91.8 us -> 154 us  [the longest x1 88.2 us: attend_back(): pl.pallas_call(functools.partial(attend_back_kernel, frames, mesh_shape),...]
    unnamed x41 -> x12, local copies, waits for them, and re-layouts: 30.3 us -> 17.8 us
  transfers between devices with their start and end apart: 8 -> 0, of which waited for: 6 -> 0; matrix products, arithmetic and copies ran while one was open for 3% -> 0% of each run, Pallas kernels for 3% -> 0%
where the time goes in v2:
time: 242 us; the launch traced here: 241 us
  Pallas kernels  212 us (88%)
  local copies, waits for them, and re-layouts  28.1 us (12%)
    pallas_call x1, Pallas kernels, attend_back(): pl.pallas_call(functools.partial(attend_back_kernel, frames, mesh_shape),...  88.2 us
    pallas_call x1, Pallas kernels, attend(): pl.pallas_call(functools.partial(attend_kernel, frames, mesh_shape), out_...  66 us
    pallas_call x1, Pallas kernels, mlp(): pl.pallas_call(functools.partial(mlp_kernel, frames), grid=(padded // ROW...  57.8 us
    unnamed x12, local copies, waits for them, and re-layouts  17.8 us
    concatenate x1, local copies, waits for them, and re-layouts, staged(): jnp.concatenate(short + [jnp.zeros((width // 2 - 192,), BF16)])[None]  6.1 us

profile of v2, /device:TPU:0, one launch (start us, length us, event | category | flops | bytes accessed | tf_op | source)
XLA Modules:
  0.0 241.5 jit_solution(11390598586223267788)
XLA Ops:
  1.3 6.1 %concatenate.3 = bf16[256]{0:T(256)(128)(2,1)S(1)} concatenate(bf16[16]{0:T(256)(128)(2,1)} %param.27, bf16[16]{0:T(256)(128)(2,1)} %param.28, bf16[16]{0:T(256)(128)(2,1)} %param.29, bf16[16]{0:T(256)(128)(2,1)} %param.31, bf16[16]{0:T(256)(128)(2,1)} %param.32, bf16[16]{0:T(256)(128)(2,1)} %param.33, bf16[16]{0:T(256)(128)(2,1)} %param.34, bf16[16]{0:T(256)(128)(2,1)} %param.35, ...), dimensions={0} | concatenate | bytes 1024 | tf_op jit(solution)/shard_map/concatenate | solution.py:881
  7.4 0.6 broadcast_in_dim.13.refs_1_
  8.0 66.0 %attend.1 = (bf16[8,1536,128]{2,1,0:T(8,128)(2,1)}, bf16[8,1536,128]{2,1,0:T(8,128)(2,1)}, bf16[8,80,1536]{2,1,0:T(8,128)(2,1)}, bf16[512,1536]{1,0:T(8,128)(2,1...) custom-call(bf16[1500,512]{1,0:T(8,128)(2,1)} %bitcast.28, ...), custom_call_target="tpu_custom_call" | custom-call | tf_op jit(solution)/shard_map/attend/pallas_call | solution.py:378
  74.0 57.8 %mlp.1 = (f32[1500,512]{1,0:T(8,128)}, f32[1500,512]{1,0:T(8,128)}, bf16[8,1536,128]{2,1,0:T(8,128)(2,1)}, bf16[32,144,512]{2,1,0:T(8,128)(2,1)}, f32[16,512]{1,0:T(8,128)}) custom-call(s32[1]{0:T(128)S(6)} %copy.39.flag_ref, bf16[1500,512]{1,0:T(8,128)(2,1)} %bitcast.29, bf16[1500,512]{1,0:T(8,128)(2,1)} %bitcast.34, ...), custom_call_target="tpu_custom_call" | custom-call | tf_op jit(solution)/shard_map/mlp/pallas_call | solution.py:496
  131.8 0.0 copy-start
  131.8 88.2 %attend_back.1 = (f32[1500,512]{1,0:T(8,128)}, f32[48,512]{1,0:T(8,128)}, f32[144,512]{1,0:T(8,128)}, f32[16,128]{1,0:T(8,128)}) custom-call(bf16[1500,512]{1,0:T(8,128)(2,1)} %bitcast.30, f32[1500,512]{1,0:T(8,128)} %get-tuple-element.39.refs_1_, bf16[8,1536,128]{2,1,0:T(8,128)(2,1)} %get-tuple-element.40.refs_2_, ...), custom_call_target="tpu_custom_call" | custom-call | tf_op jit(solution)/shard_map/attend_back/pallas_call | solution.py:865
  220.0 0.0 copy-start.1
  220.0 0.0 copy-done
  220.0 9.0 %copy.36 = f32[1,1500,512]{2,0,1:T(1,128)} copy(f32[1,1500,512]{2,1,0:T(8,128)S(1)} %bitcast.32) | data formatting | bytes 6144000
  229.0 0.0 copy-start.4
  229.0 0.0 copy-done.1
  229.0 0.0 copy-start.2
  229.0 0.0 copy-start.3
  229.0 8.8 %copy.37 = f32[1,1500,512]{2,0,1:T(1,128)} copy(f32[1,1500,512]{2,1,0:T(8,128)S(1)} %bitcast.33) | data formatting | bytes 6144000
  237.8 0.0 copy-done.4
  237.8 0.5 slice_bitcast_fusion.5
  238.3 0.5 slice_bitcast_fusion
  238.9 0.0 copy-done.2
  238.9 0.6 slice.48
  239.5 0.7 fusion
  240.2 0.7 copy.38
  240.8 0.0 copy-done.3
  240.8 0.6 fusion.1
  (1 shorter events, 0.0 us)
Async XLA Ops:
  131.8 88.2 %copy-start = (f32[1500,512]{1,0:T(8,128)S(1)}, f32[1500,512]{1,0:T(8,128)}, u32[]{:S(2)}) copy-start(f32[1500,512]{1,0:T(8,128)} %get-tuple-element.38) | copy-start | bytes 9216004
  220.0 9.1 %copy-start.1 = (f32[1500,512]{1,0:T(8,128)S(1)}, f32[1500,512]{1,0:T(8,128)}, u32[]{:S(2)}) copy-start(f32[1500,512]{1,0:T(8,128)} %get-tuple-element.49) | copy-start | bytes 9216004
  229.0 8.8 %copy-start.4 = (f32[16,128]{1,0:T(8,128)S(1)}, f32[16,128]{1,0:T(8,128)}, u32[]{:S(2)}) copy-start(f32[16,128]{1,0:T(8,128)} %get-tuple-element.52) | copy-start | bytes 24580
  229.0 9.8 %copy-start.2 = (f32[144,512]{1,0:T(8,128)S(1)}, f32[144,512]{1,0:T(8,128)}, u32[]{:S(2)}) copy-start(f32[144,512]{1,0:T(8,128)} %get-tuple-element.51) | copy-start | bytes 884740
  229.0 11.8 %copy-start.3 = (f32[48,512]{1,0:T(8,128)S(1)}, f32[48,512]{1,0:T(8,128)}, u32[]{:S(2)}) copy-start(f32[48,512]{1,0:T(8,128)} %get-tuple-element.50) | copy-start | bytes 294916

commit v3 on v2

--- a/solution.py
+++ b/solution.py
@@ -16,6 +16,7 @@
 BF16 = jnp.bfloat16
 MESH = pl.DeviceIdType.MESH
 ROWS = 256
+MLP_ROWS = 512
 QUERIES = 768
 FF_CHUNK = 512
 MASKED = -1e30
@@ -56,6 +57,13 @@
     return inv_std * (scaled - first_mean - unit_rows * second_mean)
 
 
+def store_rows(ref, start, rows):
+    count, width = rows.shape
+    parts = width // 128
+    for j in range(parts):
+        ref[pl.ds(start * parts + j, count, stride=parts), :] = rows[:, j * 128 : (j + 1) * 128]
+
+
 def column_sums(rows):
     return jnp.sum(rows, axis=0, keepdims=True)
 
@@ -189,21 +197,15 @@
                 self.across(dz, dxy).wait_send()
 
 
-def spread_small(vector, place):
-    row = vector.astype(F32)
-    width = 2 * row.shape[1]
-    row = jnp.broadcast_to(jnp.concatenate([row, row], axis=1), (8, width))
-    lane = lax.broadcasted_iota(jnp.int32, (8, width), 1)
+def spread_small(vectors, long, place, width):
+    wide = lambda v: jnp.concatenate(
+        [v.astype(F32).reshape(1, -1), jnp.zeros((1, width - v.shape[0]), F32)], axis=1
+    )
+    short = jnp.concatenate([wide(v) for v in vectors], axis=0)
+    short = pltpu.roll(short, place.me * 16, 1)
+    long = pltpu.roll(jnp.broadcast_to(wide(long), (8, width)), place.me % 8 * 64, 1)
     line = lax.broadcasted_iota(jnp.int32, (8, width), 0)
-    short = row
-    for p in range(1, 8):
-        short = jnp.where(line == p, pltpu.roll(row, width - 16 * p, 1), short)
-    start = place.me * 16
-    short = pltpu.roll(short, start, 1)
-    short = jnp.where((lane >= start) & (lane < start + 16), short, 0.0)
-    start = place.me % 8 * 64
-    long = pltpu.roll(pltpu.roll(row, width - 128, 1), start, 1)
-    long = jnp.where((lane >= start) & (lane < start + 64) & (line == place.me // 8), long, 0.0)
+    long = jnp.where(line == place.me // 8, long, 0.0)
     return jnp.concatenate([long, short], axis=0).astype(BF16)
 
 
@@ -218,12 +220,13 @@
         qa_ref, ka_ref, vt_ref, ht_ref, ot_ref, qe_ref = refs[3:9]
         xs, scores, peaks, key_ext, log_rows = refs[9:]
     else:
-        x_ref, vec_ref, wq_own, wk_own, wv_own, wo_own, wu_own, wd_own = refs[:8]
+        x_ref, wq_own, wk_own, wv_own, wo_own, wu_own, wd_own = refs[:7]
+        short_own = refs[7:16]
         qa_ref, ka_ref, vt_ref, ht_ref, ot_ref, qe_ref, small_ref, first_ref, second_ref = refs[
-            8:17
+            16:25
         ]
         xs, scores, peaks, key_ext, log_rows, table, own, send_1, recv_1, send_2, recv_2, keep = (
-            refs[17:]
+            refs[25:]
         )
         place = Place(mesh_shape)
         first = Spread(place, table.at[place.me], table, send_1, recv_1)
@@ -231,7 +234,9 @@
         table[place.me, 0:16, :] = wq_own[...]
         table[place.me, 16:32, :] = wk_own[...]
         table[place.me, 32:48, :] = wv_own[...]
-        table[place.me, 48:64, :] = spread_small(vec_ref[...], place)
+        table[place.me, 48:64, :] = spread_small(
+            [ref[...] for ref in short_own[:8]], short_own[8][...], place, x_ref.shape[1]
+        )
         own[0:16, :] = wo_own[...]
         chunks = wu_own.shape[1] // FF_CHUNK
         for j in range(chunks):
@@ -267,13 +272,11 @@
         v = (dot(h1, matrix(table, 32), NN) + bv).astype(BF16)
         k_high = k.astype(BF16)
         k_low = (k - k_high.astype(F32)).astype(BF16)
-        vt = v.T
+        vt_ref[:, rows] = v.T
         for h in range(HEADS):
             cols = slice(h * depth, (h + 1) * depth)
             qa_ref[h, rows, :] = jnp.concatenate([q[:, cols], q[:, cols]], axis=1)
             ka_ref[h, rows, :] = jnp.concatenate([k_high[:, cols], k_low[:, cols]], axis=1)
-            vt_ref[h, 0:depth, rows] = vt[cols, :]
-            vt_ref[h, depth : depth + 16, rows] = jnp.ones((16, ROWS), BF16)
         return carry
 
     lax.fori_loop(0, padded // ROWS, project, 0)
@@ -298,9 +301,10 @@
         cols = pl.ds(pl.multiple_of((step % blocks) * QUERIES, QUERIES), QUERIES)
         peak = peaks[slot]
         weights = jnp.exp2(scores[slot] - peak).astype(BF16)
-        mixed = dot(vt_ref[head], weights, NN)
+        rows = pl.ds(pl.multiple_of(head * depth, depth), depth)
+        ones = jnp.ones((16, padded), BF16)
+        mixed = dot(jnp.concatenate([vt_ref[rows, :], ones], axis=0), weights, NN)
         total = mixed[depth : depth + 1, :]
-        rows = pl.ds(pl.multiple_of(head * depth, depth), depth)
         ot_ref[rows, cols] = (mixed[:depth, :] * (1.0 / total)).astype(BF16)
         log_rows[head, :, cols] = peak + jnp.log2(total)
 
@@ -345,7 +349,7 @@
     out_shape = [
         jax.ShapeDtypeStruct((HEADS, padded, 128), BF16),
         jax.ShapeDtypeStruct((HEADS, padded, 128), BF16),
-        jax.ShapeDtypeStruct((HEADS, 80, padded), BF16),
+        jax.ShapeDtypeStruct((width, padded), BF16),
         jax.ShapeDtypeStruct((width, padded), BF16),
         jax.ShapeDtypeStruct((width, padded), BF16),
         jax.ShapeDtypeStruct((padded, 128), BF16),
@@ -360,8 +364,8 @@
     out_specs = [vmem] * 6
     options = {}
     if mesh_shape is not None:
-        hidden = rest[5].shape[1]
-        own_rows = 16 + hidden // FF_CHUNK * 16 + rest[6].shape[0]
+        hidden = rest[4].shape[1]
+        own_rows = 16 + hidden // FF_CHUNK * 16 + rest[5].shape[0]
         out_shape += [
             jax.ShapeDtypeStruct((16, width), F32),
             jax.ShapeDtypeStruct((blocks, 64, width), BF16),
@@ -396,7 +400,8 @@
     vec_ref,
     out_ref,
     dx_ref,
-    da_ref,
+    do_ref,
+    de_ref,
     grads_ref,
     small_ref,
     gwo,
@@ -453,7 +458,7 @@
         gwu[j] += dot(h2t, dz, NN)
         small_ref[j : j + 1, :] += column_sums(dz.astype(F32))
         dh2 = dh2 + dot(dz, up_part(j), NT)
-    out_ref[...] = out * flag
+    store_rows(out_ref, 0, out * flag)
     dx1 = dy + normalize_back(dh2, unit, inv_std, gain)
     dx_ref[...] = dx1
     da = dx1.astype(BF16)
@@ -463,15 +468,17 @@
     small_ref[11:12, :] += column_sums(dy)
     small_ref[14:15, :] += column_sums(dh2 * unit)
     small_ref[15:16, :] += column_sums(dh2)
+    do_ref[...] = do
     prod = do.astype(F32) * o.astype(F32)
-    lane = lax.broadcasted_iota(jnp.int32, (rows, 64), 1)
-    for h in range(HEADS):
-        cols = slice(h * depth, (h + 1) * depth)
-        high, middle, low = in_three(-jnp.sum(prod[:, cols], axis=1, keepdims=True))
-        extra = jnp.where(
-            lane == 0, high, jnp.where(lane == 1, middle, jnp.where(lane == 2, low, 0.0))
-        ).astype(BF16)
-        da_ref[h, :, :] = jnp.concatenate([do[:, cols], extra], axis=1)
+    high = prod.astype(BF16)
+    low = (prod - high.astype(F32)).astype(BF16)
+    owner = lax.broadcasted_iota(jnp.int32, (width, 128), 0) // depth
+    pick = lax.broadcasted_iota(jnp.int32, (width, 128), 1) // 16
+    pick = jnp.where(owner == pick, 1.0, 0.0).astype(BF16)
+    high, middle, low = in_three(-(dot(high, pick, NN) + dot(low, pick, NN)))
+    lane = lax.broadcasted_iota(jnp.int32, (rows, 128), 1) % 16
+    extra = jnp.where(lane == 1, middle, jnp.where(lane == 2, low, 0.0))
+    de_ref[...] = jnp.where(lane == 0, high, extra).astype(BF16)
 
     @pl.when(step == pl.num_programs(0) - 1)
     def _():
@@ -489,17 +496,18 @@
     padded = ot.shape[1]
     blocks, rows = table.shape[:2]
     chunks = (rows - 16) * blocks // (2 * FF_CHUNK)
-    by_rows = pl.BlockSpec((ROWS, width), lambda i: (i, 0))
+    by_rows = pl.BlockSpec((MLP_ROWS, width), lambda i: (i, 0))
     fixed = lambda shape: pl.BlockSpec(
         shape, lambda i: (0,) * len(shape), pipeline_mode=pl.Buffered(1)
     )
     return pl.pallas_call(
         functools.partial(mlp_kernel, frames),
-        grid=(padded // ROWS,),
+        grid=(padded // MLP_ROWS,),
         out_shape=[
+            jax.ShapeDtypeStruct((frames * width // 128, 128), F32),
             jax.ShapeDtypeStruct((frames, width), F32),
-            jax.ShapeDtypeStruct((frames, width), F32),
-            jax.ShapeDtypeStruct((HEADS, padded, 128), BF16),
+            jax.ShapeDtypeStruct((padded, width), BF16),
+            jax.ShapeDtypeStruct((padded, 128), BF16),
             jax.ShapeDtypeStruct(table.shape, BF16),
             jax.ShapeDtypeStruct((16, width), F32),
         ],
@@ -507,14 +515,15 @@
             pl.BlockSpec(memory_space=pltpu.SMEM),
             by_rows,
             by_rows,
-            pl.BlockSpec((width, ROWS), lambda i: (0, i)),
+            pl.BlockSpec((width, MLP_ROWS), lambda i: (0, i)),
             fixed(table.shape),
             fixed((16, width)),
         ],
         out_specs=[
+            pl.BlockSpec((MLP_ROWS * width // 128, 128), lambda i: (i, 0)),
             by_rows,
             by_rows,
-            pl.BlockSpec((HEADS, ROWS, 128), lambda i: (0, i, 0)),
+            pl.BlockSpec((MLP_ROWS, 128), lambda i: (i, 0)),
             fixed(table.shape),
             fixed((16, width)),
         ],
@@ -684,21 +693,24 @@
 
 
 def attend_back_kernel(frames, mesh_shape, *refs):
-    x_ref, dx_ref, qa_ref, ka_ref, vt_ref, ht_ref, qe_ref, da_ref, table, vec_ref, small_in = refs[
-        :11
-    ]
+    x_ref, dx_ref, qa_ref, ka_ref, vt_ref, ht_ref, qe_ref, do_ref, de_ref = refs[:9]
+    refs = refs[9:]
+    table, vec_ref, small_in = refs[:3]
     if mesh_shape is None:
-        dinput_ref, first_source, small_ref = refs[11:14]
-        dq, dkt, dvt, sum_k, sum_v, key_ext, small = refs[14:]
+        dinput_ref, first_source, small_ref = refs[3:6]
+        dq, dkt, dvt, sum_k, sum_v, key_ext, value_ext, small = refs[6:]
     else:
-        grads_ref = refs[11]
-        dinput_ref, first_own, second_own, small_ref = refs[12:16]
-        dq, dkt, dvt, sum_k, sum_v, key_ext, small, first_source = refs[16:24]
+        grads_ref = refs[3]
+        dinput_ref, gq_ref, gk_ref, gv_ref, go_ref, gu_ref, gd_ref = refs[4:11]
+        short_refs = refs[11:20]
+        refs = refs[20:]
+        dq, dkt, dvt, sum_k, sum_v, key_ext, value_ext, small, first_source = refs[:9]
+        refs = refs[9:]
         place = Place(mesh_shape)
-        first = Gather(place, first_source, *refs[24:29], refs[29:31])
-        second = Gather(place, grads_ref, *refs[31:36], refs[36:38])
-        shorts = SmallSum(place, refs[38], refs[39], refs[40:42])
-        second_half, keep = refs[42:]
+        first = Gather(place, first_source, *refs[:5], refs[5:7])
+        second = Gather(place, grads_ref, *refs[7:12], refs[12:14])
+        shorts = SmallSum(place, refs[14], refs[15], refs[16:18])
+        second_half, keep = refs[18:]
         place.meet()
         for copy in second.across():
             copy.start()
@@ -718,20 +730,28 @@
             pl.when(head == 1)(second_across)
             pl.when(head == 5)(second.fold_near)
         key_ext[...] = key_extra(head, padded, frames)
+        line = lax.broadcasted_iota(jnp.int32, (128, padded), 0)
+        mine = pl.ds(pl.multiple_of(head // 2 * 128, 128), 128)
+        values = jnp.where(line // depth == head % 2, vt_ref[mine, :].astype(F32), 0.0)
+        value_ext[0:128, :] = values.astype(BF16)
+        extra = jnp.where((line // 16 == head) & (line % 16 < 3), 1.0, 0.0)
+        value_ext[128:256, :] = extra.astype(BF16)
         for i in range(padded // ROWS):
             rows = slice(i * ROWS, (i + 1) * ROWS)
             q = qa_ref[head, rows, :]
-            d = da_ref[head, rows, :]
+            d = do_ref[rows, mine]
+            turned = d.T
+            turned = jnp.where(head % 2 == 0, turned[:depth], turned[depth:])
             s = dot(
                 jnp.concatenate([q, qe_ref[rows, :]], axis=1),
                 jnp.concatenate([ka_ref[head], key_ext[...]], axis=1),
                 NT,
             )
             p = jnp.exp2(s)
-            dp = dot(d[:, :80], vt_ref[head], NN)
+            dp = dot(jnp.concatenate([d, de_ref[rows, :]], axis=1), value_ext[...], NN)
             ds = (p * dp).astype(BF16)
             p = p.astype(BF16)
-            new_v = dot(d[:, :depth], p, TN)
+            new_v = dot(turned, p, NN)
             new_k = dot(q[:, :depth], ds, TN)
             if i == 0:
                 sum_v[...] = new_v
@@ -766,7 +786,12 @@
     if mesh_shape is not None:
         for copy in first.across():
             copy.start()
-        second_own[...] = second.result()
+        second_own = second.result()
+        chunks = gu_ref.shape[1] // FF_CHUNK
+        go_ref[...] = second_own[0:16]
+        for j in range(chunks):
+            gu_ref[:, j * FF_CHUNK : (j + 1) * FF_CHUNK] = second_own[16 + 16 * j : 32 + 16 * j]
+        gd_ref[...] = second_own[16 + 16 * chunks :]
 
     gain = vec_ref[12:13, :]
     small[...] = small_in[...]
@@ -794,7 +819,8 @@
         unit, inv_std = normalize(x_ref[rows, :].astype(F32))
         small[12:13, :] += column_sums(dh1 * unit)
         small[13:14, :] += column_sums(dh1)
-        dinput_ref[rows, :] = dx_ref[rows, :] + normalize_back(dh1, unit, inv_std, gain)
+        dinput = dx_ref[rows, :] + normalize_back(dh1, unit, inv_std, gain)
+        store_rows(dinput_ref, start, dinput)
     if mesh_shape is None:
         small_ref[...] = small[...]
     else:
@@ -802,21 +828,26 @@
         first.fold_near()
         shorts.send(1, shorts.receive(0))
         shorts.send(2, shorts.receive(1))
-        first_own[...] = first.result()
-        small_ref[...] = own_small(shorts.receive(2), place)
+        first_own = first.result()
+        for i, ref in enumerate((gq_ref, gk_ref, gv_ref)):
+            ref[...] = first_own[16 * i : 16 * i + 16]
+        small_own = own_small(shorts.receive(2), place)
+        for i, ref in enumerate(short_refs[:8]):
+            ref[...] = small_own[8 + i, :16]
+        short_refs[8][...] = small_own[0, :64]
         second.drain()
         first.drain()
         shorts.drain()
 
 
-def attend_back(mesh_shape, x, dx, qa, ka, vt, ht, qe, da, table, vectors, small, grads):
+def attend_back(mesh_shape, x, dx, qa, ka, vt, ht, qe, do, de, table, vectors, small, grads):
     frames, width = x.shape
     padded = ht.shape[1]
     blocks = width // 16
     vmem = pl.BlockSpec(memory_space=pltpu.VMEM)
-    args = [x, dx, qa, ka, vt, ht, qe, da, table, vectors, small]
+    args = [x, dx, qa, ka, vt, ht, qe, do, de, table, vectors, small]
     in_specs = [vmem] * len(args)
-    out_shape = [jax.ShapeDtypeStruct((frames, width), F32)]
+    out_shape = [jax.ShapeDtypeStruct((frames * width // 128, 128), F32)]
     scratch = [
         pltpu.VMEM((HEADS, padded, 128), BF16),
         pltpu.VMEM((width, padded), BF16),
@@ -824,6 +855,7 @@
         pltpu.VMEM((width // HEADS, padded), F32),
         pltpu.VMEM((width // HEADS, padded), F32),
         pltpu.VMEM((padded, 128), BF16),
+        pltpu.VMEM((256, padded), BF16),
         pltpu.VMEM((16, width), F32),
     ]
     options = {}
@@ -835,13 +867,19 @@
     else:
         deep = mesh_shape[0] // 2
         rows = grads.shape[1]
+        hidden = (rows - 16) * blocks // 2
         args.append(grads.reshape(deep, 4, 2, rows, width))
         in_specs.append(pl.BlockSpec(memory_space=pl.ANY))
         out_shape += [
-            jax.ShapeDtypeStruct((48, width), F32),
-            jax.ShapeDtypeStruct((rows, width), F32),
-            jax.ShapeDtypeStruct((16, 128), F32),
+            jax.ShapeDtypeStruct((16, width), F32),
+            jax.ShapeDtypeStruct((16, width), F32),
+            jax.ShapeDtypeStruct((16, width), F32),
+            jax.ShapeDtypeStruct((16, width), F32),
+            jax.ShapeDtypeStruct((16, hidden), F32),
+            jax.ShapeDtypeStruct((hidden // blocks, width), F32),
         ]
+        out_shape += [jax.ShapeDtypeStruct((16,), F32)] * 8
+        out_shape += [jax.ShapeDtypeStruct((hidden // blocks,), F32)]
         scratch.append(pltpu.VMEM((deep, 4, 2, 48, width), BF16))
         for count in (48, rows):
             scratch += [
@@ -873,40 +911,67 @@
     )(*args)
 
 
+def hand_over_kernel(count, *refs):
+    large, small = refs[0], refs[1 : count + 1]
+    large_buf, small_buf = refs[2 * count + 2], refs[2 * count + 3 : 3 * count + 3]
+    large_out, small_out = refs[count + 1], refs[count + 2 : 2 * count + 2]
+    sem_in, sem_out = refs[3 * count + 3 :]
+    pieces = large_buf.shape[0]
+    rows = large_buf.shape[1]
+    sources = [large.at[pl.ds(i * rows, rows)] for i in range(pieces)] + list(small)
+    buffers = [large_buf.at[i] for i in range(pieces)] + list(small_buf)
+    targets = [large_out.at[pl.ds(i * rows, rows)] for i in range(pieces)] + list(small_out)
+    inward = [
+        pltpu.make_async_copy(source, buffer, sem_in.at[i])
+        for i, (source, buffer) in enumerate(zip(sources, buffers))
+    ]
+    outward = [
+        pltpu.make_async_copy(buffer, target, sem_out.at[i])
+        for i, (buffer, target) in enumerate(zip(buffers, targets))
+    ]
+    for copy in inward:
+        copy.start()
+    for first, then in zip(inward, outward):
+        first.wait()
+        then.start()
+    for copy in outward:
+        copy.wait()
+
+
+def hand_over(large, *small):
+    anywhere = pl.BlockSpec(memory_space=pltpu.HBM)
+    arrays = (large,) + small
+    rows = large.shape[0]
+    pieces = 6 if rows % 48 == 0 else 1
+    return pl.pallas_call(
+        functools.partial(hand_over_kernel, len(small)),
+        out_shape=[jax.ShapeDtypeStruct(array.shape, array.dtype) for array in arrays],
+        in_specs=[anywhere] * len(arrays),
+        out_specs=[anywhere] * len(arrays),
+        scratch_shapes=[pltpu.VMEM((pieces, rows // pieces) + large.shape[1:], large.dtype)]
+        + [pltpu.VMEM(array.shape, array.dtype) for array in small]
+        + [pltpu.SemaphoreType.DMA((len(small) + pieces,))] * 2,
+        compiler_params=pltpu.CompilerParams(vmem_limit_bytes=60 << 20),
+        name="hand_over",
+    )(*arrays)
+
+
 def staged(mesh_shape, windows, cotangent, valid, *owned):
     x, cot = windows[0], cotangent[0]
     bq, bv, bo, bu, bd, gain_one, shift_one, gain_two, shift_two = owned[6:]
     short = [bq, bv, bo, bd, gain_one, shift_one, gain_two, shift_two, bu]
-    width = x.shape[1]
-    vector = jnp.concatenate(short + [jnp.zeros((width // 2 - 192,), BF16)])[None]
-    qa, ka, vt, ht, ot, qe, vectors, first, second = attend(mesh_shape, x, vector, *owned[:6])
-    out, dx, da, grads, small = mlp(valid, x, cot, ot, second, vectors)
-    dinput, first_own, second_own, small_own = attend_back(
-        mesh_shape, x, dx, qa, ka, vt, ht, qe, da, first, vectors, small, grads
+    qa, ka, vt, ht, ot, qe, vectors, first, second = attend(mesh_shape, x, *owned[:6], *short)
+    out, dx, do, de, grads, small = mlp(valid, x, cot, ot, second, vectors)
+    results = attend_back(
+        mesh_shape, x, dx, qa, ka, vt, ht, qe, do, de, first, vectors, small, grads
     )
-    hidden = owned[4].shape[1]
-    ups = second_own[16 : 16 + hidden // FF_CHUNK * 16]
-    up = ups.reshape(-1, 16, FF_CHUNK).transpose(1, 0, 2).reshape(16, hidden)
-    down = second_own[16 + hidden // FF_CHUNK * 16 :]
-    line = lambda r: small_own[r, :16]
+    dinput, gq, gk, gv, go, gu, gd, *shorts = hand_over(*results)
+    gbq, gbv, gbo, gbd, *gains, gbu = shorts
     return (
-        out[None],
-        dinput[None],
-        first_own[0:16],
-        first_own[16:32],
-        first_own[32:48],
-        second_own[0:16],
-        up,
-        down,
-        line(8),
-        line(9),
-        line(10),
-        small_own[0, :64],
-        line(11),
-        line(12),
-        line(13),
-        line(14),
-        line(15),
+        out.reshape(windows.shape),
+        dinput.reshape(windows.shape),
+        *(gq, gk, gv, go, gu, gd, gbq, gbv, gbo, gbu, gbd),
+        *gains,
     )
 
 
@@ -928,9 +993,9 @@
     ups = ups.reshape(blocks, 16 * chunks, FF_CHUNK)
     second = jnp.concatenate([split(wo), ups, split(wd)], axis=1)
     qa, ka, vt, ht, ot, qe = attend(None, x, first, vectors)
-    out, dx, da, grads, small = mlp(valid, x, cot, ot, second, vectors)
+    out, dx, do, de, grads, small = mlp(valid, x, cot, ot, second, vectors)
     dinput, first_grads, small = attend_back(
-        None, x, dx, qa, ka, vt, ht, qe, da, first, vectors, small, None
+        None, x, dx, qa, ka, vt, ht, qe, do, de, first, vectors, small, None
     )
     first_grads, grads = first_grads.astype(F32), grads.astype(F32)
     joined = lambda part: part.reshape(-1, width)
@@ -954,7 +1019,7 @@
         small[15],
     )
     grads = [lax.psum_scatter(total, axes, scatter_dimension=0, tiled=True) for total in totals]
-    return (out[None], dinput[None], *grads)
+    return (out.reshape(windows.shape), dinput.reshape(windows.shape), *grads)
 
 
 def solution(mesh):

time: 242 us -> 201 us (0.83)
  local copies, waits for them, and re-layouts: 28.1 us -> 0 us
  Pallas kernels: 212 us -> 199 us
    unnamed x12 -> x0, local copies, waits for them, and re-layouts: 17.8 us -> none
    pallas_call x1 -> x2, Pallas kernels: 57.8 us -> 46.3 us  [the longest x1 43.1 us: mlp(): pl.pallas_call(functools.partial(mlp_kernel, frames), grid=(padded // MLP...]
    concatenate x1 -> x0, local copies, waits for them, and re-layouts: 6.1 us -> none  [staged(): jnp.concatenate(short + [jnp.zeros((width // 2 - 192,), BF16)])[None]]
where the time goes in v3:
time: 201 us
  Pallas kernels  199 us (99%)
    pallas_call x1, Pallas kernels, attend_back(): pl.pallas_call(functools.partial(attend_back_kernel, frames, mesh_shape),...  87.6 us
    pallas_call x1, Pallas kernels, attend(): pl.pallas_call(functools.partial(attend_kernel, frames, mesh_shape), out_...  65.3 us
    pallas_call x1, Pallas kernels, mlp(): pl.pallas_call(functools.partial(mlp_kernel, frames), grid=(padded // MLP...  43.1 us

profile of v3, /device:TPU:0, one launch (start us, length us, event | category | flops | bytes accessed | tf_op | source)
XLA Modules:
  0.0 200.8 jit_solution(3349171992708354356)
XLA Ops:
  1.3 65.3 %attend.1 = (bf16[8,1536,128]{2,1,0:T(8,128)(2,1)}, bf16[8,1536,128]{2,1,0:T(8,128)(2,1)}, bf16[512,1536]{1,0:T(8,128)(2,1)}, bf16[512,1536]{1,0:T(8,128)(2,1)},...) custom-call(bf16[1500,512]{1,0:T(8,128)(2,1)} %bitcast.5, ...), custom_call_target="tpu_custom_call" | custom-call | tf_op jit(solution)/shard_map/attend/pallas_call | solution.py:382
  66.6 43.1 %mlp.1 = (f32[6000,128]{1,0:T(8,128)}, f32[1500,512]{1,0:T(8,128)}, bf16[1536,512]{1,0:T(8,128)(2,1)}, bf16[1536,128]{1,0:T(8,128)(2,1)}, bf16[32,144,512]{2,1,0:T(8,128)(2,1)}, /*index=5*/f32[16,512]{1,0:T(8,128)}) custom-call(s32[1]{0:T(128)S(6)} %copy.39.flag_ref, bf16[1500,512]{1,0:T(8,128)(2,1)} %bitcast.6, bf16[1500,512]{1,0:T(8,128)(2,1)} %bitcast.9, ...), custom_call_target="tpu_custom_call" | custom-call | tf_op jit(solution)/shard_map/mlp/pallas_call | solution.py:503
  109.8 87.6 %attend_back.1 = (f32[6000,128]{1,0:T(8,128)}, f32[16,512]{1,0:T(8,128)}, f32[16,512]{1,0:T(8,128)}, f32[16,512]{1,0:T(8,128)}, f32[16,512]{1,0:T(8,128)}, /*ind...) custom-call(bf16[1500,512]{1,0:T(8,128)(2,1)} %bitcast.7, ...), custom_call_target="tpu_custom_call" | custom-call | tf_op jit(solution)/shard_map/attend_back/pallas_call | solution.py:903
  197.4 3.2 %hand_over.1 = (f32[6000,128]{1,0:T(8,128)}, f32[16,512]{1,0:T(8,128)}, f32[16,512]{1,0:T(8,128)}, f32[16,512]{1,0:T(8,128)}, f32[16,512]{1,0:T(8,128)}, /*index...) custom-call(f32[6000,128]{1,0:T(8,128)} %get-tuple-element.79.refs_0, ...), custom_call_target="tpu_custom_call" | custom-call | tf_op jit(solution)/shard_map/hand_over/pallas_call | solution.py:946

commit v4 on v3

--- a/solution.py
+++ b/solution.py
@@ -17,6 +17,9 @@
 MESH = pl.DeviceIdType.MESH
 ROWS = 256
 MLP_ROWS = 512
+FAR_AT = 0
+NEAR_AT = 7
+FOLD_AT = 2
 QUERIES = 768
 FF_CHUNK = 512
 MASKED = -1e30
@@ -120,11 +123,13 @@
         near = [self.moved(dxy=dxy) for dxy in range(1, 4)]
         return far + near + [self.moved(flip=1)]
 
-    def meet(self):
+    def greet(self):
         barrier = pltpu.get_barrier_semaphore()
         for partner in self.partners():
             pl.semaphore_signal(barrier, inc=1, device_id=partner, device_id_type=MESH)
-        pl.semaphore_wait(barrier, self.deep + 3)
+
+    def meet(self):
+        pl.semaphore_wait(pltpu.get_barrier_semaphore(), self.deep + 3)
 
 
 class Spread:
@@ -215,56 +220,81 @@
 
 
 def attend_kernel(frames, mesh_shape, *refs):
+    x_in = refs[0]
     if mesh_shape is None:
-        x_ref, table, small_ref = refs[:3]
-        qa_ref, ka_ref, vt_ref, ht_ref, ot_ref, qe_ref = refs[3:9]
-        xs, scores, peaks, key_ext, log_rows = refs[9:]
+        table, small_ref = refs[1:3]
+        refs = refs[3:]
     else:
-        x_ref, wq_own, wk_own, wv_own, wo_own, wu_own, wd_own = refs[:7]
+        wq_own, wk_own, wv_own, wo_own, wu_own, wd_own = refs[1:7]
         short_own = refs[7:16]
-        qa_ref, ka_ref, vt_ref, ht_ref, ot_ref, qe_ref, small_ref, first_ref, second_ref = refs[
-            16:25
-        ]
-        xs, scores, peaks, key_ext, log_rows, table, own, send_1, recv_1, send_2, recv_2, keep = (
-            refs[25:]
-        )
+        refs = refs[16:]
+    outputs, refs = refs[:6], refs[6:]
+    if mesh_shape is not None:
+        small_ref, first_ref, second_ref = refs[:3]
+        refs = refs[3:]
+    results, refs = refs[:6], refs[6:]
+    qa_ref, ka_ref, vt_ref, ht_ref, ot_ref, qe_ref = results
+    x_ref, units, scores, peaks, key_ext, log_rows, load, store = refs[:8]
+    padded, width = units.shape
+    depth = width // HEADS
+    read = pltpu.make_async_copy(x_in, x_ref, load)
+    read.start()
+
+    def unit_rows():
+        read.wait()
+        for start in range(0, padded, ROWS):
+            count = min(ROWS, frames - start)
+            units[start : start + count, :] = normalize(
+                x_ref[start : start + count, :].astype(F32)
+            )[0]
+        units[frames:, :] = jnp.zeros((padded - frames, width), F32)
+
+    if mesh_shape is None:
+        unit_rows()
+    else:
+        table, own, send_1, recv_1, send_2, recv_2, keep = refs[8:]
         place = Place(mesh_shape)
+        place.greet()
         first = Spread(place, table.at[place.me], table, send_1, recv_1)
         second = Spread(place, own, second_ref, send_2, recv_2)
         table[place.me, 0:16, :] = wq_own[...]
         table[place.me, 16:32, :] = wk_own[...]
         table[place.me, 32:48, :] = wv_own[...]
         table[place.me, 48:64, :] = spread_small(
-            [ref[...] for ref in short_own[:8]], short_own[8][...], place, x_ref.shape[1]
+            [ref[...] for ref in short_own[:8]], short_own[8][...], place, width
         )
+        place.meet()
+        first.begin()
         own[0:16, :] = wo_own[...]
         chunks = wu_own.shape[1] // FF_CHUNK
         for j in range(chunks):
             own[16 + 16 * j : 32 + 16 * j, :] = wu_own[:, j * FF_CHUNK : (j + 1) * FF_CHUNK]
         own[16 + 16 * chunks :, :] = wd_own[...]
-        place.meet()
-        first.begin()
+        unit_rows()
         first.relay_far()
         first.relay_near()
         second.begin()
         keep_own = pltpu.make_async_copy(own, second_ref.at[place.me], keep.at[0])
         keep_own.start()
-
-    padded, width = xs.shape
-    depth = width // HEADS
-    xs[pl.ds(0, frames), :] = x_ref[...]
-    xs[pl.ds(frames, padded - frames), :] = jnp.zeros((padded - frames, width), BF16)
-    if mesh_shape is not None:
         first.arrive()
         keep_first = pltpu.make_async_copy(table, first_ref, keep.at[1])
         keep_first.start()
         small_ref[...] = jnp.sum(table[:, 48:64, :].astype(F32), axis=0)
+
+    writes = [
+        pltpu.make_async_copy(results[i], outputs[i], store.at[i]) for i in (0, 1, 2, 3)
+    ]
+    last_write = pltpu.make_async_copy(qe_ref, outputs[5], store.at[4])
+
+    def head_write(head):
+        rows = pl.ds(pl.multiple_of(head * depth, depth), depth)
+        return pltpu.make_async_copy(ot_ref.at[rows], outputs[4].at[rows], store.at[5 + head])
+
     bq, bv, gain, shift = (small_ref[r : r + 1, :] for r in (8, 9, 12, 13))
 
     def project(i, carry):
         rows = pl.ds(pl.multiple_of(i * ROWS, ROWS), ROWS)
-        unit, _ = normalize(xs[rows, :].astype(F32))
-        h1 = (unit * gain + shift).astype(BF16)
+        h1 = (units[rows, :] * gain + shift).astype(BF16)
         ht_ref[:, rows] = h1.T
         q = (dot(h1, matrix(table, 0), NN) + bq).astype(BF16)
         k = dot(h1, matrix(table, 16), NN).astype(BF16).astype(F32)
@@ -280,6 +310,8 @@
         return carry
 
     lax.fori_loop(0, padded // ROWS, project, 0)
+    for copy in writes:
+        copy.start()
 
     blocks = padded // QUERIES
     steps = HEADS * blocks
@@ -312,12 +344,13 @@
 
     def pair(i, carry):
         if mesh_shape is not None:
-            pl.when(i == 1)(second.relay_far)
-            pl.when(i == 5)(second.relay_near)
+            pl.when(i == FAR_AT)(second.relay_far)
+            pl.when(i == NEAR_AT)(second.relay_near)
         score(i * 2 + 1, 1)
         finish(i * 2, 0)
         score(jnp.minimum(i * 2 + 2, steps - 1), 0)
         finish(i * 2 + 1, 1)
+        head_write(i).start()
         return carry
 
     lax.fori_loop(0, steps // 2, pair, 0)
@@ -332,6 +365,9 @@
         return carry
 
     lax.fori_loop(0, padded // ROWS, extend, 0)
+    last_write.start()
+    for copy in writes + [last_write] + [head_write(head) for head in range(HEADS)]:
+        copy.wait()
     if mesh_shape is not None:
         second.arrive()
         keep_own.wait()
@@ -345,7 +381,7 @@
     padded = -(-frames // QUERIES) * QUERIES
     blocks = width // 16
     vmem = pl.BlockSpec(memory_space=pltpu.VMEM)
-    anywhere = pl.BlockSpec(memory_space=pl.ANY)
+    hbm = pl.BlockSpec(memory_space=pltpu.HBM)
     out_shape = [
         jax.ShapeDtypeStruct((HEADS, padded, 128), BF16),
         jax.ShapeDtypeStruct((HEADS, padded, 128), BF16),
@@ -354,14 +390,18 @@
         jax.ShapeDtypeStruct((width, padded), BF16),
         jax.ShapeDtypeStruct((padded, 128), BF16),
     ]
-    scratch = [
-        pltpu.VMEM((padded, width), BF16),
+    scratch = [pltpu.VMEM(shape.shape, shape.dtype) for shape in out_shape]
+    scratch += [
+        pltpu.VMEM((frames, width), BF16),
+        pltpu.VMEM((padded, width), F32),
         pltpu.VMEM((2, padded, QUERIES), F32),
         pltpu.VMEM((2, 1, QUERIES), F32),
         pltpu.VMEM((2, padded, 128), BF16),
         pltpu.VMEM((HEADS, 1, padded), F32),
+        pltpu.SemaphoreType.DMA,
+        pltpu.SemaphoreType.DMA((5 + HEADS,)),
     ]
-    out_specs = [vmem] * 6
+    out_specs = [hbm] * 6
     options = {}
     if mesh_shape is not None:
         hidden = rest[4].shape[1]
@@ -371,7 +411,7 @@
             jax.ShapeDtypeStruct((blocks, 64, width), BF16),
             jax.ShapeDtypeStruct((blocks, own_rows, width), BF16),
         ]
-        out_specs += [vmem, anywhere, anywhere]
+        out_specs += [vmem, hbm, hbm]
         scratch += [
             pltpu.VMEM((blocks, 64, width), BF16),
             pltpu.VMEM((own_rows, width), BF16),
@@ -382,7 +422,7 @@
     return pl.pallas_call(
         functools.partial(attend_kernel, frames, mesh_shape),
         out_shape=out_shape,
-        in_specs=[vmem] * (1 + len(rest)),
+        in_specs=[hbm] + [vmem] * len(rest),
         out_specs=out_specs,
         scratch_shapes=scratch,
         compiler_params=pltpu.CompilerParams(vmem_limit_bytes=60 << 20, **options),
@@ -693,42 +733,113 @@
 
 
 def attend_back_kernel(frames, mesh_shape, *refs):
-    x_ref, dx_ref, qa_ref, ka_ref, vt_ref, ht_ref, qe_ref, do_ref, de_ref = refs[:9]
-    refs = refs[9:]
-    table, vec_ref, small_in = refs[:3]
+    x_in, dx_in, qa_in, ka_in, vt_in, ht_in, qe_in, do_in, de_in, table_in = refs[:10]
+    vec_ref, small_in = refs[10:12]
+    refs = refs[12:]
     if mesh_shape is None:
-        dinput_ref, first_source, small_ref = refs[3:6]
-        dq, dkt, dvt, sum_k, sum_v, key_ext, value_ext, small = refs[6:]
+        dinput_out, source, small_ref = refs[:3]
+        refs = refs[3:]
     else:
-        grads_ref = refs[3]
-        dinput_ref, gq_ref, gk_ref, gv_ref, go_ref, gu_ref, gd_ref = refs[4:11]
-        short_refs = refs[11:20]
-        refs = refs[20:]
-        dq, dkt, dvt, sum_k, sum_v, key_ext, value_ext, small, first_source = refs[:9]
-        refs = refs[9:]
+        grads_ref = refs[0]
+        dinput_out, gq_ref, gk_ref, gv_ref, go_ref, gu_ref, gd_ref = refs[1:8]
+        short_refs = refs[8:17]
+        refs = refs[17:]
+    x_ref, dx_ref, qa_ref, ka_ref, vt_ref, ht_ref, qe_ref, do_ref, de_ref, table = refs[:10]
+    dinput_ref, load, store = refs[10:13]
+    dq, dkt, dvt, sum_k, sum_v, key_ext, value_ext, small = refs[13:21]
+    refs = refs[21:]
+
+    padded = qa_ref.shape[1]
+    width = ht_ref.shape[0]
+    depth = width // HEADS
+
+    def head_loads(head):
+        return [
+            pltpu.make_async_copy(qa_in.at[head], qa_ref.at[head], load.at[2 * head]),
+            pltpu.make_async_copy(ka_in.at[head], ka_ref.at[head], load.at[2 * head + 1]),
+        ]
+
+    sources = (vt_in, do_in, de_in, qe_in, ht_in, table_in.at[:, 0:48], x_in, dx_in)
+    targets = (vt_ref, do_ref, de_ref, qe_ref, ht_ref, table, x_ref, dx_ref)
+    loads = [
+        pltpu.make_async_copy(source_ref, target_ref, load.at[2 * HEADS + i])
+        for i, (source_ref, target_ref) in enumerate(zip(sources, targets))
+    ]
+    for copy in head_loads(0) + loads[:4]:
+        copy.start()
+    for head in range(1, HEADS):
+        for copy in head_loads(head):
+            copy.start()
+    for copy in loads[4:]:
+        copy.start()
+
+    if mesh_shape is not None:
         place = Place(mesh_shape)
-        first = Gather(place, first_source, *refs[:5], refs[5:7])
-        second = Gather(place, grads_ref, *refs[7:12], refs[12:14])
-        shorts = SmallSum(place, refs[14], refs[15], refs[16:18])
-        second_half, keep = refs[18:]
+        halves = [
+            Gather(place, refs[8 * t], *refs[8 * t + 1 : 8 * t + 6], refs[8 * t + 6 : 8 * t + 8])
+            for t in range(2)
+        ]
+        second = Gather(place, grads_ref, *refs[16:21], refs[21:23])
+        shorts = SmallSum(place, refs[23], refs[24], refs[25:27])
+        second_half, keep = refs[27:]
+        place.greet()
         place.meet()
         for copy in second.across():
             copy.start()
         keep_half = pltpu.make_async_copy(grads_ref.at[:, :, place.core], second_half, keep)
         keep_half.start()
-
-    padded = qa_ref.shape[1]
-    width = ht_ref.shape[0]
-    depth = width // HEADS
+    for copy in loads[:4]:
+        copy.wait()
 
     def second_across():
         keep_half.wait()
         second.fold_across(lambda z, q: second_half[z, q])
 
+    lane_half = lax.broadcasted_iota(jnp.int32, (padded, 128), 1) < depth
+
+    def weight_grads(t):
+        cols = slice(t * (width // 2), (t + 1) * (width // 2))
+        heads = range(t * (HEADS // 2), (t + 1) * (HEADS // 2), 2)
+        queries = jnp.concatenate([jnp.where(lane_half, dq[h], dq[h + 1]) for h in heads], axis=1)
+        ht = ht_ref[...]
+        parts = (
+            dot(ht, queries, NN),
+            dot(ht, dkt[cols, :], NT),
+            dot(ht, dvt[cols, :], NT),
+        )
+        for i, part in enumerate(parts):
+            part = part.astype(BF16)
+            if mesh_shape is None:
+                source[:, 16 * i : 16 * i + 16, cols] = part.reshape(-1, 16, width // 2)
+            else:
+                target = halves[t].source
+                target[:, :, :, 16 * i : 16 * i + 16, :] = part.reshape(
+                    target.shape[:3] + (16, width // 2)
+                )
+        if mesh_shape is not None:
+            for copy in halves[t].across():
+                copy.start()
+
+    def fold_half(t):
+        halves[t].fold_across(lambda z, q: halves[t].source[z, q, place.core])
+
+    def half_result(t):
+        total = halves[t].result()
+        for i, ref in enumerate((gq_ref, gk_ref, gv_ref)):
+            ref[:, t * (width // 2) : (t + 1) * (width // 2)] = total[16 * i : 16 * i + 16]
+
+    def first_weight_grads():
+        loads[4].wait()
+        weight_grads(0)
+
     def one_head(head, carry):
+        pl.when(head == HEADS // 2)(first_weight_grads)
         if mesh_shape is not None:
             pl.when(head == 1)(second_across)
             pl.when(head == 5)(second.fold_near)
+            pl.when(head == 6)(functools.partial(fold_half, 0))
+        for copy in head_loads(head):
+            copy.wait()
         key_ext[...] = key_extra(head, padded, frames)
         line = lax.broadcasted_iota(jnp.int32, (128, padded), 0)
         mine = pl.ds(pl.multiple_of(head // 2 * 128, 128), 128)
@@ -769,23 +880,11 @@
 
     lax.fori_loop(0, HEADS, one_head, 0)
 
-    half = lax.broadcasted_iota(jnp.int32, (padded, 128), 1) < depth
-
-    def keep_grad(first_row, cols, value):
-        shape = first_source.shape[:-2] + (16, value.shape[1])
-        index = (slice(None),) * (len(shape) - 2)
-        first_source[index + (slice(first_row, first_row + 16), cols)] = value.astype(BF16).reshape(
-            shape
-        )
-
-    for h in range(0, HEADS, 2):
-        both = jnp.where(half, dq[h], dq[h + 1])
-        keep_grad(0, slice(h * depth, (h + 2) * depth), dot(ht_ref[...], both, NN))
-    keep_grad(16, slice(0, width), dot(ht_ref[...], dkt[...], NT))
-    keep_grad(32, slice(0, width), dot(ht_ref[...], dvt[...], NT))
+    weight_grads(1)
+    for copy in loads[5:]:
+        copy.wait()
     if mesh_shape is not None:
-        for copy in first.across():
-            copy.start()
+        halves[0].fold_near()
         second_own = second.result()
         chunks = gu_ref.shape[1] // FF_CHUNK
         go_ref[...] = second_own[0:16]
@@ -795,13 +894,14 @@
 
     gain = vec_ref[12:13, :]
     small[...] = small_in[...]
+    stores = []
     for index, start in enumerate(range(0, frames, ROWS)):
-        if mesh_shape is not None and index == 2:
-            first.fold_across(lambda z, q: first_source[z, q, place.core])
+        if mesh_shape is not None and index == FOLD_AT:
+            fold_half(1)
         count = min(ROWS, frames - start)
         rows = slice(start, start + count)
         wide = slice(start, start + ROWS)
-        some = half[:ROWS]
+        some = lane_half[:ROWS]
         dq_rows = jnp.concatenate(
             [jnp.where(some, dq[h, wide, :], dq[h + 1, wide, :]) for h in range(0, HEADS, 2)],
             axis=1,
@@ -821,23 +921,30 @@
         small[13:14, :] += column_sums(dh1)
         dinput = dx_ref[rows, :] + normalize_back(dh1, unit, inv_std, gain)
         store_rows(dinput_ref, start, dinput)
+        part = pl.ds(start * (width // 128), count * (width // 128))
+        stores.append(
+            pltpu.make_async_copy(dinput_ref.at[part], dinput_out.at[part], store.at[index])
+        )
+        stores[-1].start()
     if mesh_shape is None:
         small_ref[...] = small[...]
     else:
         shorts.send(0, small[...])
-        first.fold_near()
+        half_result(0)
         shorts.send(1, shorts.receive(0))
+        halves[1].fold_near()
         shorts.send(2, shorts.receive(1))
-        first_own = first.result()
-        for i, ref in enumerate((gq_ref, gk_ref, gv_ref)):
-            ref[...] = first_own[16 * i : 16 * i + 16]
+        second.drain()
+        halves[0].drain()
+        half_result(1)
         small_own = own_small(shorts.receive(2), place)
         for i, ref in enumerate(short_refs[:8]):
             ref[...] = small_own[8 + i, :16]
         short_refs[8][...] = small_own[0, :64]
-        second.drain()
-        first.drain()
+        halves[1].drain()
         shorts.drain()
+    for copy in stores:
+        copy.wait()
 
 
 def attend_back(mesh_shape, x, dx, qa, ka, vt, ht, qe, do, de, table, vectors, small, grads):
@@ -845,10 +952,17 @@
     padded = ht.shape[1]
     blocks = width // 16
     vmem = pl.BlockSpec(memory_space=pltpu.VMEM)
+    hbm = pl.BlockSpec(memory_space=pltpu.HBM)
     args = [x, dx, qa, ka, vt, ht, qe, do, de, table, vectors, small]
-    in_specs = [vmem] * len(args)
-    out_shape = [jax.ShapeDtypeStruct((frames * width // 128, 128), F32)]
-    scratch = [
+    in_specs = [hbm] * 10 + [vmem] * 2
+    lines = frames * width // 128
+    out_shape = [jax.ShapeDtypeStruct((lines, 128), F32)]
+    scratch = [pltpu.VMEM(array.shape, array.dtype) for array in args[:9]]
+    scratch += [
+        pltpu.VMEM((blocks, 48, width), BF16),
+        pltpu.VMEM((lines, 128), F32),
+        pltpu.SemaphoreType.DMA((2 * HEADS + 8,)),
+        pltpu.SemaphoreType.DMA((padded // ROWS,)),
         pltpu.VMEM((HEADS, padded, 128), BF16),
         pltpu.VMEM((width, padded), BF16),
         pltpu.VMEM((width, padded), BF16),
@@ -869,7 +983,7 @@
         rows = grads.shape[1]
         hidden = (rows - 16) * blocks // 2
         args.append(grads.reshape(deep, 4, 2, rows, width))
-        in_specs.append(pl.BlockSpec(memory_space=pl.ANY))
+        in_specs.append(hbm)
         out_shape += [
             jax.ShapeDtypeStruct((16, width), F32),
             jax.ShapeDtypeStruct((16, width), F32),
@@ -880,17 +994,22 @@
         ]
         out_shape += [jax.ShapeDtypeStruct((16,), F32)] * 8
         out_shape += [jax.ShapeDtypeStruct((hidden // blocks,), F32)]
-        scratch.append(pltpu.VMEM((deep, 4, 2, 48, width), BF16))
-        for count in (48, rows):
-            scratch += [
-                pltpu.VMEM((deep, 4, count, width), BF16),
-                pltpu.VMEM((deep, 4, count, width), BF16),
-                pltpu.VMEM((3, deep, count, width), BF16),
-                pltpu.VMEM((deep, count, width), BF16),
-                pltpu.VMEM((deep - 1, count, width), BF16),
+
+        def stages(shape):
+            return [
+                pltpu.VMEM((deep, 4) + shape, BF16),
+                pltpu.VMEM((deep, 4) + shape, BF16),
+                pltpu.VMEM((3, deep) + shape, BF16),
+                pltpu.VMEM((deep,) + shape, BF16),
+                pltpu.VMEM((deep - 1,) + shape, BF16),
                 pltpu.SemaphoreType.DMA((2 * deep + 2,)),
                 pltpu.SemaphoreType.DMA((2 * deep + 2,)),
             ]
+
+        half_shape = (48, width // 2)
+        for _ in range(2):
+            scratch += [pltpu.VMEM((deep, 4, 2) + half_shape, BF16)] + stages(half_shape)
+        scratch += stages((rows, width))
         scratch += [
             pltpu.VMEM((3, 16, width), F32),
             pltpu.VMEM((deep + 3, 16, width), F32),
@@ -904,7 +1023,7 @@
         functools.partial(attend_back_kernel, frames, mesh_shape),
         out_shape=out_shape,
         in_specs=in_specs,
-        out_specs=[vmem] * len(out_shape),
+        out_specs=[hbm] + [vmem] * (len(out_shape) - 1),
         scratch_shapes=scratch,
         compiler_params=pltpu.CompilerParams(vmem_limit_bytes=60 << 20, **options),
         name="attend_back",

time: 201 us -> 176 us (0.88)
  Pallas kernels: 199 us -> 174 us
    pallas_call x1, Pallas kernels: 87.6 us -> 73.3 us  [attend_back(): pl.pallas_call(functools.partial(attend_back_kernel, frames, mesh_shape),...]
    pallas_call x1, Pallas kernels: 65.3 us -> 54.2 us  [attend(): pl.pallas_call(functools.partial(attend_kernel, frames, mesh_shape), out_...]
where the time goes in v4:
time: 176 us; the launch traced here: 175 us
  Pallas kernels  174 us (99%)
    pallas_call x1, Pallas kernels, attend_back(): pl.pallas_call(functools.partial(attend_back_kernel, frames, mesh_shape),...  73.3 us
    pallas_call x1, Pallas kernels, attend(): pl.pallas_call(functools.partial(attend_kernel, frames, mesh_shape), out_...  54.2 us
    pallas_call x1, Pallas kernels, mlp(): pl.pallas_call(functools.partial(mlp_kernel, frames), grid=(padded // MLP...  43.1 us

profile of v4, /device:TPU:0, one launch (start us, length us, event | category | flops | bytes accessed | tf_op | source)
XLA Modules:
  0.0 175.4 jit_solution(6165768396772855763)
XLA Ops:
  1.3 54.2 %attend.1 = (bf16[8,1536,128]{2,1,0:T(8,128)(2,1)}, bf16[8,1536,128]{2,1,0:T(8,128)(2,1)}, bf16[512,1536]{1,0:T(8,128)(2,1)}, bf16[512,1536]{1,0:T(8,128)(2,1)},...) custom-call(bf16[1500,512]{1,0:T(8,128)(2,1)} %bitcast.5, ...), custom_call_target="tpu_custom_call" | custom-call | tf_op jit(solution)/shard_map/attend/pallas_call | solution.py:422
  55.6 43.1 %mlp.1 = (f32[6000,128]{1,0:T(8,128)}, f32[1500,512]{1,0:T(8,128)}, bf16[1536,512]{1,0:T(8,128)(2,1)}, bf16[1536,128]{1,0:T(8,128)(2,1)}, bf16[32,144,512]{2,1,0:T(8,128)(2,1)}, /*index=5*/f32[16,512]{1,0:T(8,128)}) custom-call(s32[1]{0:T(128)S(6)} %copy.39.flag_ref, bf16[1500,512]{1,0:T(8,128)(2,1)} %bitcast.6, bf16[1500,512]{1,0:T(8,128)(2,1)} %bitcast.9, ...), custom_call_target="tpu_custom_call" | custom-call | tf_op jit(solution)/shard_map/mlp/pallas_call | solution.py:543
  98.7 73.3 %attend_back.1 = (f32[6000,128]{1,0:T(8,128)}, f32[16,512]{1,0:T(8,128)}, f32[16,512]{1,0:T(8,128)}, f32[16,512]{1,0:T(8,128)}, f32[16,512]{1,0:T(8,128)}, /*ind...) custom-call(bf16[1500,512]{1,0:T(8,128)(2,1)} %bitcast.7, ...), custom_call_target="tpu_custom_call" | custom-call | tf_op jit(solution)/shard_map/attend_back/pallas_call | solution.py:1022
  172.0 3.2 %hand_over.1 = (f32[6000,128]{1,0:T(8,128)}, f32[16,512]{1,0:T(8,128)}, f32[16,512]{1,0:T(8,128)}, f32[16,512]{1,0:T(8,128)}, f32[16,512]{1,0:T(8,128)}, /*index...) custom-call(f32[6000,128]{1,0:T(8,128)} %get-tuple-element.79.refs_0, ...), custom_call_target="tpu_custom_call" | custom-call | tf_op jit(solution)/shard_map/hand_over/pallas_call | solution.py:1065

commit v5 on v4

--- a/solution.py
+++ b/solution.py
@@ -17,9 +17,15 @@
 MESH = pl.DeviceIdType.MESH
 ROWS = 256
 MLP_ROWS = 512
-FAR_AT = 0
+EARLY_HEADS = 4
+B_FAR_AT = 0
+B_NEAR_AT = 2
+FAR_AT = 2
 NEAR_AT = 7
 FOLD_AT = 2
+ACROSS_AT = 1
+SQUARE_AT = 5
+PARTS = ((0, 4), (4, 8))
 QUERIES = 768
 FF_CHUNK = 512
 MASKED = -1e30
@@ -28,17 +34,16 @@
 NT = (((1,), (1,)), ((), ()))
 TN = (((0,), (0,)), ((), ()))
 
-TAIL_RATE = 0.2625
+TAIL_RATE = 0.3
 TAIL = (
-    0.10474836168174968,
-    0.10416468281706748,
-    0.10263486984927783,
-    0.056568077030165455,
-    0.14744499390073365,
-    -0.13092736820325213,
-    0.23259357413631826,
-    -0.14775373854130247,
-    0.03052653723595064,
+    0.1196320072075501,
+    0.12071213658889111,
+    0.10017594509547065,
+    0.12769178078587456,
+    -0.0520340331315144,
+    0.2045568015805396,
+    -0.1561584571261984,
+    0.03542373729935703,
 )
 
 
@@ -165,9 +170,11 @@
         copy.start()
         self.started.append(copy)
 
-    def begin(self):
+    def begin_far(self):
         for dz in range(1, self.place.deep):
             self.launch(self.far(dz))
+
+    def begin_near(self):
         for dxy in range(1, 4):
             self.launch(self.near(0, dxy))
         self.launch(self.across(0, 0))
@@ -179,8 +186,8 @@
                 self.launch(self.near(dz, dxy))
             self.launch(self.across(dz, 0))
 
-    def relay_near(self):
-        for dz in range(self.place.deep):
+    def relay_near(self, low, high):
+        for dz in range(low, high):
             for dxy in range(1, 4):
                 self.near(dz, dxy).wait_recv()
                 self.launch(self.across(dz, dxy))
@@ -202,16 +209,32 @@
                 self.across(dz, dxy).wait_send()
 
 
-def spread_small(vectors, long, place, width):
-    wide = lambda v: jnp.concatenate(
-        [v.astype(F32).reshape(1, -1), jnp.zeros((1, width - v.shape[0]), F32)], axis=1
-    )
-    short = jnp.concatenate([wide(v) for v in vectors], axis=0)
-    short = pltpu.roll(short, place.me * 16, 1)
-    long = pltpu.roll(jnp.broadcast_to(wide(long), (8, width)), place.me % 8 * 64, 1)
-    line = lax.broadcasted_iota(jnp.int32, (8, width), 0)
-    long = jnp.where(line == place.me // 8, long, 0.0)
-    return jnp.concatenate([long, short], axis=0).astype(BF16)
+def small_tile(vectors, long):
+    wide = lambda v: jnp.concatenate([v, jnp.zeros((1, 128 - v.shape[1]), F32)], axis=1)
+    long = long.astype(F32).reshape(1, -1)
+    lines = [wide(v.astype(F32).reshape(1, -1)) for v in vectors]
+    lines += [wide(long[:, 16 * c : 16 * c + 16]) for c in range(4)]
+    lines.append(jnp.zeros((128 - len(lines), 128), F32))
+    return jnp.concatenate(lines, axis=0).T[:16].astype(BF16)
+
+
+def small_lines(tiles):
+    width = 16 * tiles.shape[0]
+    columns = tiles.reshape(width, 128).astype(F32).T
+    quarters = width // 128
+    rows = [
+        jnp.concatenate(
+            [columns[8 + c : 9 + c, 128 * j : 128 * j + 128] for c in range(4)], axis=1
+        )
+        for j in range(quarters)
+    ]
+    rows.append(jnp.zeros((8 - quarters, width), F32))
+    source = lax.broadcasted_iota(jnp.int32, (width, width), 0)
+    target = lax.broadcasted_iota(jnp.int32, (width, width), 1)
+    goal = source // 16 % 8 * 64 + source // 128 * 16 + source % 16
+    moved = jnp.where(goal == target, 1.0, 0.0).astype(BF16)
+    long = dot(jnp.concatenate(rows, axis=0).astype(BF16), moved, NN)
+    return jnp.concatenate([long, columns[:8]], axis=0)
 
 
 def matrix(table, first, count=16):
@@ -234,7 +257,7 @@
         refs = refs[3:]
     results, refs = refs[:6], refs[6:]
     qa_ref, ka_ref, vt_ref, ht_ref, ot_ref, qe_ref = results
-    x_ref, units, scores, peaks, key_ext, log_rows, load, store = refs[:8]
+    x_ref, units, rows_low, scores, peaks, key_ext, log_rows, load, store = refs[:9]
     padded, width = units.shape
     depth = width // HEADS
     read = pltpu.make_async_copy(x_in, x_ref, load)
@@ -252,34 +275,47 @@
     if mesh_shape is None:
         unit_rows()
     else:
-        table, own, send_1, recv_1, send_2, recv_2, keep = refs[8:]
+        table_a, table_b, own, *sems, keep = refs[9:]
         place = Place(mesh_shape)
         place.greet()
-        first = Spread(place, table.at[place.me], table, send_1, recv_1)
-        second = Spread(place, own, second_ref, send_2, recv_2)
-        table[place.me, 0:16, :] = wq_own[...]
-        table[place.me, 16:32, :] = wk_own[...]
-        table[place.me, 32:48, :] = wv_own[...]
-        table[place.me, 48:64, :] = spread_small(
-            [ref[...] for ref in short_own[:8]], short_own[8][...], place, width
+        part_a = Spread(place, table_a.at[place.me], table_a, *sems[0:2])
+        part_b = Spread(place, table_b.at[place.me], table_b, *sems[2:4])
+        second = Spread(place, own, second_ref, *sems[4:6])
+        early = EARLY_HEADS * depth
+        if early > 128:
+            table_a[place.me, 48:64, 128:] = jnp.zeros((16, early - 128), BF16)
+        for i, weight_own in enumerate((wq_own, wk_own, wv_own)):
+            table_a[place.me, 16 * i : 16 * i + 16, :] = weight_own[:, :early]
+            table_b[place.me, 16 * i : 16 * i + 16, :] = weight_own[:, early:]
+        table_a[place.me, 48:64, 0:128] = small_tile(
+            [ref[...] for ref in short_own[:8]], short_own[8][...]
         )
         place.meet()
-        first.begin()
+        part_a.begin_far()
+        part_a.begin_near()
         own[0:16, :] = wo_own[...]
         chunks = wu_own.shape[1] // FF_CHUNK
         for j in range(chunks):
             own[16 + 16 * j : 32 + 16 * j, :] = wu_own[:, j * FF_CHUNK : (j + 1) * FF_CHUNK]
         own[16 + 16 * chunks :, :] = wd_own[...]
         unit_rows()
-        first.relay_far()
-        first.relay_near()
-        second.begin()
+        part_a.relay_far()
+        part_b.begin_far()
+        part_a.relay_near(0, place.deep)
+        part_b.begin_near()
+        second.begin_far()
+        second.begin_near()
         keep_own = pltpu.make_async_copy(own, second_ref.at[place.me], keep.at[0])
         keep_own.start()
-        first.arrive()
-        keep_first = pltpu.make_async_copy(table, first_ref, keep.at[1])
-        keep_first.start()
-        small_ref[...] = jnp.sum(table[:, 48:64, :].astype(F32), axis=0)
+        part_a.arrive()
+        keep_a = pltpu.make_async_copy(
+            table_a.at[:, 0:48], first_ref.at[:, :, pl.ds(0, early)], keep.at[1]
+        )
+        keep_a.start()
+        keep_b = pltpu.make_async_copy(
+            table_b, first_ref.at[:, :, pl.ds(early, width - early)], keep.at[2]
+        )
+        small_ref[...] = small_lines(table_a[:, 48:64, 0:128])
 
     writes = [
         pltpu.make_async_copy(results[i], outputs[i], store.at[i]) for i in (0, 1, 2, 3)
@@ -292,26 +328,44 @@
 
     bq, bv, gain, shift = (small_ref[r : r + 1, :] for r in (8, 9, 12, 13))
 
-    def project(i, carry):
+    def project(heads, i, carry):
+        low, high = heads
+        lanes = slice(low * depth, high * depth)
+
+        def weight(which):
+            if mesh_shape is None:
+                return matrix(table[:, :, lanes], 16 * which)
+            return matrix(table_a if low == 0 else table_b, 16 * which)
+
         rows = pl.ds(pl.multiple_of(i * ROWS, ROWS), ROWS)
-        h1 = (units[rows, :] * gain + shift).astype(BF16)
-        ht_ref[:, rows] = h1.T
-        q = (dot(h1, matrix(table, 0), NN) + bq).astype(BF16)
-        k = dot(h1, matrix(table, 16), NN).astype(BF16).astype(F32)
+        if low == 0:
+            h1 = (units[rows, :] * gain + shift).astype(BF16)
+            rows_low[rows, :] = h1
+            ht_ref[:, rows] = h1.T
+        else:
+            h1 = rows_low[rows, :]
+        q = (dot(h1, weight(0), NN) + bq[:, lanes]).astype(BF16)
+        k = dot(h1, weight(1), NN).astype(BF16).astype(F32)
         k = k * (LOG2E / math.sqrt(depth))
-        v = (dot(h1, matrix(table, 32), NN) + bv).astype(BF16)
+        v = (dot(h1, weight(2), NN) + bv[:, lanes]).astype(BF16)
         k_high = k.astype(BF16)
         k_low = (k - k_high.astype(F32)).astype(BF16)
-        vt_ref[:, rows] = v.T
-        for h in range(HEADS):
-            cols = slice(h * depth, (h + 1) * depth)
+        vt_ref[lanes, rows] = v.T
+        for h in range(low, high):
+            cols = slice((h - low) * depth, (h - low + 1) * depth)
             qa_ref[h, rows, :] = jnp.concatenate([q[:, cols], q[:, cols]], axis=1)
             ka_ref[h, rows, :] = jnp.concatenate([k_high[:, cols], k_low[:, cols]], axis=1)
         return carry
 
-    lax.fori_loop(0, padded // ROWS, project, 0)
-    for copy in writes:
-        copy.start()
+    lax.fori_loop(0, padded // ROWS, functools.partial(project, (0, EARLY_HEADS)), 0)
+
+    def project_rest():
+        if mesh_shape is not None:
+            part_b.arrive()
+            keep_b.start()
+        lax.fori_loop(0, padded // ROWS, functools.partial(project, (EARLY_HEADS, HEADS)), 0)
+        for copy in writes:
+            copy.start()
 
     blocks = padded // QUERIES
     steps = HEADS * blocks
@@ -344,8 +398,11 @@
 
     def pair(i, carry):
         if mesh_shape is not None:
+            pl.when(i == B_FAR_AT)(part_b.relay_far)
+            pl.when(i == B_NEAR_AT)(functools.partial(part_b.relay_near, 0, place.deep))
             pl.when(i == FAR_AT)(second.relay_far)
-            pl.when(i == NEAR_AT)(second.relay_near)
+            pl.when(i == NEAR_AT)(functools.partial(second.relay_near, 0, 2))
+        pl.when(i == EARLY_HEADS - 1)(project_rest)
         score(i * 2 + 1, 1)
         finish(i * 2, 0)
         score(jnp.minimum(i * 2 + 2, steps - 1), 0)
@@ -364,6 +421,8 @@
         qe_ref[rows, :] = jnp.concatenate(pieces, axis=0).T.astype(BF16)
         return carry
 
+    if mesh_shape is not None:
+        second.relay_near(2, place.deep)
     lax.fori_loop(0, padded // ROWS, extend, 0)
     last_write.start()
     for copy in writes + [last_write] + [head_write(head) for head in range(HEADS)]:
@@ -371,8 +430,10 @@
     if mesh_shape is not None:
         second.arrive()
         keep_own.wait()
-        keep_first.wait()
-        first.drain()
+        keep_a.wait()
+        keep_b.wait()
+        part_a.drain()
+        part_b.drain()
         second.drain()
 
 
@@ -394,6 +455,7 @@
     scratch += [
         pltpu.VMEM((frames, width), BF16),
         pltpu.VMEM((padded, width), F32),
+        pltpu.VMEM((padded, width), BF16),
         pltpu.VMEM((2, padded, QUERIES), F32),
         pltpu.VMEM((2, 1, QUERIES), F32),
         pltpu.VMEM((2, padded, 128), BF16),
@@ -404,20 +466,22 @@
     out_specs = [hbm] * 6
     options = {}
     if mesh_shape is not None:
+        early = EARLY_HEADS * (width // HEADS)
         hidden = rest[4].shape[1]
         own_rows = 16 + hidden // FF_CHUNK * 16 + rest[5].shape[0]
         out_shape += [
             jax.ShapeDtypeStruct((16, width), F32),
-            jax.ShapeDtypeStruct((blocks, 64, width), BF16),
+            jax.ShapeDtypeStruct((blocks, 48, width), BF16),
             jax.ShapeDtypeStruct((blocks, own_rows, width), BF16),
         ]
         out_specs += [vmem, hbm, hbm]
         scratch += [
-            pltpu.VMEM((blocks, 64, width), BF16),
+            pltpu.VMEM((blocks, 64, early), BF16),
+            pltpu.VMEM((blocks, 48, width - early), BF16),
             pltpu.VMEM((own_rows, width), BF16),
         ]
-        scratch += [pltpu.SemaphoreType.DMA((blocks - 1,)) for _ in range(4)]
-        scratch += [pltpu.SemaphoreType.DMA((2,))]
+        scratch += [pltpu.SemaphoreType.DMA((blocks - 1,)) for _ in range(6)]
+        scratch += [pltpu.SemaphoreType.DMA((3,))]
         options = dict(collective_id=0, has_side_effects=True)
     return pl.pallas_call(
         functools.partial(attend_kernel, frames, mesh_shape),
@@ -436,17 +500,21 @@
     x_ref,
     cot_ref,
     ot_ref,
-    table,
+    table_in,
     vec_ref,
     out_ref,
     dx_ref,
     do_ref,
     de_ref,
-    grads_ref,
+    grads_out,
     small_ref,
     gwo,
     gwu,
     gwd,
+    table,
+    grads_ref,
+    load,
+    store,
 ):
     step = pl.program_id(0)
     rows, width = x_ref.shape
@@ -462,12 +530,21 @@
         part = table[j * per_chunk : (j + 1) * per_chunk, 16 + 16 * chunks :, :]
         return part.reshape(FF_CHUNK, width)
 
+    bounds = (0, 16, 16 + 16 * chunks, table.shape[1])
+    loads = [
+        pltpu.make_async_copy(table_in.at[:, low:high], table.at[:, low:high], load.at[i])
+        for i, (low, high) in enumerate(zip(bounds, bounds[1:]))
+    ]
+
     @pl.when(step == 0)
     def _():
-        gwo[...] = jnp.zeros_like(gwo)
-        gwu[...] = jnp.zeros_like(gwu)
-        gwd[...] = jnp.zeros_like(gwd)
+        for copy in loads:
+            copy.start()
         small_ref[...] = jnp.zeros_like(small_ref)
+        loads[0].wait()
+
+    def kept(ref, *index):
+        return jnp.where(step == 0, 0.0, ref[index] if index else ref[...])
 
     flag = flag_ref[0].astype(F32)
     inside = step * rows + lax.broadcasted_iota(jnp.int32, (rows, width), 0) < frames
@@ -482,6 +559,12 @@
     unit, inv_std = normalize(x1)
     h2 = (unit * gain + shift).astype(BF16)
     h2t = h2.T
+
+    @pl.when(step == 0)
+    def _():
+        loads[1].wait()
+        loads[2].wait()
+
     z_next = dot(h2, up_part(0), NN)
     out = x1 + bd
     dh2 = jnp.zeros((rows, width), F32)
@@ -494,15 +577,15 @@
         g = g.astype(BF16)
         dz = (dg * slope).astype(BF16)
         out = out + dot(g, down_part(j), NN)
-        gwd[j] += dot(g, dy_low, TN)
-        gwu[j] += dot(h2t, dz, NN)
+        gwd[j] = kept(gwd, j) + dot(g, dy_low, TN)
+        gwu[j] = kept(gwu, j) + dot(h2t, dz, NN)
         small_ref[j : j + 1, :] += column_sums(dz.astype(F32))
         dh2 = dh2 + dot(dz, up_part(j), NT)
     store_rows(out_ref, 0, out * flag)
     dx1 = dy + normalize_back(dh2, unit, inv_std, gain)
     dx_ref[...] = dx1
     da = dx1.astype(BF16)
-    gwo[...] += dot(ot, da, NN)
+    gwo[...] = kept(gwo) + dot(ot, da, NN)
     do = dot(da, wo, NT).astype(BF16)
     small_ref[10:11, :] += column_sums(da.astype(F32))
     small_ref[11:12, :] += column_sums(dy)
@@ -523,12 +606,28 @@
     @pl.when(step == pl.num_programs(0) - 1)
     def _():
         split = lambda part, count: part.astype(BF16).reshape(-1, count, width)
+        copies = []
+
+        def send(*index):
+            copies.append(
+                pltpu.make_async_copy(
+                    grads_ref.at[index], grads_out.at[index], store.at[len(copies)]
+                )
+            )
+            copies[-1].start()
+
+        for j in range(chunks):
+            rows_up = slice(16 + 16 * j, 32 + 16 * j)
+            grads_ref[:, rows_up, :] = split(gwu[j], 16)
+            send(slice(None), rows_up)
+            blocks_down = slice(j * per_chunk, (j + 1) * per_chunk)
+            rows_down = slice(16 + 16 * chunks, table.shape[1])
+            grads_ref[blocks_down, rows_down, :] = split(gwd[j], down)
+            send(blocks_down, rows_down)
         grads_ref[:, 0:16, :] = split(gwo[...], 16)
-        for j in range(chunks):
-            grads_ref[:, 16 + 16 * j : 32 + 16 * j, :] = split(gwu[j], 16)
-            grads_ref[j * per_chunk : (j + 1) * per_chunk, 16 + 16 * chunks :, :] = split(
-                gwd[j], down
-            )
+        send(slice(None), slice(0, 16))
+        for copy in copies:
+            copy.wait()
 
 
 def mlp(flag, x, cot, ot, table, vectors):
@@ -556,7 +655,7 @@
             by_rows,
             by_rows,
             pl.BlockSpec((width, MLP_ROWS), lambda i: (0, i)),
-            fixed(table.shape),
+            pl.BlockSpec(memory_space=pltpu.HBM),
             fixed((16, width)),
         ],
         out_specs=[
@@ -564,13 +663,17 @@
             by_rows,
             by_rows,
             pl.BlockSpec((MLP_ROWS, 128), lambda i: (i, 0)),
-            fixed(table.shape),
+            pl.BlockSpec(memory_space=pltpu.HBM),
             fixed((16, width)),
         ],
         scratch_shapes=[
             pltpu.VMEM((width, width), F32),
             pltpu.VMEM((chunks, width, FF_CHUNK), F32),
             pltpu.VMEM((chunks, FF_CHUNK, width), F32),
+            pltpu.VMEM(table.shape, BF16),
+            pltpu.VMEM(table.shape, BF16),
+            pltpu.SemaphoreType.DMA((3,)),
+            pltpu.SemaphoreType.DMA((2 * chunks + 1,)),
         ],
         compiler_params=pltpu.CompilerParams(
             vmem_limit_bytes=60 << 20, dimension_semantics=("arbitrary",)
@@ -775,18 +878,18 @@
 
     if mesh_shape is not None:
         place = Place(mesh_shape)
-        halves = [
-            Gather(place, refs[8 * t], *refs[8 * t + 1 : 8 * t + 6], refs[8 * t + 6 : 8 * t + 8])
-            for t in range(2)
-        ]
-        second = Gather(place, grads_ref, *refs[16:21], refs[21:23])
-        shorts = SmallSum(place, refs[23], refs[24], refs[25:27])
-        second_half, keep = refs[27:]
         place.greet()
+        parts = []
+        for _ in PARTS:
+            parts.append(Gather(place, refs[0], *refs[1:6], refs[6:8]))
+            refs = refs[8:]
+        second = Gather(place, grads_ref, *refs[:5], refs[5:7])
+        shorts = SmallSum(place, refs[7], refs[8], refs[9:11])
+        second_half, keep = refs[11:]
+        keep_half = pltpu.make_async_copy(grads_ref.at[:, :, place.core], second_half, keep)
         place.meet()
         for copy in second.across():
             copy.start()
-        keep_half = pltpu.make_async_copy(grads_ref.at[:, :, place.core], second_half, keep)
         keep_half.start()
     for copy in loads[:4]:
         copy.wait()
@@ -798,46 +901,54 @@
     lane_half = lax.broadcasted_iota(jnp.int32, (padded, 128), 1) < depth
 
     def weight_grads(t):
-        cols = slice(t * (width // 2), (t + 1) * (width // 2))
-        heads = range(t * (HEADS // 2), (t + 1) * (HEADS // 2), 2)
-        queries = jnp.concatenate([jnp.where(lane_half, dq[h], dq[h + 1]) for h in heads], axis=1)
+        low, high = PARTS[t]
+        cols = slice(low * depth, high * depth)
+        wide = (high - low) * depth
+        queries = jnp.concatenate(
+            [jnp.where(lane_half, dq[h], dq[h + 1]) for h in range(low, high, 2)], axis=1
+        )
         ht = ht_ref[...]
-        parts = (
+        grads = (
             dot(ht, queries, NN),
             dot(ht, dkt[cols, :], NT),
             dot(ht, dvt[cols, :], NT),
         )
-        for i, part in enumerate(parts):
-            part = part.astype(BF16)
+        for i, grad in enumerate(grads):
+            grad = grad.astype(BF16)
             if mesh_shape is None:
-                source[:, 16 * i : 16 * i + 16, cols] = part.reshape(-1, 16, width // 2)
+                source[:, 16 * i : 16 * i + 16, cols] = grad.reshape(-1, 16, wide)
             else:
-                target = halves[t].source
-                target[:, :, :, 16 * i : 16 * i + 16, :] = part.reshape(
-                    target.shape[:3] + (16, width // 2)
+                target = parts[t].source
+                target[:, :, :, 16 * i : 16 * i + 16, :] = grad.reshape(
+                    target.shape[:3] + (16, wide)
                 )
         if mesh_shape is not None:
-            for copy in halves[t].across():
+            for copy in parts[t].across():
                 copy.start()
 
-    def fold_half(t):
-        halves[t].fold_across(lambda z, q: halves[t].source[z, q, place.core])
-
-    def half_result(t):
-        total = halves[t].result()
+    def fold_part(t):
+        parts[t].fold_across(lambda z, q: parts[t].source[z, q, place.core])
+
+    def part_result(t):
+        total = parts[t].result()
         for i, ref in enumerate((gq_ref, gk_ref, gv_ref)):
-            ref[:, t * (width // 2) : (t + 1) * (width // 2)] = total[16 * i : 16 * i + 16]
-
-    def first_weight_grads():
-        loads[4].wait()
-        weight_grads(0)
+            ref[:, PARTS[t][0] * depth : PARTS[t][1] * depth] = total[16 * i : 16 * i + 16]
+
+    def early_weight_grads(t):
+        if t == 0:
+            loads[4].wait()
+        weight_grads(t)
+
+    last = len(PARTS) - 1
 
     def one_head(head, carry):
-        pl.when(head == HEADS // 2)(first_weight_grads)
+        for t in range(last):
+            pl.when(head == PARTS[t][1])(functools.partial(early_weight_grads, t))
+            if mesh_shape is not None and PARTS[t][1] + 1 < HEADS:
+                pl.when(head == PARTS[t][1] + 1)(functools.partial(fold_part, t))
         if mesh_shape is not None:
-            pl.when(head == 1)(second_across)
-            pl.when(head == 5)(second.fold_near)
-            pl.when(head == 6)(functools.partial(fold_half, 0))
+            pl.when(head == ACROSS_AT)(second_across)
+            pl.when(head == SQUARE_AT)(second.fold_near)
         for copy in head_loads(head):
             copy.wait()
         key_ext[...] = key_extra(head, padded, frames)
@@ -880,11 +991,15 @@
 
     lax.fori_loop(0, HEADS, one_head, 0)
 
-    weight_grads(1)
+    weight_grads(last)
     for copy in loads[5:]:
         copy.wait()
     if mesh_shape is not None:
-        halves[0].fold_near()
+        for t in range(last):
+            if PARTS[t][1] + 1 >= HEADS:
+                fold_part(t)
+            else:
+                parts[t].fold_near()
         second_own = second.result()
         chunks = gu_ref.shape[1] // FF_CHUNK
         go_ref[...] = second_own[0:16]
@@ -897,7 +1012,10 @@
     stores = []
     for index, start in enumerate(range(0, frames, ROWS)):
         if mesh_shape is not None and index == FOLD_AT:
-            fold_half(1)
+            fold_part(last)
+            for t in range(last):
+                if PARTS[t][1] + 1 >= HEADS:
+                    parts[t].fold_near()
         count = min(ROWS, frames - start)
         rows = slice(start, start + count)
         wide = slice(start, start + ROWS)
@@ -930,18 +1048,20 @@
         small_ref[...] = small[...]
     else:
         shorts.send(0, small[...])
-        half_result(0)
+        for t in range(last):
+            part_result(t)
         shorts.send(1, shorts.receive(0))
-        halves[1].fold_near()
+        parts[last].fold_near()
         shorts.send(2, shorts.receive(1))
         second.drain()
-        halves[0].drain()
-        half_result(1)
+        for t in range(last):
+            parts[t].drain()
+        part_result(last)
         small_own = own_small(shorts.receive(2), place)
         for i, ref in enumerate(short_refs[:8]):
             ref[...] = small_own[8 + i, :16]
         short_refs[8][...] = small_own[0, :64]
-        halves[1].drain()
+        parts[last].drain()
         shorts.drain()
     for copy in stores:
         copy.wait()
@@ -1006,9 +1126,9 @@
                 pltpu.SemaphoreType.DMA((2 * deep + 2,)),
             ]
 
-        half_shape = (48, width // 2)
-        for _ in range(2):
-            scratch += [pltpu.VMEM((deep, 4, 2) + half_shape, BF16)] + stages(half_shape)
+        for low, high in PARTS:
+            shape = (48, (high - low) * (width // HEADS))
+            scratch += [pltpu.VMEM((deep, 4, 2) + shape, BF16)] + stages(shape)
         scratch += stages((rows, width))
         scratch += [
             pltpu.VMEM((3, 16, width), F32),

time: 176 us -> 174 us (0.989)
  Pallas kernels: 174 us -> 172 us
    pallas_call x1, Pallas kernels: 54.2 us -> 52.3 us  [attend(): pl.pallas_call(functools.partial(attend_kernel, frames, mesh_shape), out_...]
where the time goes in v5:
time: 174 us
  Pallas kernels  172 us (99%)
    pallas_call x1, Pallas kernels, attend_back(): pl.pallas_call(functools.partial(attend_back_kernel, frames, mesh_shape),...  73.9 us
    pallas_call x1, Pallas kernels, attend(): pl.pallas_call(functools.partial(attend_kernel, frames, mesh_shape), out_...  52.3 us
    pallas_call x1, Pallas kernels, mlp(): pl.pallas_call(functools.partial(mlp_kernel, frames), grid=(padded // MLP...  42.7 us

profile of v5, /device:TPU:0, one launch (start us, length us, event | category | flops | bytes accessed | tf_op | source)
XLA Modules:
  0.0 173.6 jit_solution(14437103866806560651)
XLA Ops:
  1.3 52.3 %attend.1 = (bf16[8,1536,128]{2,1,0:T(8,128)(2,1)}, bf16[8,1536,128]{2,1,0:T(8,128)(2,1)}, bf16[512,1536]{1,0:T(8,128)(2,1)}, bf16[512,1536]{1,0:T(8,128)(2,1)},...) custom-call(bf16[1500,512]{1,0:T(8,128)(2,1)} %bitcast.5, ...), custom_call_target="tpu_custom_call" | custom-call | tf_op jit(solution)/shard_map/attend/pallas_call | solution.py:486
  53.6 42.7 %mlp.1 = (f32[6000,128]{1,0:T(8,128)}, f32[1500,512]{1,0:T(8,128)}, bf16[1536,512]{1,0:T(8,128)(2,1)}, bf16[1536,128]{1,0:T(8,128)(2,1)}, bf16[32,144,512]{2,1,0:T(8,128)(2,1)}, /*index=5*/f32[16,512]{1,0:T(8,128)}) custom-call(s32[1]{0:T(128)S(6)} %copy.39.flag_ref, bf16[1500,512]{1,0:T(8,128)(2,1)} %bitcast.6, bf16[1500,512]{1,0:T(8,128)(2,1)} %bitcast.9, ...), custom_call_target="tpu_custom_call" | custom-call | tf_op jit(solution)/shard_map/mlp/pallas_call | solution.py:642
  96.3 73.9 %attend_back.1 = (f32[6000,128]{1,0:T(8,128)}, f32[16,512]{1,0:T(8,128)}, f32[16,512]{1,0:T(8,128)}, f32[16,512]{1,0:T(8,128)}, f32[16,512]{1,0:T(8,128)}, /*ind...) custom-call(bf16[1500,512]{1,0:T(8,128)(2,1)} %bitcast.7, ...), custom_call_target="tpu_custom_call" | custom-call | tf_op jit(solution)/shard_map/attend_back/pallas_call | solution.py:1142
  170.2 3.2 %hand_over.1 = (f32[6000,128]{1,0:T(8,128)}, f32[16,512]{1,0:T(8,128)}, f32[16,512]{1,0:T(8,128)}, f32[16,512]{1,0:T(8,128)}, f32[16,512]{1,0:T(8,128)}, /*index...) custom-call(f32[6000,128]{1,0:T(8,128)} %get-tuple-element.79.refs_0, ...), custom_call_target="tpu_custom_call" | custom-call | tf_op jit(solution)/shard_map/hand_over/pallas_call | solution.py:1185

commit v6 on v5

--- a/solution.py
+++ b/solution.py
@@ -17,11 +17,13 @@
 MESH = pl.DeviceIdType.MESH
 ROWS = 256
 MLP_ROWS = 512
+PROJECT_ROWS = 768
 EARLY_HEADS = 4
 B_FAR_AT = 0
 B_NEAR_AT = 2
 FAR_AT = 2
-NEAR_AT = 7
+NEAR_AT = 5
+CORNER_AT = 7
 FOLD_AT = 2
 ACROSS_AT = 1
 SQUARE_AT = 5
@@ -138,8 +140,9 @@
 
 
 class Spread:
-    def __init__(self, place, own, table, send_sem, recv_sem):
+    def __init__(self, place, own, table, send_sem, recv_sem, relayed=False):
         self.place, self.own, self.table = place, own, table
+        self.direct = range(1, 3) if relayed else range(1, 4)
         self.send_sem, self.recv_sem = send_sem, recv_sem
         self.started = []
 
@@ -166,6 +169,21 @@
         slot = self.place.deep * 4 - 1 + dz * 4 + dxy
         return self.copy(slot, dz, dxy, self.place.moved(flip=1))
 
+    def corner(self, dz, dxy):
+        count = self.table.shape[1]
+        middle = -(-count // 32) * 16
+        part = pl.ds(0, middle) if dxy == 2 else pl.ds(middle, count - middle)
+        slot = self.place.deep - 1 + dz * 3 + 2 if dxy == 2 else self.place.deep * 8 - 1 + dz
+        block = self.place.block(dz, dxy)
+        return pltpu.make_async_remote_copy(
+            src_ref=self.table.at[block, part],
+            dst_ref=self.table.at[block, part],
+            send_sem=self.send_sem.at[slot],
+            recv_sem=self.recv_sem.at[slot],
+            device_id=self.place.moved(dxy=3 - dxy),
+            device_id_type=MESH,
+        )
+
     def launch(self, copy):
         copy.start()
         self.started.append(copy)
@@ -175,22 +193,30 @@
             self.launch(self.far(dz))
 
     def begin_near(self):
-        for dxy in range(1, 4):
+        for dxy in self.direct:
             self.launch(self.near(0, dxy))
         self.launch(self.across(0, 0))
 
     def relay_far(self):
         for dz in range(1, self.place.deep):
             self.far(dz).wait_recv()
-            for dxy in range(1, 4):
+            for dxy in self.direct:
                 self.launch(self.near(dz, dxy))
             self.launch(self.across(dz, 0))
 
     def relay_near(self, low, high):
         for dz in range(low, high):
-            for dxy in range(1, 4):
+            for dxy in self.direct:
                 self.near(dz, dxy).wait_recv()
+                if 3 not in self.direct:
+                    self.launch(self.corner(dz, dxy))
                 self.launch(self.across(dz, dxy))
+
+    def relay_corner(self, low, high):
+        for dz in range(low, high):
+            for dxy in (1, 2):
+                self.corner(dz, dxy).wait_recv()
+            self.launch(self.across(dz, 3))
 
     def arrive(self):
         for dz in range(self.place.deep):
@@ -202,8 +228,11 @@
         for dz in range(1, deep):
             self.far(dz).wait_send()
         for dz in range(deep):
-            for dxy in range(1, 4):
+            for dxy in self.direct:
                 self.near(dz, dxy).wait_send()
+            if 3 not in self.direct:
+                for dxy in (1, 2):
+                    self.corner(dz, dxy).wait_send()
         for dz in range(deep):
             for dxy in range(4):
                 self.across(dz, dxy).wait_send()
@@ -280,7 +309,7 @@
         place.greet()
         part_a = Spread(place, table_a.at[place.me], table_a, *sems[0:2])
         part_b = Spread(place, table_b.at[place.me], table_b, *sems[2:4])
-        second = Spread(place, own, second_ref, *sems[4:6])
+        second = Spread(place, own, second_ref, *sems[4:6], relayed=True)
         early = EARLY_HEADS * depth
         if early > 128:
             table_a[place.me, 48:64, 128:] = jnp.zeros((16, early - 128), BF16)
@@ -337,7 +366,7 @@
                 return matrix(table[:, :, lanes], 16 * which)
             return matrix(table_a if low == 0 else table_b, 16 * which)
 
-        rows = pl.ds(pl.multiple_of(i * ROWS, ROWS), ROWS)
+        rows = pl.ds(pl.multiple_of(i * PROJECT_ROWS, PROJECT_ROWS), PROJECT_ROWS)
         if low == 0:
             h1 = (units[rows, :] * gain + shift).astype(BF16)
             rows_low[rows, :] = h1
@@ -357,13 +386,13 @@
             ka_ref[h, rows, :] = jnp.concatenate([k_high[:, cols], k_low[:, cols]], axis=1)
         return carry
 
-    lax.fori_loop(0, padded // ROWS, functools.partial(project, (0, EARLY_HEADS)), 0)
+    lax.fori_loop(0, padded // PROJECT_ROWS, functools.partial(project, (0, EARLY_HEADS)), 0)
 
     def project_rest():
         if mesh_shape is not None:
             part_b.arrive()
             keep_b.start()
-        lax.fori_loop(0, padded // ROWS, functools.partial(project, (EARLY_HEADS, HEADS)), 0)
+        lax.fori_loop(0, padded // PROJECT_ROWS, functools.partial(project, (EARLY_HEADS, HEADS)), 0)
         for copy in writes:
             copy.start()
 
@@ -402,6 +431,8 @@
             pl.when(i == B_NEAR_AT)(functools.partial(part_b.relay_near, 0, place.deep))
             pl.when(i == FAR_AT)(second.relay_far)
             pl.when(i == NEAR_AT)(functools.partial(second.relay_near, 0, 2))
+            pl.when(i == NEAR_AT + 1)(functools.partial(second.relay_near, 2, place.deep))
+            pl.when(i == CORNER_AT)(functools.partial(second.relay_corner, 0, 2))
         pl.when(i == EARLY_HEADS - 1)(project_rest)
         score(i * 2 + 1, 1)
         finish(i * 2, 0)
@@ -422,7 +453,7 @@
         return carry
 
     if mesh_shape is not None:
-        second.relay_near(2, place.deep)
+        second.relay_corner(2, place.deep)
     lax.fori_loop(0, padded // ROWS, extend, 0)
     last_write.start()
     for copy in writes + [last_write] + [head_write(head) for head in range(HEADS)]:
@@ -480,7 +511,8 @@
             pltpu.VMEM((blocks, 48, width - early), BF16),
             pltpu.VMEM((own_rows, width), BF16),
         ]
-        scratch += [pltpu.SemaphoreType.DMA((blocks - 1,)) for _ in range(6)]
+        scratch += [pltpu.SemaphoreType.DMA((blocks - 1,)) for _ in range(4)]
+        scratch += [pltpu.SemaphoreType.DMA((mesh_shape[0] * 4 + 3,)) for _ in range(2)]
         scratch += [pltpu.SemaphoreType.DMA((3,))]
         options = dict(collective_id=0, has_side_effects=True)
     return pl.pallas_call(

time: 174 us -> 170 us (0.977)
  Pallas kernels: 172 us -> 169 us
    pallas_call x1, Pallas kernels: 52.3 us -> 48 us  [attend(): pl.pallas_call(functools.partial(attend_kernel, frames, mesh_shape), out_...]
where the time goes in v6:
time: 170 us
  Pallas kernels  169 us (99%)
    pallas_call x1, Pallas kernels, attend_back(): pl.pallas_call(functools.partial(attend_back_kernel, frames, mesh_shape),...  74.8 us
    pallas_call x1, Pallas kernels, attend(): pl.pallas_call(functools.partial(attend_kernel, frames, mesh_shape), out_...  48 us
    pallas_call x1, Pallas kernels, mlp(): pl.pallas_call(functools.partial(mlp_kernel, frames), grid=(padded // MLP...  42.7 us

profile of v6, /device:TPU:0, one launch (start us, length us, event | category | flops | bytes accessed | tf_op | source)
XLA Modules:
  0.0 170.2 jit_solution(9564341934391477538)
XLA Ops:
  1.3 48.0 %attend.1 = (bf16[8,1536,128]{2,1,0:T(8,128)(2,1)}, bf16[8,1536,128]{2,1,0:T(8,128)(2,1)}, bf16[512,1536]{1,0:T(8,128)(2,1)}, bf16[512,1536]{1,0:T(8,128)(2,1)},...) custom-call(bf16[1500,512]{1,0:T(8,128)(2,1)} %bitcast.5, ...), custom_call_target="tpu_custom_call" | custom-call | tf_op jit(solution)/shard_map/attend/pallas_call | solution.py:518
  49.3 42.7 %mlp.1 = (f32[6000,128]{1,0:T(8,128)}, f32[1500,512]{1,0:T(8,128)}, bf16[1536,512]{1,0:T(8,128)(2,1)}, bf16[1536,128]{1,0:T(8,128)(2,1)}, bf16[32,144,512]{2,1,0:T(8,128)(2,1)}, /*index=5*/f32[16,512]{1,0:T(8,128)}) custom-call(s32[1]{0:T(128)S(6)} %copy.39.flag_ref, bf16[1500,512]{1,0:T(8,128)(2,1)} %bitcast.6, bf16[1500,512]{1,0:T(8,128)(2,1)} %bitcast.9, ...), custom_call_target="tpu_custom_call" | custom-call | tf_op jit(solution)/shard_map/mlp/pallas_call | solution.py:674
  92.0 74.8 %attend_back.1 = (f32[6000,128]{1,0:T(8,128)}, f32[16,512]{1,0:T(8,128)}, f32[16,512]{1,0:T(8,128)}, f32[16,512]{1,0:T(8,128)}, f32[16,512]{1,0:T(8,128)}, /*ind...) custom-call(bf16[1500,512]{1,0:T(8,128)(2,1)} %bitcast.7, ...), custom_call_target="tpu_custom_call" | custom-call | tf_op jit(solution)/shard_map/attend_back/pallas_call | solution.py:1174
  166.8 3.2 %hand_over.1 = (f32[6000,128]{1,0:T(8,128)}, f32[16,512]{1,0:T(8,128)}, f32[16,512]{1,0:T(8,128)}, f32[16,512]{1,0:T(8,128)}, f32[16,512]{1,0:T(8,128)}, /*index...) custom-call(f32[6000,128]{1,0:T(8,128)} %get-tuple-element.79.refs_0, ...), custom_call_target="tpu_custom_call" | custom-call | tf_op jit(solution)/shard_map/hand_over/pallas_call | solution.py:1217

commit v7 on v6

--- a/solution.py
+++ b/solution.py
@@ -1080,11 +1080,11 @@
         small_ref[...] = small[...]
     else:
         shorts.send(0, small[...])
-        for t in range(last):
-            part_result(t)
         shorts.send(1, shorts.receive(0))
         parts[last].fold_near()
         shorts.send(2, shorts.receive(1))
+        for t in range(last):
+            part_result(t)
         second.drain()
         for t in range(last):
             parts[t].drain()

time: 170 us -> 170 us (level)
  no operation moved by 1% of the time
where the time goes in v7:
time: 170 us
  Pallas kernels  169 us (99%)
    pallas_call x1, Pallas kernels, attend_back(): pl.pallas_call(functools.partial(attend_back_kernel, frames, mesh_shape),...  74.8 us
    pallas_call x1, Pallas kernels, attend(): pl.pallas_call(functools.partial(attend_kernel, frames, mesh_shape), out_...  48 us
    pallas_call x1, Pallas kernels, mlp(): pl.pallas_call(functools.partial(mlp_kernel, frames), grid=(padded // MLP...  42.7 us

profile of v7, /device:TPU:0, one launch (start us, length us, event | category | flops | bytes accessed | tf_op | source)
XLA Modules:
  0.0 170.2 jit_solution(9082229461098941253)
XLA Ops:
  1.3 48.0 %attend.1 = (bf16[8,1536,128]{2,1,0:T(8,128)(2,1)}, bf16[8,1536,128]{2,1,0:T(8,128)(2,1)}, bf16[512,1536]{1,0:T(8,128)(2,1)}, bf16[512,1536]{1,0:T(8,128)(2,1)},...) custom-call(bf16[1500,512]{1,0:T(8,128)(2,1)} %bitcast.5, ...), custom_call_target="tpu_custom_call" | custom-call | tf_op jit(solution)/shard_map/attend/pallas_call | solution.py:518
  49.3 42.7 %mlp.1 = (f32[6000,128]{1,0:T(8,128)}, f32[1500,512]{1,0:T(8,128)}, bf16[1536,512]{1,0:T(8,128)(2,1)}, bf16[1536,128]{1,0:T(8,128)(2,1)}, bf16[32,144,512]{2,1,0:T(8,128)(2,1)}, /*index=5*/f32[16,512]{1,0:T(8,128)}) custom-call(s32[1]{0:T(128)S(6)} %copy.39.flag_ref, bf16[1500,512]{1,0:T(8,128)(2,1)} %bitcast.6, bf16[1500,512]{1,0:T(8,128)(2,1)} %bitcast.9, ...), custom_call_target="tpu_custom_call" | custom-call | tf_op jit(solution)/shard_map/mlp/pallas_call | solution.py:674
  92.0 74.8 %attend_back.1 = (f32[6000,128]{1,0:T(8,128)}, f32[16,512]{1,0:T(8,128)}, f32[16,512]{1,0:T(8,128)}, f32[16,512]{1,0:T(8,128)}, f32[16,512]{1,0:T(8,128)}, /*ind...) custom-call(bf16[1500,512]{1,0:T(8,128)(2,1)} %bitcast.7, ...), custom_call_target="tpu_custom_call" | custom-call | tf_op jit(solution)/shard_map/attend_back/pallas_call | solution.py:1174
  166.8 3.2 %hand_over.1 = (f32[6000,128]{1,0:T(8,128)}, f32[16,512]{1,0:T(8,128)}, f32[16,512]{1,0:T(8,128)}, f32[16,512]{1,0:T(8,128)}, f32[16,512]{1,0:T(8,128)}, /*index...) custom-call(f32[6000,128]{1,0:T(8,128)} %get-tuple-element.79.refs_0, ...), custom_call_target="tpu_custom_call" | custom-call | tf_op jit(solution)/shard_map/hand_over/pallas_call | solution.py:1217
